TPU v7x, 32 devices: a whole 2x2x4 slice. The times are simulated.
32 devices in a mesh: tm: 8 (over z, y), space: 4 (over x, core).
Axes of the slice: x: 2, y: 2, z: 4, core: 2. Of those that a mesh axis runs over, the one named last changes fastest.
Arguments:
- attn_query: bfloat16 [4096, 2560], P(('tm', 'space')), may hold values from -8 to 8
- attn_key: bfloat16 [4096, 2560], P(('tm', 'space')), may hold values from -8 to 8
- attn_value: bfloat16 [4096, 2560], P(('tm', 'space')), may hold values from -6 to 6
- attn_outgrad: bfloat16 [4096, 2560], P(('tm', 'space')), may hold values from -6 to 6
- fast_query: bfloat16 [4096, 1536], P('tm'), may hold values from -6 to 6
- fast_outgrad: bfloat16 [4096, 1536], P('tm'), may hold values from -6 to 6
- fast_key: bfloat16 [4096, 1536], P('tm'), may hold values from -6 to 6
- gate_weights: bfloat16 [8, 1536, 3072], P('tm', None, 'space'), may hold values from -0.15625 to 0.15625
- up_weights: bfloat16 [8, 1536, 3072], P('tm', None, 'space'), may hold values from -0.15625 to 0.15625
- down_weights: bfloat16 [8, 3072, 1536], P('tm', 'space'), may hold values from -0.109375 to 0.109375
- gate_factor: bfloat16 [4096, 3072], P('tm', 'space'), may hold values from -0.15625 to 0.15625
- clip_groups: int32 [4], replicated, may hold values from 1 to 4, 8 in all
Outputs:
- query_grad: bfloat16 [4096, 2560], P(('tm', 'space'))
- key_grad: bfloat16 [4096, 2560], P(('tm', 'space'))
- value_grad: bfloat16 [4096, 2560], P(('tm', 'space'))
- fast_grad: bfloat16 [4096, 1536], P(('tm', 'space'))
- rate_grad: float32 [4096], P(('tm', 'space'))
Inputs may be any that keep to these rules, and one draw needn't show every extreme that they name: `clip_groups`: clip k covers the groups after those of clips 0 to k - 1; the counts sum to 8.
All inputs are finite; a program needn't handle non-finite values.
Results may differ from a plain program's by a relative error of at most 0.012.
Values may be sent and summed in bfloat16 or wider, within the bound.
No kernel may reach another device: no remote copies, remote signals or barrier semaphores. Data moves between devices by JAX's collectives and lax.ppermute only.
A program may use at most 192 MiB of HBM per device.

v0:
```python
import functools
import math

import jax
import jax.numpy as jnp
from jax import lax
from jax.experimental import pallas as pl
from jax.experimental.pallas import tpu as pltpu
from jax.sharding import PartitionSpec as P


HEAD = 128

CONTRACT_LAST = (((1,), (1,)), ((), ()))
CONTRACT_FIRST = (((0,), (0,)), ((), ()))
F32 = jnp.float32
BF16 = jnp.bfloat16


def dot_last(a, b):
    return lax.dot_general(a, b, CONTRACT_LAST, preferred_element_type=F32)


def cost(flops, moved, transcendentals=0):
    return pl.CostEstimate(flops=flops, bytes_accessed=moved, transcendentals=transcendentals)


def pick_kernel(scal, fk, fq, k, v, out, hc, hx, sems):
    reach = hc.shape[1]
    odd = scal[1] % 2
    first = pltpu.make_async_copy(fk, out, sems.at[0])

    @pl.when(odd == 0)
    def _():
        first.start()

    @pl.when(odd == 1)
    def _():
        pltpu.make_async_copy(fq, out, sems.at[0]).start()

    copies = []
    for i, source in enumerate((k, v)):
        for j, (half, at) in enumerate(((hx, odd), (hc, 1 - odd))):
            rows = pl.ds(pl.multiple_of(at * reach, reach), reach)
            copies.append(pltpu.make_async_copy(source.at[rows], half.at[i], sems.at[1 + 2 * i + j]))
    for copy in copies:
        copy.start()
    first.wait()
    for copy in copies:
        copy.wait()


def pick(scal, fast_key, fast_query, key, value):
    rows, width = key.shape
    half = jax.ShapeDtypeStruct((2, rows // 2, width), BF16)
    return pl.pallas_call(
        pick_kernel,
        in_specs=[pl.BlockSpec(memory_space=pltpu.SMEM)]
        + [pl.BlockSpec(memory_space=pl.ANY)] * 4,
        out_specs=[pl.BlockSpec(memory_space=pltpu.VMEM)] * 3,
        out_shape=[jax.ShapeDtypeStruct(fast_key.shape, BF16), half, half],
        scratch_shapes=[pltpu.SemaphoreType.DMA((5,))],
        cost_estimate=cost(0, 4 * fast_key.size + 8 * rows * width),
        name="pick_outgoing",
    )(scal, fast_key, fast_query, key, value)


def weights_kernel(shifts, scal, clips, out):
    at = scal[0]
    starts, total = [], 0
    for n in range(clips.shape[0]):
        starts.append(total)
        total = total + clips[n]

    def together(u, v):
        apart = jnp.bool_(False)
        for x in range(1 - u, v + 1):
            for start in starts:
                apart = apart | (start == at + x)
        return jnp.where(apart, 0.0, 1.0)

    for n, (u, v) in enumerate([(1, 0)] + [(u, v) for v in shifts for u in (0, 1)]):
        out[n : n + 1, :] = jnp.full((1, out.shape[1]), together(u, v), F32)


def pair_weights(scal, clips, shifts):
    return pl.pallas_call(
        functools.partial(weights_kernel, shifts),
        in_specs=[pl.BlockSpec(memory_space=pltpu.SMEM)] * 2,
        out_specs=pl.BlockSpec(memory_space=pltpu.VMEM),
        out_shape=jax.ShapeDtypeStruct((1 + 2 * len(shifts), HEAD), F32),
        cost_estimate=cost(20 * 10**9, 4096),
        compiler_params=pltpu.CompilerParams(vmem_limit_bytes=1 << 20),
        name="pair_weights",
    )(scal, clips)


def fast_kernel(step, q, og, gw, uw, dw, gate_out, part_out, gate_grad, up_grad, part, sems):
    for j in range(gw.shape[2] // step):
        cols = slice(j * step, (j + 1) * step)
        gate = jnp.dot(q[...], gw[0, :, cols], preferred_element_type=F32)
        up = jnp.dot(q[...], uw[0, :, cols], preferred_element_type=F32)
        hidden = dot_last(og[...], dw[0, cols, :])
        sig = jax.nn.sigmoid(gate)
        gate_grad[:, cols] = (hidden * up * sig * (1.0 + gate * (1.0 - sig))).astype(BF16)
        up_grad[:, cols] = (hidden * (gate * sig)).astype(BF16)
    copies = [pltpu.make_async_copy(gate_grad, gate_out, sems.at[0])]
    copies[0].start()
    for j in range(q.shape[1] // step):
        rows = slice(j * step, (j + 1) * step)
        part[:, rows] = (
            dot_last(gate_grad[...], gw[0, rows, :]) + dot_last(up_grad[...], uw[0, rows, :])
        ).astype(BF16)
        copy = pltpu.make_async_copy(part.at[:, rows], part_out.at[:, rows], sems.at[1 + j])
        copy.start()
        copies.append(copy)
    for copy in copies:
        copy.wait()


def fast(query, outgrad, gate_w, up_w, down_w):
    rows, width = query.shape
    hidden = gate_w.shape[2]
    step = next(s for s in (256, 128) if hidden % s == 0 and width % s == 0)
    vmem = pl.BlockSpec(memory_space=pltpu.VMEM)
    return pl.pallas_call(
        functools.partial(fast_kernel, step),
        in_specs=[vmem] * 5,
        out_specs=[pl.BlockSpec(memory_space=pltpu.HBM)] * 2,
        out_shape=[
            jax.ShapeDtypeStruct((rows, hidden), BF16),
            jax.ShapeDtypeStruct((rows, width), BF16),
        ],
        scratch_shapes=[
            pltpu.VMEM((rows, hidden), BF16),
            pltpu.VMEM((rows, hidden), BF16),
            pltpu.VMEM((rows, width), BF16),
            pltpu.SemaphoreType.DMA((1 + width // step,)),
        ],
        cost_estimate=cost(20 * 10**9, 6 * width * hidden + 8 * rows * width),
        compiler_params=pltpu.CompilerParams(vmem_limit_bytes=26 << 20),
        name="fast_weights",
    )(query, outgrad, gate_w, up_w, down_w)


def attention_kernel(reach, last, every, scal, q, g, k, v, hc, hx, *refs):
    outs, held, sems = refs[:5], refs[5:10], refs[10]
    dq, dk_own, dv_own, mc, mx = held
    copies = []
    rows = q.shape[0]
    keys = rows + 2 * reach
    wide = 2 * HEAD
    at = scal[1]
    even = at % 2 == 0
    scaling = 1.0 / math.sqrt(HEAD)
    key_row = lax.broadcasted_iota(jnp.int32, (keys, rows), 0)
    query_row = lax.broadcasted_iota(jnp.int32, (keys, rows), 1)
    shift_c = jnp.where(even, 0, -(rows + reach))
    shift_x = jnp.where(even, -(rows + 2 * reach), -reach)
    key_pos = key_row + jnp.where(
        key_row < rows, 0, jnp.where(key_row < rows + reach, shift_c, shift_x)
    )
    offset = at * rows
    live = (key_pos + offset >= 0) & (key_pos + offset < last)
    bias = jnp.where(live & (jnp.abs(key_pos - query_row) <= reach), 0.0, -1e30)
    bias = jnp.concatenate([bias, bias], axis=1)
    zero = jnp.zeros((rows, HEAD), BF16)

    def diagonal(ref, at):
        head, other = ref[:, at : at + HEAD], ref[:, at + HEAD : at + wide]
        return jnp.concatenate(
            [jnp.concatenate([head, zero], axis=1), jnp.concatenate([zero, other], axis=1)], axis=0
        )

    for start in range(0, q.shape[1], wide):
        col = slice(start, start + wide)
        kk = jnp.concatenate([k[:, col], hc[0, :, col], hx[0, :, col]], axis=0)
        vv = jnp.concatenate([v[:, col], hc[1, :, col], hx[1, :, col]], axis=0)
        qd, gd = diagonal(q, start), diagonal(g, start)
        scores = dot_last(kk, qd) * scaling + bias
        exponent = jnp.exp(scores - jnp.max(scores, axis=0, keepdims=True))
        probs = exponent * (1.0 / jnp.sum(exponent, axis=0, keepdims=True))
        probs_b = probs.astype(BF16)
        dprobs = dot_last(vv, gd)
        delta = jnp.sum(probs_b.astype(F32) * dprobs, axis=0, keepdims=True)
        dscores_b = (probs * (dprobs - delta)).astype(BF16)
        dv = jnp.dot(probs_b, gd, preferred_element_type=F32)
        dk = jnp.dot(dscores_b, qd, preferred_element_type=F32) * scaling
        both = lax.dot_general(dscores_b, kk, CONTRACT_FIRST, preferred_element_type=F32)
        dq[:, start : start + HEAD] = (both[:rows, :HEAD] * scaling).astype(BF16)
        dq[:, start + HEAD : start + wide] = (both[rows:, HEAD:] * scaling).astype(BF16)
        for i, (grad, own) in enumerate(((dk, dk_own), (dv, dv_own))):
            own[:, col] = grad[:rows].astype(BF16)
            mc[i, :, col] = grad[rows : rows + reach].astype(BF16)
            mx[i, :, col] = grad[rows + reach :].astype(BF16)
        if (start + wide) % every == 0:
            done = (Ellipsis, slice(start + wide - every, start + wide))
            for i, (ref, out) in enumerate(zip(held, outs)):
                sem = sems.at[start // every, i]
                copies.append(pltpu.make_async_copy(ref.at[done], out.at[done], sem))
                copies[-1].start()
    for copy in copies:
        copy.wait()


def attention(scal, query, out_grad, key, value, halo_c, halo_x, last):
    rows, width = query.shape
    reach = halo_c.shape[1]
    keys = rows + 2 * reach
    every = next(n for n in (4, 2) if width % (n * HEAD) == 0) * HEAD
    vmem = pl.BlockSpec(memory_space=pltpu.VMEM)
    flat = jax.ShapeDtypeStruct((rows, width), BF16)
    half = jax.ShapeDtypeStruct((2, reach, width), BF16)
    return pl.pallas_call(
        functools.partial(attention_kernel, reach, last, every),
        in_specs=[pl.BlockSpec(memory_space=pltpu.SMEM)] + [vmem] * 6,
        out_specs=[pl.BlockSpec(memory_space=pltpu.HBM)] * 5,
        out_shape=[flat] * 3 + [half] * 2,
        scratch_shapes=[pltpu.VMEM(out.shape, out.dtype) for out in [flat] * 3 + [half] * 2]
        + [pltpu.SemaphoreType.DMA((width // every, 5))],
        cost_estimate=cost(
            20 * rows * keys * width, 22 * width * rows, width // HEAD * rows * keys
        ),
        compiler_params=pltpu.CompilerParams(vmem_limit_bytes=14 << 20),
        name="window_attention",
    )(scal, query, out_grad, key, value, halo_c, halo_x)


def scores_kernel(scal, k0, q0, *refs):
    twos, out = refs[:-1], refs[-1]
    even = scal[1] % 2 == 0

    def fill(arrays):
        k1, queries = arrays[0], arrays[1:]
        out[0] = dot_last(q0[...], k1[...]).astype(BF16)
        for n in range((out.shape[0] - 1) // 2):
            out[2 * n + 1] = dot_last(queries[n][...], k0[...]).astype(BF16)
            out[2 * n + 2] = dot_last(queries[n][...], k1[...]).astype(BF16)

    @pl.when(even)
    def _():
        fill(twos)

    @pl.when(jnp.logical_not(even))
    def _():
        fill([twos[n ^ 1] for n in range(len(twos))])


def scores(scal, k0, q0, twos, pairs):
    rows, width = k0.shape
    vmem = pl.BlockSpec(memory_space=pltpu.VMEM)
    return pl.pallas_call(
        scores_kernel,
        in_specs=[pl.BlockSpec(memory_space=pltpu.SMEM)] + [vmem] * (2 + len(twos)),
        out_specs=vmem,
        out_shape=jax.ShapeDtypeStruct((pairs, rows, rows), BF16),
        cost_estimate=cost(
            2 * pairs * rows * rows * width, 2 * (pairs * rows * rows + (2 + pairs) * rows * width)
        ),
        compiler_params=pltpu.CompilerParams(vmem_limit_bytes=20 << 20),
        name="pair_scores",
    )(scal, k0, q0, *twos)


def rates_kernel(share, together, f0, f1, st, g0, *refs):
    moved, out = refs[:-1], refs[-1]
    lanes = out.shape[2]
    step = st.shape[2] // 2
    for block in range(0, st.shape[2], step):
        rows = slice(block, block + step)

        def pair(n, g, f):
            products = dot_last(g[...], f[rows, :])
            summed = jnp.sum(st[n, :, rows].astype(F32) * products, axis=0, keepdims=True)
            return summed * (together[n : n + 1, 0:1] * share)

        before = pair(0, g0, f1)
        own = jnp.zeros_like(before)
        for n, g in enumerate(moved):
            own += pair(2 * n + 1, g, f0)
            before += pair(2 * n + 2, g, f1)
        for at in range(0, step, lanes):
            part = slice(at, at + lanes)
            n = (block + at) // lanes
            out[n, 0:1, :] = own[:, part]
            out[n, 1:2, :] = before[:, part]


def rates(together, f0, f1, st, g0, moved, tiles):
    rows, width = f0.shape
    pairs = st.shape[0]
    vmem = pl.BlockSpec(memory_space=pltpu.VMEM)
    return pl.pallas_call(
        functools.partial(rates_kernel, 1.0 / rows),
        in_specs=[vmem] * (5 + len(moved)),
        out_specs=vmem,
        out_shape=jax.ShapeDtypeStruct((tiles, 2, rows // tiles), F32),
        cost_estimate=cost(
            2 * pairs * rows * rows * width, 2 * (pairs * rows * rows + (2 + pairs) * rows * width)
        ),
        compiler_params=pltpu.CompilerParams(vmem_limit_bytes=16 << 20),
        name="pair_rates",
    )(together, f0, f1, st, g0, *moved)


def margins_kernel(scal, dk, dv, mc, mx, key_grad, value_grad):
    reach = mc.shape[1]
    even = scal[1] % 2 == 0
    for i, (own, out) in enumerate(((dk, key_grad), (dv, value_grad))):
        from_c, from_x = mc[i].astype(F32), mx[i].astype(F32)
        head = jnp.where(even, from_x, from_c)
        tail = jnp.where(even, from_c, from_x)
        out[:reach] = (own[:reach].astype(F32) + head).astype(BF16)
        out[reach:] = (own[reach:].astype(F32) + tail).astype(BF16)


def add_margins(scal, dk, dv, mc, mx):
    rows, width = dk.shape
    vmem = pl.BlockSpec(memory_space=pltpu.VMEM)
    return pl.pallas_call(
        margins_kernel,
        in_specs=[pl.BlockSpec(memory_space=pltpu.SMEM)] + [vmem] * 4,
        out_specs=[vmem] * 2,
        out_shape=[jax.ShapeDtypeStruct((rows, width), BF16)] * 2,
        input_output_aliases={1: 0, 2: 1},
        cost_estimate=cost(2 * rows * width, 12 * rows * width),
        compiler_params=pltpu.CompilerParams(vmem_limit_bytes=8 << 20),
        name="add_margins",
    )(scal, dk, dv, mc, mx)


def sum_kernel(parts, out):
    total = parts[0].astype(F32)
    for n in range(1, parts.shape[0]):
        total += parts[n].astype(F32)
    out[...] = total.astype(BF16)


def sum_parts(parts):
    vmem = pl.BlockSpec(memory_space=pltpu.VMEM)
    return pl.pallas_call(
        sum_kernel,
        in_specs=[vmem],
        out_specs=vmem,
        out_shape=jax.ShapeDtypeStruct(parts.shape[1:], BF16),
        cost_estimate=cost(parts.size, 2 * parts.size),
        compiler_params=pltpu.CompilerParams(vmem_limit_bytes=8 << 20),
        name="sum_parts",
    )(parts)


def shifted(array, axis, by):
    devices = lax.axis_size(axis)
    pairs = [(i + by, i) for i in range(devices) if 0 <= i + by < devices]
    return lax.ppermute(array, axis, pairs)


def swapped(array, axis, first):
    devices = lax.axis_size(axis)
    pairs = [(i, i + 1) for i in range(first, devices - 1, 2)]
    return lax.ppermute(array, axis, pairs + [(j, i) for i, j in pairs])


def moved_apart(array, by_even, by_odd):
    groups, tiles = lax.axis_size("tm"), lax.axis_size("space")
    pairs = []
    for group in range(groups):
        for tile in range(tiles):
            source = group + (by_odd if tile % 2 else by_even)
            if 0 <= source < groups:
                pairs.append((source * tiles + tile, group * tiles + tile))
    return lax.ppermute(array, ("tm", "space"), pairs)


def per_device(
    attn_query,
    attn_key,
    attn_value,
    attn_outgrad,
    fast_query,
    fast_outgrad,
    fast_key,
    gate_weights,
    up_weights,
    down_weights,
    gate_factor,
    clip_groups,
):
    groups, tiles = lax.axis_size("tm"), lax.axis_size("space")
    group, tile = lax.axis_index("tm"), lax.axis_index("space")
    scal = jnp.stack([group, tile]).astype(jnp.int32)
    rows = fast_query.shape[0]
    tile_rows, _ = attn_query.shape
    most = groups // 2
    shifts = tuple(range(2, most, 2))
    travels = [-1, *shifts]
    travels += travels[-1:] * (len(travels) % 2)

    outgoing, halo_c, halo_x = pick(scal, fast_key, fast_query, attn_key, attn_value)
    received = []
    for n in range(0, len(travels), 2):
        array = outgoing if n == 0 else fast_query
        received.append(moved_apart(array, travels[n], travels[n + 1]))
    together = pair_weights(scal, clip_groups, shifts)
    factor_before = shifted(gate_factor, "tm", -1)
    halo_c = swapped(halo_c, "space", 0)
    halo_x = swapped(halo_x, "space", 1)

    gate_grad_b, input_part = fast(fast_query, fast_outgrad, gate_weights, up_weights, down_weights)
    moved = []
    for v in shifts:
        moved.append(shifted(gate_grad_b, "tm", v))

    parts = lax.all_to_all(input_part.reshape(tiles, tile_rows, -1), "space", 0, 0)

    query_grad, dk, dv, margin_c, margin_x = attention(
        scal, attn_query, attn_outgrad, attn_key, attn_value, halo_c, halo_x, rows
    )
    margin_c = swapped(margin_c, "space", 0)
    margin_x = swapped(margin_x, "space", 1)

    twos = []
    for array in received:
        twos += [array, swapped(array, "space", 0)]
    st = scores(scal, fast_key, fast_query, twos, 1 + 2 * len(shifts))
    fast_grad = sum_parts(parts)
    key_grad, value_grad = add_margins(scal, dk, dv, margin_c, margin_x)
    rate = rates(together, gate_factor, factor_before, st, gate_grad_b, moved, tiles)
    rate = lax.all_to_all(rate, "space", 0, 0)
    rate = jnp.sum(rate, axis=0)
    rate_grad = rate[0] + shifted(rate[1], "tm", 1)
    return query_grad, key_grad, value_grad, fast_grad, rate_grad


def solution(mesh):
    over = ("tm", "space")
    tiled = P(over, None)
    in_specs = (
        (tiled,) * 4
        + (P("tm", None),) * 3
        + (P("tm", None, "space"),) * 2
        + (P("tm", "space", None), P("tm", "space"), P())
    )
    return jax.shard_map(
        per_device,
        mesh=mesh,
        in_specs=in_specs,
        out_specs=(tiled,) * 4 + (P(over),),
        check_vma=False,
    )
```

profile of v0, /device:TPU:25, one launch (start us, length us, event | category | flops | bytes accessed | tf_op | source)
XLA Modules:
  0.0 91.3 jit_solution(17564514961844502570)
XLA Ops:
  0.6 0.6 pad_add_fusion.scal
  1.2 4.2 %pick_outgoing.1 = (bf16[512,1536]{1,0:T(8,128)(2,1)}, bf16[2,64,2560]{2,1,0:T(8,128)(2,1)}, bf16[2,64,2560]{2,1,0:T(8,128)(2,1)}) custom-call(s32[2]{0:T(128)} %pad_add_fusion.scal, bf16[512,1536]{1,0:T(8,128)(2,1)} %k0.1, bf16[512,1536]{1,0:T(8,128)(2,1)} %q0.1, bf16[128,2560]{1,0:T(8,128)(2,1)} %k.3, bf16[128,2560]{1,0:T(8,128)(2,1)} %v.3), custom_call_target="tpu_custom_call" | custom-call | bytes 5767168 | tf_op jit(solution)/shard_map/pick_outgoing/pallas_call | solution.py:56
  5.4 0.7 collective-permute-start
  6.1 3.0 %collective-permute-start.1 = (bf16[2,64,2560]{2,1,0:T(8,128)(2,1)}, bf16[2,64,2560]{2,1,0:T(8,128)(2,1)}, u32[]{:S(2)}, u32[]{:S(2)}) collective-permute-start(bf16[2,64,2560]{2,1,0:T(8,128)(2,1)} %get-tuple-element.18), channel_id=1, source_target_pairs={{1,2},{2,1},{5,6},{6,5},{9,10},{10,9},{13,14},{14,13},{17,18},{18,... | collective-permute-start | bytes 1966088 | tf_op jit(solution)/shard_map/ppermute | solution.py:361
  9.2 0.0 copy-start.2
  9.2 2.3 %collective-permute-start.5 = (bf16[512,1536]{1,0:T(8,128)(2,1)}, bf16[512,1536]{1,0:T(8,128)(2,1)S(1)}, u32[]{:S(2)}, u32[]{:S(2)}) collective-permute-start(bf16[512,1536]{1,0:T(8,128)(2,1)} %get-tuple-element.27), channel_id=1, source_target_pairs={{9,1},{11,3},{0,4},{13,5},{2,6},{15,7},{4,8},{17,9},{6,10},{19,11}... | collective-permute-start | bytes 4718600 | tf_op jit(solution)/shard_map/ppermute | solution.py:372
  11.5 1.7 %copy-done.6 = bf16[1,1536,768]{2,1,0:T(8,128)(2,1)S(1)} copy-done((bf16[1,1536,768]{2,1,0:T(8,128)(2,1)S(1)}, bf16[1,1536,768]{2,1,0:T(8,128)(2,1)}, u32[]{:S(2)}) %copy-start.6) | copy-done | bytes 2359320
  13.2 1.7 %copy-done.7 = bf16[1,1536,768]{2,1,0:T(8,128)(2,1)S(1)} copy-done((bf16[1,1536,768]{2,1,0:T(8,128)(2,1)S(1)}, bf16[1,1536,768]{2,1,0:T(8,128)(2,1)}, u32[]{:S(2)}) %copy-start.7) | copy-done | bytes 2359320
  14.8 1.7 %copy-done.8 = bf16[1,768,1536]{2,1,0:T(8,128)(2,1)S(1)} copy-done((bf16[1,768,1536]{2,1,0:T(8,128)(2,1)S(1)}, bf16[1,768,1536]{2,1,0:T(8,128)(2,1)}, u32[]{:S(2)}) %copy-start.8) | copy-done | bytes 2359320
  16.5 1.4 %copy-done.9 = bf16[512,1536]{1,0:T(8,128)(2,1)S(1)} copy-done((bf16[512,1536]{1,0:T(8,128)(2,1)S(1)}, bf16[512,1536]{1,0:T(8,128)(2,1)}, u32[]{:S(2)}) %copy-start.9) | copy-done | bytes 1572888
  17.9 7.6 %fast_weights.1 = (bf16[512,768]{1,0:T(8,128)(2,1)S(1)}, bf16[512,1536]{1,0:T(8,128)(2,1)}) custom-call(bf16[512,1536]{1,0:T(8,128)(2,1)S(1)} %copy-done.1, bf16[512,1536]{1,0:T(8,128)(2,1)S(1)} %copy-done.9, bf16[1,1536,768]{2,1,0:T(8,128)(2,1)S(1)} %copy-done.6, bf16[1,1536,768]{2,1,0:T(8,128)(2,1)S(1)} %copy-done.7, bf16[1,768,1536]{2,1,0:T(8,128)(2,1)S(1)} %copy-done.8), custom_call_target="tpu_custom_call" | custom-call | flops 20000000000 | bytes 13369344 | tf_op jit(solution)/shard_map/fast_weights/pallas_call | solution.py:126
  25.6 2.2 %collective-permute-start.7 = (bf16[512,768]{1,0:T(8,128)(2,1)S(1)}, bf16[512,768]{1,0:T(8,128)(2,1)S(1)}, u32[]{:S(2)}, u32[]{:S(2)}) collective-permute-start(bf16[512,768]{1,0:T(8,128)(2,1)S(1)} %get-tuple-element.28.g0), channel_id=1, source_target_pairs={{8,0},{12,4},{16,8},{20,12},{24,16},{28,20},{9,1},{13,5},{17,9},{2... | collective-permute-start | bytes 2359304 | tf_op jit(solution)/shard_map/ppermute | solution.py:355
  27.7 3.1 %collective-permute-start.4 = (bf16[512,768]{1,0:T(8,128)(2,1)S(1)}, bf16[512,768]{1,0:T(8,128)(2,1)S(1)}, u32[]{:S(2)}, u32[]{:S(2)}) collective-permute-start(bf16[512,768]{1,0:T(8,128)(2,1)S(1)} %copy-done.2), channel_id=1, source_target_pairs={{0,4},{4,8},{8,12},{12,16},{16,20},{20,24},{24,28},{1,5},{5,9},{9,... | collective-permute-start | bytes 2359304 | tf_op jit(solution)/shard_map/ppermute | solution.py:355
  30.9 0.4 collective-permute-start.6
  31.3 0.6 pair_weights.1.together
  31.9 2.5 %collective-permute-done.6.refs_1_ = bf16[512,1536]{1,0:T(8,128)(2,1)S(1)} collective-permute-done((bf16[512,1536]{1,0:T(8,128)(2,1)S(1)}, bf16[512,1536]{1,0:T(8,128)(2,1)S(1)}, u32[]{:S(2)}, u32[]{:S(2)}) %collective-permute-start.6) | collective-permute-done | bytes 1572896 | tf_op jit(solution)/shard_map/ppermute | solution.py:361
  34.4 3.2 %pair_scores.1.st = bf16[3,512,512]{2,1,0:T(8,128)(2,1)S(1)} custom-call(s32[2]{0:T(128)S(1)} %copy-done.5, bf16[512,1536]{1,0:T(8,128)(2,1)S(1)} %copy-done, bf16[512,1536]{1,0:T(8,128)(2,1)S(1)} %copy-done.1, bf16[512,1536]{1,0:T(8,128)(2,1)S(1)} %collective-permute-done.5.refs_0_, bf16[512,1536]{1,0:T(8,128)(2,1)S(1)} %collective-permute-done.6.refs_1_), custom_call_target="tpu_custom_call" | custom-call | flops 2415919104 | bytes 9437184 | tf_op jit(solution)/shard_map/pair_scores/pallas_call | solution.py:252
  37.6 8.2 %collective-permute-done.7.refs_0_ = bf16[512,768]{1,0:T(8,128)(2,1)S(1)} collective-permute-done((bf16[512,768]{1,0:T(8,128)(2,1)S(1)}, bf16[512,768]{1,0:T(8,128)(2,1)S(1)}, u32[]{:S(2)}, u32[]{:S(2)}) %collective-permute-start.7) | collective-permute-done | bytes 786464 | tf_op jit(solution)/shard_map/ppermute | solution.py:355
  45.8 3.7 %collective-permute-done.4.f1 = bf16[512,768]{1,0:T(8,128)(2,1)S(1)} collective-permute-done((bf16[512,768]{1,0:T(8,128)(2,1)S(1)}, bf16[512,768]{1,0:T(8,128)(2,1)S(1)}, u32[]{:S(2)}, u32[]{:S(2)}) %collective-permute-start.4) | collective-permute-done | bytes 786464 | tf_op jit(solution)/shard_map/ppermute | solution.py:355
  49.5 1.4 %pair_rates.1 = f32[4,2,128]{2,1,0:T(2,128)S(1)} custom-call(f32[3,128]{1,0:T(4,128)S(1)} %pair_weights.1.together, bf16[512,768]{1,0:T(8,128)(2,1)S(1)} %copy-done.2, bf16[512,768]{1,0:T(8,128)(2,1)S(1)} %collective-permute-done.4.f1, bf16[3,512,512]{2,1,0:T(8,128)(2,1)S(1)} %pair_scores.1.st, bf16[512,768]{1,0:T(8,128)(2,1)S(1)} %get-tuple-element.28.g0, ...), custom_call_target="tpu_custom_call" | custom-call | flops 1207959552 | bytes 5505024 | tf_op jit(solution)/shard_map/pair_rates/pallas_call | solution.py:293
  51.0 6.4 %all_to_all.10 = f32[4,2,128]{2,1,0:T(2,128)S(1)} all-to-all(f32[4,2,128]{2,1,0:T(2,128)S(1)} %pair_rates.1), channel_id=1, replica_groups=mesh['tm'=8,'space'=4] {'space'}, dimensions={0} | all-to-all | bytes 8192 | tf_op jit(solution)/shard_map/all_to_all | solution.py:429
  57.4 4.4 %all-to-all-start = ((bf16[4,128,1536]{2,1,0:T(8,128)(2,1)}), bf16[4,128,1536]{2,1,0:T(8,128)(2,1)S(1)}, u32[]{:S(2)}, u32[]{:S(2)}) async-start(bf16[4,128,1536]{2,1,0:T(8,128)(2,1)} %bitcast.2), calls=%async_computation | async-start | bytes 3145728 | tf_op jit(solution)/shard_map/all_to_all | solution.py:414
  61.8 1.1 %copy-done.11 = bf16[128,2560]{1,0:T(8,128)(2,1)S(1)} copy-done((bf16[128,2560]{1,0:T(8,128)(2,1)S(1)}, bf16[128,2560]{1,0:T(8,128)(2,1)}, u32[]{:S(2)}) %copy-start.11) | copy-done | bytes 655384
  62.8 6.6 %window_attention.1 = (bf16[128,2560]{1,0:T(8,128)(2,1)}, bf16[128,2560]{1,0:T(8,128)(2,1)}, bf16[128,2560]{1,0:T(8,128)(2,1)}, bf16[2,64,2560]{2,1,0:T(8,128)(2,1)}, bf16[2,64,2560]{2,1,0:T(8,128)(2,1)}) custom-call(s32[2]{0:T(128)S(1)} %copy-done.5, bf16[128,2560]{1,0:T(8,128)(2,1)S(1)} %copy-done.10, bf16[128,2560]{1,0:T(8,128)(2,1)S(1)} %copy-done.11, ...), custom_call_target="tpu_custom_call" | custom-call | flops 1677721600 | bytes 7208960 | tf_op jit(solution)/shard_map/window_attention/pallas_call | solution.py:214
  69.4 0.3 collective-permute-start.2
  69.7 3.4 %collective-permute-start.3 = (bf16[2,64,2560]{2,1,0:T(8,128)(2,1)}, bf16[2,64,2560]{2,1,0:T(8,128)(2,1)S(1)}, u32[]{:S(2)}, u32[]{:S(2)}) collective-permute-start(bf16[2,64,2560]{2,1,0:T(8,128)(2,1)} %get-tuple-element.23), channel_id=1, source_target_pairs={{1,2},{2,1},{5,6},{6,5},{9,10},{10,9},{13,14},{14,13},{17,18},{18,... | collective-permute-start | bytes 1966088 | tf_op jit(solution)/shard_map/ppermute | solution.py:361
  73.2 2.1 %collective-permute-start.8 = (f32[128]{0:T(128)S(1)}, f32[128]{0:T(128)S(1)}, u32[]{:S(2)}, u32[]{:S(2)}) collective-permute-start(f32[128]{0:T(128)S(1)} %slice_bitcast_fusion), channel_id=1, source_target_pairs={{4,0},{8,4},{12,8},{16,12},{20,16},{24,20},{28,24},{5,1},{9,5},{13... | collective-permute-start | bytes 1544 | tf_op jit(solution)/shard_map/ppermute | solution.py:355
  75.3 5.5 %all-to-all-done.parts = bf16[4,128,1536]{2,1,0:T(8,128)(2,1)S(1)} async-done(((bf16[4,128,1536]{2,1,0:T(8,128)(2,1)}), bf16[4,128,1536]{2,1,0:T(8,128)(2,1)S(1)}, u32[]{:S(2)}, u32[]{:S(2)}) %all-to-all-start) | async-done | bytes 1572896 | tf_op jit(solution)/shard_map/all_to_all | solution.py:414
  80.8 0.9 %sum_parts.1 = bf16[128,1536]{1,0:T(8,128)(2,1)} custom-call(bf16[4,128,1536]{2,1,0:T(8,128)(2,1)S(1)} %all-to-all-done.parts), custom_call_target="tpu_custom_call" | custom-call | flops 786432 | bytes 1572864 | tf_op jit(solution)/shard_map/sum_parts/pallas_call | solution.py:341
  81.8 6.4 %collective-permute-done.3.mx = bf16[2,64,2560]{2,1,0:T(8,128)(2,1)S(1)} collective-permute-done((bf16[2,64,2560]{2,1,0:T(8,128)(2,1)}, bf16[2,64,2560]{2,1,0:T(8,128)(2,1)S(1)}, u32[]{:S(2)}, u32[]{:S(2)}) %collective-permute-start.3) | collective-permute-done | bytes 655392 | tf_op jit(solution)/shard_map/ppermute | solution.py:361
  88.1 2.7 %add_margins.1 = (bf16[128,2560]{1,0:T(8,128)(2,1)}, bf16[128,2560]{1,0:T(8,128)(2,1)}) custom-call(s32[2]{0:T(128)S(1)} %copy-done.5, bf16[128,2560]{1,0:T(8,128)(2,1)} %get-tuple-element.20.dk, bf16[128,2560]{1,0:T(8,128)(2,1)} %get-tuple-element.21.dv, ...), custom_call_target="tpu_custom_call", output_to_operand_aliasing={{0}: (1, {}), {1}: (2, {})} | custom-call | flops 655360 | bytes 3932160 | tf_op jit(solution)/shard_map/add_margins/pallas_call | solution.py:320
  90.8 0.5 bitcast_add_fusion
  (27 shorter events, 0.1 us)
Async XLA Ops:
  1.2 10.3 %copy-start.1 = (bf16[512,1536]{1,0:T(8,128)(2,1)S(1)}, bf16[512,1536]{1,0:T(8,128)(2,1)}, u32[]{:S(2)}) copy-start(bf16[512,1536]{1,0:T(8,128)(2,1)} %q0.1) | copy-start | bytes 4718596
  5.4 56.3 %collective-permute-start = (bf16[2,64,2560]{2,1,0:T(8,128)(2,1)}, bf16[2,64,2560]{2,1,0:T(8,128)(2,1)}, u32[]{:S(2)}, u32[]{:S(2)}) collective-permute-start(bf16[2,64,2560]{2,1,0:T(8,128)(2,1)} %get-tuple-element.17), channel_id=1, source_target_pairs={{0,1},{2,3},{1,0},{3,2},{4,5},{6,7},{5,4},{7,6},{8,9},{10,11},{9,8... | collective-permute-start | bytes 1966088 | tf_op jit(solution)/shard_map/ppermute | solution.py:361
  6.1 55.6 %collective-permute-start.1 = (bf16[2,64,2560]{2,1,0:T(8,128)(2,1)}, bf16[2,64,2560]{2,1,0:T(8,128)(2,1)}, u32[]{:S(2)}, u32[]{:S(2)}) collective-permute-start(bf16[2,64,2560]{2,1,0:T(8,128)(2,1)} %get-tuple-element.18), channel_id=1, source_target_pairs={{1,2},{2,1},{5,6},{6,5},{9,10},{10,9},{13,14},{14,13},{17,18},{18,... | collective-permute-start | bytes 1966088 | tf_op jit(solution)/shard_map/ppermute | solution.py:361
  9.2 18.6 %copy-start.2 = (bf16[512,768]{1,0:T(8,128)(2,1)S(1)}, bf16[512,768]{1,0:T(8,128)(2,1)}, u32[]{:S(2)}) copy-start(bf16[512,768]{1,0:T(8,128)(2,1)} %f0.1) | copy-start | bytes 2359300
  9.2 22.2 %copy-start.5 = (s32[2]{0:T(128)S(1)}, s32[2]{0:T(128)}, u32[]{:S(2)}) copy-start(s32[2]{0:T(128)} %pad_add_fusion.scal) | copy-start | bytes 28
  9.2 21.7 %collective-permute-start.5 = (bf16[512,1536]{1,0:T(8,128)(2,1)}, bf16[512,1536]{1,0:T(8,128)(2,1)S(1)}, u32[]{:S(2)}, u32[]{:S(2)}) collective-permute-start(bf16[512,1536]{1,0:T(8,128)(2,1)} %get-tuple-element.27), channel_id=1, source_target_pairs={{9,1},{11,3},{0,4},{13,5},{2,6},{15,7},{4,8},{17,9},{6,10},{19,11}... | collective-permute-start | bytes 4718600 | tf_op jit(solution)/shard_map/ppermute | solution.py:372
  11.5 1.7 %copy-start.6 = (bf16[1,1536,768]{2,1,0:T(8,128)(2,1)S(1)}, bf16[1,1536,768]{2,1,0:T(8,128)(2,1)}, u32[]{:S(2)}) copy-start(bf16[1,1536,768]{2,1,0:T(8,128)(2,1)} %gw.1) | copy-start | bytes 7077892
  13.2 1.7 %copy-start.7 = (bf16[1,1536,768]{2,1,0:T(8,128)(2,1)S(1)}, bf16[1,1536,768]{2,1,0:T(8,128)(2,1)}, u32[]{:S(2)}) copy-start(bf16[1,1536,768]{2,1,0:T(8,128)(2,1)} %uw.1) | copy-start | bytes 7077892
  14.8 1.7 %copy-start.8 = (bf16[1,768,1536]{2,1,0:T(8,128)(2,1)S(1)}, bf16[1,768,1536]{2,1,0:T(8,128)(2,1)}, u32[]{:S(2)}) copy-start(bf16[1,768,1536]{2,1,0:T(8,128)(2,1)} %dw.1) | copy-start | bytes 7077892
  16.5 1.4 %copy-start.9 = (bf16[512,1536]{1,0:T(8,128)(2,1)S(1)}, bf16[512,1536]{1,0:T(8,128)(2,1)}, u32[]{:S(2)}) copy-start(bf16[512,1536]{1,0:T(8,128)(2,1)} %og.1) | copy-start | bytes 4718596
  17.9 13.4 %copy-start.12 = (s32[4]{0:T(128)S(1)}, s32[4]{0:T(128)}, u32[]{:S(2)}) copy-start(s32[4]{0:T(128)} %clips.1) | copy-start | bytes 52
  25.5 8.8 %copy-start = (bf16[512,1536]{1,0:T(8,128)(2,1)S(1)}, bf16[512,1536]{1,0:T(8,128)(2,1)}, u32[]{:S(2)}) copy-start(bf16[512,1536]{1,0:T(8,128)(2,1)} %k0.1) | copy-start | bytes 4718596
  25.6 20.2 %collective-permute-start.7 = (bf16[512,768]{1,0:T(8,128)(2,1)S(1)}, bf16[512,768]{1,0:T(8,128)(2,1)S(1)}, u32[]{:S(2)}, u32[]{:S(2)}) collective-permute-start(bf16[512,768]{1,0:T(8,128)(2,1)S(1)} %get-tuple-element.28.g0), channel_id=1, source_target_pairs={{8,0},{12,4},{16,8},{20,12},{24,16},{28,20},{9,1},{13,5},{17,9},{2... | collective-permute-start | bytes 2359304 | tf_op jit(solution)/shard_map/ppermute | solution.py:355
  27.7 21.8 %collective-permute-start.4 = (bf16[512,768]{1,0:T(8,128)(2,1)S(1)}, bf16[512,768]{1,0:T(8,128)(2,1)S(1)}, u32[]{:S(2)}, u32[]{:S(2)}) collective-permute-start(bf16[512,768]{1,0:T(8,128)(2,1)S(1)} %copy-done.2), channel_id=1, source_target_pairs={{0,4},{4,8},{8,12},{12,16},{16,20},{20,24},{24,28},{1,5},{5,9},{9,... | collective-permute-start | bytes 2359304 | tf_op jit(solution)/shard_map/ppermute | solution.py:355
  30.9 3.5 %collective-permute-start.6 = (bf16[512,1536]{1,0:T(8,128)(2,1)S(1)}, bf16[512,1536]{1,0:T(8,128)(2,1)S(1)}, u32[]{:S(2)}, u32[]{:S(2)}) collective-permute-start(bf16[512,1536]{1,0:T(8,128)(2,1)S(1)} %collective-permute-done.5.refs_0_), channel_id=1, source_target_pairs={{0,1},{2,3},{1,0},{3,2},{4,5},{6,7},{5,4},{7,6},{8,9},{10,11},{9,8... | collective-permute-start | bytes 4718600 | tf_op jit(solution)/shard_map/ppermute | solution.py:361
  57.4 4.4 %copy-start.3 = (bf16[128,2560]{1,0:T(8,128)(2,1)S(1)}, bf16[128,2560]{1,0:T(8,128)(2,1)}, u32[]{:S(2)}) copy-start(bf16[128,2560]{1,0:T(8,128)(2,1)} %k.3) | copy-start | bytes 1966084
  57.4 4.4 %copy-start.4 = (bf16[128,2560]{1,0:T(8,128)(2,1)S(1)}, bf16[128,2560]{1,0:T(8,128)(2,1)}, u32[]{:S(2)}) copy-start(bf16[128,2560]{1,0:T(8,128)(2,1)} %v.3) | copy-start | bytes 1966084
  57.4 4.4 %copy-start.10 = (bf16[128,2560]{1,0:T(8,128)(2,1)S(1)}, bf16[128,2560]{1,0:T(8,128)(2,1)}, u32[]{:S(2)}) copy-start(bf16[128,2560]{1,0:T(8,128)(2,1)} %q.2) | copy-start | bytes 1966084
  57.4 23.4 %all-to-all-start = ((bf16[4,128,1536]{2,1,0:T(8,128)(2,1)}), bf16[4,128,1536]{2,1,0:T(8,128)(2,1)S(1)}, u32[]{:S(2)}, u32[]{:S(2)}) async-start(bf16[4,128,1536]{2,1,0:T(8,128)(2,1)} %bitcast.2), calls=%async_computation | async-start | bytes 3145728 | tf_op jit(solution)/shard_map/all_to_all | solution.py:414
  61.8 1.1 %copy-start.11 = (bf16[128,2560]{1,0:T(8,128)(2,1)S(1)}, bf16[128,2560]{1,0:T(8,128)(2,1)}, u32[]{:S(2)}) copy-start(bf16[128,2560]{1,0:T(8,128)(2,1)} %g.1) | copy-start | bytes 1966084
  69.4 12.3 %collective-permute-start.2 = (bf16[2,64,2560]{2,1,0:T(8,128)(2,1)}, bf16[2,64,2560]{2,1,0:T(8,128)(2,1)S(1)}, u32[]{:S(2)}, u32[]{:S(2)}) collective-permute-start(bf16[2,64,2560]{2,1,0:T(8,128)(2,1)} %get-tuple-element.22), channel_id=1, source_target_pairs={{0,1},{2,3},{1,0},{3,2},{4,5},{6,7},{5,4},{7,6},{8,9},{10,11},{9,8... | collective-permute-start | bytes 1966088 | tf_op jit(solution)/shard_map/ppermute | solution.py:361
  69.7 18.4 %collective-permute-start.3 = (bf16[2,64,2560]{2,1,0:T(8,128)(2,1)}, bf16[2,64,2560]{2,1,0:T(8,128)(2,1)S(1)}, u32[]{:S(2)}, u32[]{:S(2)}) collective-permute-start(bf16[2,64,2560]{2,1,0:T(8,128)(2,1)} %get-tuple-element.23), channel_id=1, source_target_pairs={{1,2},{2,1},{5,6},{6,5},{9,10},{10,9},{13,14},{14,13},{17,18},{18,... | collective-permute-start | bytes 1966088 | tf_op jit(solution)/shard_map/ppermute | solution.py:361
  73.2 17.6 %collective-permute-start.8 = (f32[128]{0:T(128)S(1)}, f32[128]{0:T(128)S(1)}, u32[]{:S(2)}, u32[]{:S(2)}) collective-permute-start(f32[128]{0:T(128)S(1)} %slice_bitcast_fusion), channel_id=1, source_target_pairs={{4,0},{8,4},{12,8},{16,12},{20,16},{24,20},{28,24},{5,1},{9,5},{13... | collective-permute-start | bytes 1544 | tf_op jit(solution)/shard_map/ppermute | solution.py:355
where the time goes:
time: 92 us; the launch traced here: 91.3 us
  Pallas kernels  27.2 us (30%)
  waiting for transfers between devices  26.3 us (29%)
  starting transfers between devices  22 us (24%)
  local copies, waits for them, and re-layouts  7.52 us (8%)
  blocking collectives  6.38 us (7%)
  other arithmetic  1.11 us (1%)
    ppermute x3, waiting for transfers between devices, shifted(): return lax.ppermute(array, axis, pairs)  12 us
    ppermute x5, waiting for transfers between devices, swapped(): return lax.ppermute(array, axis, pairs + [(j, i) for i, j in pairs])  8.83 us
    ppermute x5, starting transfers between devices, swapped(): return lax.ppermute(array, axis, pairs + [(j, i) for i, j in pairs])  7.93 us
    pallas_call x1, Pallas kernels, fast(): pl.pallas_call(functools.partial(fast_kernel, step), in_specs=[vmem] * 5,...  7.62 us
    unnamed x26, local copies, waits for them, and re-layouts  7.52 us
    ppermute x3, starting transfers between devices, shifted(): return lax.ppermute(array, axis, pairs)  7.4 us
    pallas_call x1, Pallas kernels, attention(): pl.pallas_call(functools.partial(attention_kernel, reach, last, every), i...  6.56 us
    all_to_all x1, blocking collectives, per_device(): rate = lax.all_to_all(rate, 'space', 0, 0)  6.38 us
  transfers between devices with their start and end apart: 10, of which 5 were waited for; matrix products, arithmetic and copies ran while one was open for 0% of the time, Pallas kernels for 25%

commit v1 on v0

v1 whole, which is shorter than its diff:
```python
import functools
import math

import jax
import jax.numpy as jnp
from jax import lax
from jax.experimental import pallas as pl
from jax.experimental.pallas import tpu as pltpu
from jax.sharding import PartitionSpec as P


HEAD = 128

CONTRACT_LAST = (((1,), (1,)), ((), ()))
CONTRACT_FIRST = (((0,), (0,)), ((), ()))
F32 = jnp.float32
BF16 = jnp.bfloat16


def dot_last(a, b):
    return lax.dot_general(a, b, CONTRACT_LAST, preferred_element_type=F32)


def far(*arrays):
    return [pltpu.with_memory_space_constraint(array, pltpu.HBM) for array in arrays]


def near(*arrays):
    return [pltpu.with_memory_space_constraint(array, pltpu.VMEM) for array in arrays]


def room(least, needed):
    return pltpu.CompilerParams(vmem_limit_bytes=max(least << 20, needed))


def cost(flops, moved, transcendentals=0):
    return pl.CostEstimate(flops=flops, bytes_accessed=moved, transcendentals=transcendentals)


def pick_kernel(scal, fk, fq, out, sem):
    odd = scal[0] % 2
    copy = pltpu.make_async_copy(fk, out, sem)
    pl.when(odd == 0)(copy.start)
    pl.when(odd == 1)(pltpu.make_async_copy(fq, out, sem).start)
    copy.wait()


def pick(scal, fast_key, fast_query):
    return pl.pallas_call(
        pick_kernel,
        in_specs=[pl.BlockSpec(memory_space=pltpu.SMEM)]
        + [pl.BlockSpec(memory_space=pltpu.HBM)] * 2,
        out_specs=pl.BlockSpec(memory_space=pltpu.VMEM),
        out_shape=pltpu.VMEM(fast_key.shape, BF16),
        scratch_shapes=[pltpu.SemaphoreType.DMA],
        cost_estimate=cost(0, 4 * fast_key.size),
        compiler_params=pltpu.CompilerParams(vmem_limit_bytes=4 << 20),
        name="pick_outgoing",
    )(scal, *far(fast_key, fast_query))


def halos_kernel(scal, k, v, hc, hx, sems):
    reach = hc.shape[1]
    odd = scal[0] % 2
    copies = []
    for i, source in enumerate((k, v)):
        for j, (half, at) in enumerate(((hx, odd), (hc, 1 - odd))):
            rows = pl.ds(pl.multiple_of(at * reach, reach), reach)
            copies.append(pltpu.make_async_copy(source.at[rows], half.at[i], sems.at[i, j]))
    for copy in copies:
        copy.start()
    for copy in copies:
        copy.wait()


def pick_halos(scal, key, value):
    rows, width = key.shape
    half = jax.ShapeDtypeStruct((2, rows // 2, width), BF16)
    return pl.pallas_call(
        halos_kernel,
        in_specs=[pl.BlockSpec(memory_space=pltpu.SMEM)]
        + [pl.BlockSpec(memory_space=pltpu.HBM)] * 2,
        out_specs=[pl.BlockSpec(memory_space=pltpu.VMEM)] * 2,
        out_shape=[half, half],
        scratch_shapes=[pltpu.SemaphoreType.DMA((2, 2))],
        cost_estimate=cost(0, 8 * rows * width),
        compiler_params=pltpu.CompilerParams(vmem_limit_bytes=4 << 20),
        name="pick_halos",
    )(scal, *far(key, value))


def weights_kernel(shifts, tiles, scal, clips, out):
    at = lax.div(scal[0], tiles)
    starts, total = [], 0
    for n in range(clips.shape[0]):
        starts.append(total)
        total = total + clips[n]

    def together(u, v):
        apart = jnp.bool_(False)
        for x in range(1 - u, v + 1):
            for start in starts:
                apart = apart | (start == at + x)
        return jnp.where(apart, 0.0, 1.0)

    for n, (u, v) in enumerate([(1, 0)] + [(u, v) for v in shifts for u in (0, 1)]):
        out[n : n + 1, :] = jnp.full((1, out.shape[1]), together(u, v), F32)


def pair_weights(scal, clips, shifts, tiles):
    return pl.pallas_call(
        functools.partial(weights_kernel, shifts, tiles),
        in_specs=[pl.BlockSpec(memory_space=pltpu.SMEM)] * 2,
        out_specs=pl.BlockSpec(memory_space=pltpu.VMEM),
        out_shape=jax.ShapeDtypeStruct((1 + 2 * len(shifts), HEAD), F32),
        cost_estimate=cost(20 * 10**9, 4096),
        compiler_params=pltpu.CompilerParams(vmem_limit_bytes=1 << 20),
        name="pair_weights",
    )(scal, clips)


def fast_kernel(step, q, og, gw, uw, dw, gate_out, part_out, gate_grad, up_grad, part, sems):
    for j in range(gw.shape[2] // step):
        cols = slice(j * step, (j + 1) * step)
        gate = jnp.dot(q[...], gw[0, :, cols], preferred_element_type=F32)
        up = jnp.dot(q[...], uw[0, :, cols], preferred_element_type=F32)
        hidden = dot_last(og[...], dw[0, cols, :])
        sig = jax.nn.sigmoid(gate)
        gate_grad[:, cols] = (hidden * up * sig * (1.0 + gate * (1.0 - sig))).astype(BF16)
        up_grad[:, cols] = (hidden * (gate * sig)).astype(BF16)
    copies = [pltpu.make_async_copy(gate_grad, gate_out, sems.at[0])]
    copies[0].start()
    for j in range(q.shape[1] // step):
        rows = slice(j * step, (j + 1) * step)
        part[:, rows] = (
            dot_last(gate_grad[...], gw[0, rows, :]) + dot_last(up_grad[...], uw[0, rows, :])
        ).astype(BF16)
        copy = pltpu.make_async_copy(part.at[:, rows], part_out.at[:, rows], sems.at[1 + j])
        copy.start()
        copies.append(copy)
    for copy in copies:
        copy.wait()


def fast(query, outgrad, gate_w, up_w, down_w):
    rows, width = query.shape
    hidden = gate_w.shape[2]
    step = next(s for s in (256, 128) if hidden % s == 0 and width % s == 0)
    vmem = pl.BlockSpec(memory_space=pltpu.VMEM)
    return pl.pallas_call(
        functools.partial(fast_kernel, step),
        in_specs=[vmem] * 5,
        out_specs=[pl.BlockSpec(memory_space=pltpu.HBM)] * 2,
        out_shape=[pltpu.HBM((rows, n), BF16) for n in (hidden, width)],
        scratch_shapes=[
            pltpu.VMEM((rows, hidden), BF16),
            pltpu.VMEM((rows, hidden), BF16),
            pltpu.VMEM((rows, width), BF16),
            pltpu.SemaphoreType.DMA((1 + width // step,)),
        ],
        cost_estimate=cost(20 * 10**9, 6 * width * hidden + 8 * rows * width),
        compiler_params=room(16, (6 * rows * width + 6 * width * hidden + 4 * rows * hidden) * 5 // 4),
        name="fast_weights",
    )(query, outgrad, gate_w, up_w, down_w)


def bias_kernel(reach, last, scal, out):
    keys, rows = out.shape[0], out.shape[1] // 2
    at = lax.rem(scal[0], last // rows)
    even = at % 2 == 0
    key_row = lax.broadcasted_iota(jnp.int32, (keys, rows), 0)
    query_row = lax.broadcasted_iota(jnp.int32, (keys, rows), 1)
    shift_c = jnp.where(even, 0, -(rows + reach))
    shift_x = jnp.where(even, -(rows + 2 * reach), -reach)
    key_pos = key_row + jnp.where(
        key_row < rows, 0, jnp.where(key_row < rows + reach, shift_c, shift_x)
    )
    offset = at * rows
    live = (key_pos + offset >= 0) & (key_pos + offset < last)
    bias = jnp.where(live & (jnp.abs(key_pos - query_row) <= reach), 0.0, -1e30)
    out[:, :rows] = bias
    out[:, rows:] = bias


def window_bias(scal, rows, reach, last):
    return pl.pallas_call(
        functools.partial(bias_kernel, reach, last),
        in_specs=[pl.BlockSpec(memory_space=pltpu.SMEM)],
        out_specs=pl.BlockSpec(memory_space=pltpu.VMEM),
        out_shape=jax.ShapeDtypeStruct((rows + 2 * reach, 2 * rows), F32),
        cost_estimate=cost(20 * 10**9, 16 * rows * rows),
        compiler_params=pltpu.CompilerParams(vmem_limit_bytes=2 << 20),
        name="window_bias",
    )(scal)


def attention_kernel(every, bias, *refs):
    sources, outs, local, held = refs[:6], refs[6:11], refs[11:17], refs[17:22]
    load_sems, sems = refs[22:]
    q, g, k, v, hc, hx = local
    dk_own, dv_own, dq, mc, mx = held
    loads, copies = [], []
    for at in range(0, q.shape[1], every):
        part = (Ellipsis, slice(at, at + every))
        for i, (source, ref) in enumerate(zip(sources, local)):
            sem = load_sems.at[at // every, i]
            loads.append(pltpu.make_async_copy(source.at[part], ref.at[part], sem))
            loads[-1].start()
    rows, reach = q.shape[0], hc.shape[1]
    wide = 2 * HEAD
    scaling = 1.0 / math.sqrt(HEAD)
    zero = jnp.zeros((rows, HEAD), BF16)

    def diagonal(ref, at):
        head, other = ref[:, at : at + HEAD], ref[:, at + HEAD : at + wide]
        return jnp.concatenate(
            [jnp.concatenate([head, zero], axis=1), jnp.concatenate([zero, other], axis=1)], axis=0
        )

    for start in range(0, q.shape[1], wide):
        if start % every == 0:
            for copy in loads[start // every * 6 : start // every * 6 + 6]:
                copy.wait()
        col = slice(start, start + wide)
        kk = jnp.concatenate([k[:, col], hc[0, :, col], hx[0, :, col]], axis=0)
        vv = jnp.concatenate([v[:, col], hc[1, :, col], hx[1, :, col]], axis=0)
        qd, gd = diagonal(q, start), diagonal(g, start)
        scores = dot_last(kk, qd) * scaling + bias[...]
        exponent = jnp.exp(scores - jnp.max(scores, axis=0, keepdims=True))
        probs = exponent * (1.0 / jnp.sum(exponent, axis=0, keepdims=True))
        probs_b = probs.astype(BF16)
        dprobs = dot_last(vv, gd)
        delta = jnp.sum(probs_b.astype(F32) * dprobs, axis=0, keepdims=True)
        dscores_b = (probs * (dprobs - delta)).astype(BF16)
        dv = jnp.dot(probs_b, gd, preferred_element_type=F32)
        dk = jnp.dot(dscores_b, qd, preferred_element_type=F32) * scaling
        both = lax.dot_general(dscores_b, kk, CONTRACT_FIRST, preferred_element_type=F32)
        dq[:, start : start + HEAD] = (both[:rows, :HEAD] * scaling).astype(BF16)
        dq[:, start + HEAD : start + wide] = (both[rows:, HEAD:] * scaling).astype(BF16)
        for i, (grad, own) in enumerate(((dk, dk_own), (dv, dv_own))):
            own[:, col] = grad[:rows].astype(BF16)
            mc[i, :, col] = grad[rows : rows + reach].astype(BF16)
            mx[i, :, col] = grad[rows + reach :].astype(BF16)
        if (start + wide) % every == 0:
            done = (Ellipsis, slice(start + wide - every, start + wide))
            for i, (ref, out) in enumerate(zip(held, outs)):
                sem = sems.at[start // every, i]
                copies.append(pltpu.make_async_copy(ref.at[done], out.at[done], sem))
                copies[-1].start()
    for copy in copies:
        copy.wait()


def attention(bias, query, out_grad, key, value, halo_c, halo_x):
    rows, width = query.shape
    reach = halo_c.shape[1]
    keys = rows + 2 * reach
    every = next(n for n in (10, 4, 2) if width % (n * HEAD) == 0) * HEAD
    vmem = pl.BlockSpec(memory_space=pltpu.VMEM)
    flat, half = (rows, width), (2, reach, width)
    return pl.pallas_call(
        functools.partial(attention_kernel, every),
        in_specs=[vmem] + [pl.BlockSpec(memory_space=pltpu.HBM)] * 6,
        out_specs=[pl.BlockSpec(memory_space=pltpu.HBM)] * 5,
        out_shape=[pltpu.HBM(x, BF16) for x in (flat, flat, flat, half, half)],
        scratch_shapes=[pltpu.VMEM(x, BF16) for x in [flat] * 4 + [half] * 2 + [flat] * 3 + [half] * 2]
        + [pltpu.SemaphoreType.DMA((width // every, 6)), pltpu.SemaphoreType.DMA((width // every, 5))],
        cost_estimate=cost(
            20 * rows * keys * width, 22 * width * rows, width // HEAD * rows * keys
        ),
        compiler_params=pltpu.CompilerParams(vmem_limit_bytes=14 << 20),
        name="window_attention",
    )(bias, *far(query, out_grad, key, value, halo_c, halo_x))


def scores_kernel(n_two, scal, k0, q0, *refs):
    paired, received, out = refs[:n_two], refs[n_two : 2 * n_two], refs[2 * n_two]
    local, held, load_sems, sems = refs[2 * n_two + 1 : 3 * n_two + 1], *refs[3 * n_two + 1 :]
    odd = scal[0] % 2
    loads = [
        pltpu.make_async_copy(source, ref, load_sems.at[n])
        for n, (source, ref) in enumerate(zip(received, local))
    ]
    for copy in loads:
        copy.start()

    def work(side):
        arrays = []
        for n in range(n_two):
            both = [(local[n], loads[n]), (paired[n], None)]
            arrays += both[::-1] if side else both
        k1, queries = arrays[0], arrays[1:]
        pairs = [(0, (q0, None), k1)]
        for n in range((held.shape[0] - 1) // 2):
            pairs += [(2 * n + 1, queries[n], (k0, None)), (2 * n + 2, queries[n], k1)]
        pairs.sort(key=lambda pair: sum(load is not None for _, load in pair[1:]))
        copies, waited = [], []
        for n, (q, load_q), (k, load_k) in pairs:
            for load in (load_q, load_k):
                if load is not None and id(load) not in waited:
                    load.wait()
                    waited.append(id(load))
            held[n] = dot_last(q[...], k[...]).astype(BF16)
            copies.append(pltpu.make_async_copy(held.at[n], out.at[n], sems.at[n]))
            copies[-1].start()
        for copy in [load for load in loads if id(load) not in waited] + copies:
            copy.wait()

    pl.when(odd == 0)(functools.partial(work, 0))
    pl.when(odd == 1)(functools.partial(work, 1))


def scores(scal, k0, q0, received, paired, pairs):
    rows, width = k0.shape
    n_two = len(received)
    vmem = pl.BlockSpec(memory_space=pltpu.VMEM)
    hbm = pl.BlockSpec(memory_space=pltpu.HBM)
    return pl.pallas_call(
        functools.partial(scores_kernel, n_two),
        in_specs=[pl.BlockSpec(memory_space=pltpu.SMEM)] + [vmem] * (2 + n_two) + [hbm] * n_two,
        out_specs=hbm,
        out_shape=pltpu.HBM((pairs, rows, rows), BF16),
        scratch_shapes=[pltpu.VMEM((rows, width), BF16)] * n_two
        + [
            pltpu.VMEM((pairs, rows, rows), BF16),
            pltpu.SemaphoreType.DMA((n_two,)),
            pltpu.SemaphoreType.DMA((pairs,)),
        ],
        cost_estimate=cost(20 * 10**9, 2 * pairs * rows * rows),
        compiler_params=room(20, 14 * pairs * rows * rows // 3 + 4 * (1 + n_two) * rows * width),
        name="pair_scores",
    )(scal, k0, q0, *paired, *far(*received))


def rates_kernel(share, n_far, scal, together, st, g0, *refs):
    sources, own_out, before_out = refs[:n_far], refs[n_far], refs[n_far + 1]
    held, sems = refs[n_far + 2 : -1], refs[-1]
    f1, moved, f0 = held[0], held[1:-1], held[-1]
    loads = [
        pltpu.make_async_copy(source, ref, sems.at[n])
        for n, (source, ref) in enumerate(zip(sources, held))
    ]
    for copy in loads:
        copy.start()
    lanes = own_out.shape[2]

    def pair(n, g, f):
        products = dot_last(g[...], f[...])
        summed = jnp.sum(st[n].astype(F32) * products, axis=0, keepdims=True)
        return summed * (together[n : n + 1, 0:1] * share)

    loads[0].wait()
    before = pair(0, g0, f1)
    own = jnp.zeros_like(before)
    for n, g in enumerate(moved):
        loads[1 + n].wait()
        before += pair(2 * n + 2, g, f1)
    loads[-1].wait()
    for n, g in enumerate(moved):
        own += pair(2 * n + 1, g, f0)
    for n in range(own_out.shape[0]):
        part = slice(n * lanes, (n + 1) * lanes)
        own_out[n] = own[:, part]
        before_out[n] = before[:, part]


def rates(scal, together, st, f0, f1, g0, moved, tiles):
    rows, width = f0.shape
    pairs = st.shape[0]
    vmem = pl.BlockSpec(memory_space=pltpu.VMEM)
    n_far = 2 + len(moved)
    return pl.pallas_call(
        functools.partial(rates_kernel, 1.0 / rows, n_far),
        in_specs=[pl.BlockSpec(memory_space=pltpu.SMEM)]
        + [vmem] * 3
        + [pl.BlockSpec(memory_space=pltpu.HBM)] * n_far,
        out_specs=[vmem] * 2,
        out_shape=[jax.ShapeDtypeStruct((tiles, 1, rows // tiles), F32)] * 2,
        scratch_shapes=[pltpu.VMEM((rows, width), BF16)] * n_far
        + [pltpu.SemaphoreType.DMA((n_far,))],
        cost_estimate=cost(
            2 * pairs * rows * rows * width, 2 * (pairs * rows * rows + (2 + pairs) * rows * width)
        ),
        compiler_params=room(14, (2 * pairs + 16) * rows * rows + 4 * (1 + n_far) * rows * width),
        name="pair_rates",
    )(scal, *near(together, st, g0), *far(f1, *moved, f0))


def fold_kernel(bit, scal, kept, received, *outs):
    if len(outs) == 1:
        outs[0][...] = kept[...] + received[...]
        return
    keep, send = outs
    side = lax.rem(lax.div(scal[0], 1 << bit), 2)
    for n in range(kept.shape[0]):
        total = kept[n] + received[n]

        def put(ref):
            ref[n // 2] = total

        pl.when(side == n % 2)(functools.partial(put, keep))
        pl.when(side != n % 2)(functools.partial(put, send))


def fold(scal, kept, received, bit):
    vmem = pl.BlockSpec(memory_space=pltpu.VMEM)
    last = kept.shape[0] == 1
    shape = kept.shape if last else (kept.shape[0] // 2, *kept.shape[1:])
    out = jax.ShapeDtypeStruct(shape, kept.dtype)
    return pl.pallas_call(
        functools.partial(fold_kernel, bit),
        in_specs=[pl.BlockSpec(memory_space=pltpu.SMEM), vmem, vmem],
        out_specs=[vmem] if last else [vmem] * 2,
        out_shape=[out] if last else [out] * 2,
        cost_estimate=cost(kept.size, 12 * kept.size),
        compiler_params=pltpu.CompilerParams(vmem_limit_bytes=1 << 20),
        name="fold_rates",
    )(scal, kept, received)


def margins_kernel(parts, scal, dk, dv, mc, mx, *refs):
    outs, (own, core, chip, done), (load_sems, sems) = refs[:2], refs[2:6], refs[6:]
    even = scal[0] % 2 == 0
    reach = mc.shape[1]
    step = dk.shape[1] // parts
    steps = [(i, slice(n * step, (n + 1) * step)) for i in range(2) for n in range(parts)]
    loads, copies = [], []
    for n, (i, cols) in enumerate(steps):
        moves = (
            ((dk, dv)[i].at[:, cols], own.at[i, :, cols]),
            (mc.at[i, :, cols], core.at[i, :, cols]),
            (mx.at[i, :, cols], chip.at[i, :, cols]),
        )
        loads.append([pltpu.make_async_copy(*move, load_sems.at[n, j]) for j, move in enumerate(moves)])
        for copy in loads[-1]:
            copy.start()
    for n, (i, cols) in enumerate(steps):
        for copy in loads[n]:
            copy.wait()
        from_c, from_x = core[i, :, cols].astype(F32), chip[i, :, cols].astype(F32)
        head = jnp.where(even, from_x, from_c)
        tail = jnp.where(even, from_c, from_x)
        done[i, :reach, cols] = (own[i, :reach, cols].astype(F32) + head).astype(BF16)
        done[i, reach:, cols] = (own[i, reach:, cols].astype(F32) + tail).astype(BF16)
        copies.append(pltpu.make_async_copy(done.at[i, :, cols], outs[i].at[:, cols], sems.at[n]))
        copies[-1].start()
    for copy in copies:
        copy.wait()


def add_margins(scal, dk, dv, mc, mx):
    rows, width = dk.shape
    parts = next(n for n in (2, 1) if width % (n * HEAD) == 0)
    hbm = pl.BlockSpec(memory_space=pltpu.HBM)
    whole, half = (2, rows, width), (2, rows // 2, width)
    return pl.pallas_call(
        functools.partial(margins_kernel, parts),
        in_specs=[pl.BlockSpec(memory_space=pltpu.SMEM)]
        + [hbm] * 2
        + [pl.BlockSpec(memory_space=pl.ANY)] * 2,
        out_specs=[hbm] * 2,
        out_shape=[pltpu.HBM((rows, width), BF16)] * 2,
        scratch_shapes=[pltpu.VMEM(x, BF16) for x in (whole, half, half, whole)]
        + [pltpu.SemaphoreType.DMA((2 * parts, 3)), pltpu.SemaphoreType.DMA((2 * parts,))],
        cost_estimate=cost(2 * rows * width, 12 * rows * width),
        compiler_params=pltpu.CompilerParams(vmem_limit_bytes=8 << 20),
        name="add_margins",
    )(scal, *far(dk, dv), mc, mx)


def sum_kernel(parts, out):
    total = parts[0].astype(F32)
    for n in range(1, parts.shape[0]):
        total += parts[n].astype(F32)
    out[...] = total.astype(BF16)


def sum_parts(parts):
    vmem = pl.BlockSpec(memory_space=pltpu.VMEM)
    return pl.pallas_call(
        sum_kernel,
        in_specs=[vmem],
        out_specs=vmem,
        out_shape=jax.ShapeDtypeStruct(parts.shape[1:], BF16),
        cost_estimate=cost(parts.size, 2 * parts.size),
        compiler_params=pltpu.CompilerParams(vmem_limit_bytes=8 << 20),
        name="sum_parts",
    )(parts)


def shifted(array, axis, by):
    devices = lax.axis_size(axis)
    pairs = [(i + by, i) for i in range(devices) if 0 <= i + by < devices]
    return lax.ppermute(array, axis, pairs)


def swapped(array, axis, first):
    devices = lax.axis_size(axis)
    pairs = [(i, i + 1) for i in range(first, devices - 1, 2)]
    return lax.ppermute(array, axis, pairs + [(j, i) for i, j in pairs])


def across(array, axis, bit):
    pairs = [(i, i ^ (1 << bit)) for i in range(lax.axis_size(axis))]
    return lax.ppermute(array, axis, pairs)


def moved_apart(array, by_even, by_odd):
    groups, tiles = lax.axis_size("tm"), lax.axis_size("space")
    pairs = []
    for group in range(groups):
        for tile in range(tiles):
            source = group + (by_odd if tile % 2 else by_even)
            if 0 <= source < groups:
                pairs.append((source * tiles + tile, group * tiles + tile))
    return lax.ppermute(array, ("tm", "space"), pairs)


def per_device(
    attn_query,
    attn_key,
    attn_value,
    attn_outgrad,
    fast_query,
    fast_outgrad,
    fast_key,
    gate_weights,
    up_weights,
    down_weights,
    gate_factor,
    clip_groups,
):
    groups, tiles = lax.axis_size("tm"), lax.axis_size("space")
    scal = lax.axis_index(("tm", "space")).astype(jnp.int32).reshape(1)
    rows = fast_query.shape[0]
    tile_rows, _ = attn_query.shape
    most = groups // 2
    shifts = tuple(range(2, most, 2))
    travels = [-1, *shifts]
    travels += travels[-1:] * (len(travels) % 2)

    outgoing = pick(scal, fast_key, fast_query)
    received = []
    for n in range(0, len(travels), 2):
        array = outgoing if n == 0 else fast_query
        received.append(moved_apart(array, travels[n], travels[n + 1]))
    together = pair_weights(scal, clip_groups, shifts, tiles)
    factor_before = shifted(gate_factor, "tm", -1)
    halo_c, halo_x = pick_halos(scal, attn_key, attn_value)
    halo_c = swapped(halo_c, "space", 0)
    halo_x = swapped(halo_x, "space", 1)

    gate_grad_b, input_part = fast(fast_query, fast_outgrad, gate_weights, up_weights, down_weights)
    moved = []
    for v in shifts:
        moved.append(shifted(gate_grad_b, "tm", v))

    parts = lax.all_to_all(input_part.reshape(tiles, tile_rows, -1), "space", 0, 0)

    bias = window_bias(scal, tile_rows, tile_rows // 2, rows)
    dk, dv, query_grad, margin_c, margin_x = attention(
        bias, attn_query, attn_outgrad, attn_key, attn_value, halo_c, halo_x
    )
    margin_c = swapped(margin_c, "space", 0)
    margin_x = swapped(margin_x, "space", 1)

    paired = []
    for array in received:
        paired.append(swapped(array, "space", 0))
    pairs = 1 + 2 * len(shifts)
    st = scores(scal, fast_key, fast_query, received, paired, pairs)
    fast_grad = sum_parts(parts)
    own, before = rates(scal, together, st, gate_factor, factor_before, gate_grad_b, moved, tiles)
    arrived = shifted(before, "tm", 1)
    key_grad, value_grad = add_margins(scal, dk, dv, margin_c, margin_x)
    kept = own
    for bit in range(tiles.bit_length()):
        kept, *rest = fold(scal, kept, arrived, bit)
        if rest:
            arrived = across(rest[0], "space", bit)
    rate_grad = kept.reshape(-1)
    return query_grad, key_grad, value_grad, fast_grad, rate_grad


def solution(mesh):
    over = ("tm", "space")
    tiled = P(over, None)
    in_specs = (
        (tiled,) * 4
        + (P("tm", None),) * 3
        + (P("tm", None, "space"),) * 2
        + (P("tm", "space", None), P("tm", "space"), P())
    )
    return jax.shard_map(
        per_device,
        mesh=mesh,
        in_specs=in_specs,
        out_specs=(tiled,) * 4 + (P(over),),
        check_vma=False,
    )
```

time: 92 us -> 77.4 us (0.84)
  the two profiles are of different devices: /device:TPU:25 before, /device:TPU:0 now
where the time goes in v1:
time: 77.4 us; the launch traced here: 76.8 us
  starting transfers between devices  32.4 us (42%)
  Pallas kernels  31.6 us (41%)
  local copies, waits for them, and re-layouts  6.16 us (8%)
  waiting for transfers between devices  5.85 us (8%)
  between operations  0.84 us (1%)
    ppermute x5, starting transfers between devices, swapped(): return lax.ppermute(array, axis, pairs + [(j, i) for i, j in pairs])  14.3 us
    pallas_call x1, Pallas kernels, fast(): pl.pallas_call(functools.partial(fast_kernel, step), in_specs=[vmem] * 5,...  7.33 us
    pallas_call x1, Pallas kernels, attention(): pl.pallas_call(functools.partial(attention_kernel, every), in_specs=[vmem...  7.31 us
    unnamed x18, local copies, waits for them, and re-layouts  6.16 us
    ppermute x1, starting transfers between devices, moved_apart(): return lax.ppermute(array, ('tm', 'space'), pairs)  6.06 us
    ppermute x3, starting transfers between devices, shifted(): return lax.ppermute(array, axis, pairs)  5.78 us
    ppermute x3, waiting for transfers between devices, shifted(): return lax.ppermute(array, axis, pairs)  5.01 us
    pallas_call x1, Pallas kernels, scores(): pl.pallas_call(functools.partial(scores_kernel, n_two), in_specs=[pl.Bloc...  4.08 us
  transfers between devices with their start and end apart: 12, of which 2 were waited for; matrix products, arithmetic and copies ran while one was open for 0% of the time, Pallas kernels for 37%

profile of v1, /device:TPU:0, one launch (start us, length us, event | category | flops | bytes accessed | tf_op | source)
XLA Modules:
  0.0 76.8 jit_solution(13407160817803569635)
XLA Ops:
  0.7 2.8 %pick_outgoing.1 = bf16[512,1536]{1,0:T(8,128)(2,1)} custom-call(s32[1]{0:T(128)} %bitcast.scal, bf16[512,1536]{1,0:T(8,128)(2,1)} %k0.1, bf16[512,1536]{1,0:T(8,128)(2,1)} %q0.1), custom_call_target="tpu_custom_call" | custom-call | bytes 3145728 | tf_op jit(solution)/shard_map/pick_outgoing/pallas_call | solution.py:49
  3.4 6.1 %collective-permute-start.4 = (bf16[512,1536]{1,0:T(8,128)(2,1)}, bf16[512,1536]{1,0:T(8,128)(2,1)}, u32[]{:S(2)}, u32[]{:S(2)}) collective-permute-start(bf16[512,1536]{1,0:T(8,128)(2,1)} %pick_outgoing.1), channel_id=1, source_target_pairs={{9,1},{11,3},{0,4},{13,5},{2,6},{15,7},{4,8},{17,9},{6,10},{19,11}... | collective-permute-start | bytes 4718600 | tf_op jit(solution)/shard_map/ppermute | solution.py:516
  9.5 1.7 %copy-done.5 = bf16[1,1536,768]{2,1,0:T(8,128)(2,1)S(1)} copy-done((bf16[1,1536,768]{2,1,0:T(8,128)(2,1)S(1)}, bf16[1,1536,768]{2,1,0:T(8,128)(2,1)}, u32[]{:S(2)}) %copy-start.5) | copy-done | bytes 2359320
  11.1 1.7 %copy-done.6 = bf16[1,768,1536]{2,1,0:T(8,128)(2,1)S(1)} copy-done((bf16[1,768,1536]{2,1,0:T(8,128)(2,1)S(1)}, bf16[1,768,1536]{2,1,0:T(8,128)(2,1)}, u32[]{:S(2)}) %copy-start.6) | copy-done | bytes 2359320
  12.8 1.4 %copy-done.7 = bf16[512,1536]{1,0:T(8,128)(2,1)S(1)} copy-done((bf16[512,1536]{1,0:T(8,128)(2,1)S(1)}, bf16[512,1536]{1,0:T(8,128)(2,1)}, u32[]{:S(2)}) %copy-start.7) | copy-done | bytes 1572888
  14.2 7.3 %fast_weights.1 = (bf16[512,768]{1,0:T(8,128)(2,1)}, bf16[512,1536]{1,0:T(8,128)(2,1)}) custom-call(bf16[512,1536]{1,0:T(8,128)(2,1)S(1)} %copy-done, bf16[512,1536]{1,0:T(8,128)(2,1)S(1)} %copy-done.7, bf16[1,1536,768]{2,1,0:T(8,128)(2,1)S(1)} %copy-done.4, bf16[1,1536,768]{2,1,0:T(8,128)(2,1)S(1)} %copy-done.5, bf16[1,768,1536]{2,1,0:T(8,128)(2,1)S(1)} %copy-done.6), custom_call_target="tpu_custom_call" | custom-call | flops 20000000000 | bytes 13369344 | tf_op jit(solution)/shard_map/fast_weights/pallas_call | solution.py:150
  21.6 1.3 %collective-permute-start.7 = (bf16[512,768]{1,0:T(8,128)(2,1)}, bf16[512,768]{1,0:T(8,128)(2,1)}, u32[]{:S(2)}, u32[]{:S(2)}) collective-permute-start(bf16[512,768]{1,0:T(8,128)(2,1)} %get-tuple-element.32.g0), channel_id=1, source_target_pairs={{8,0},{12,4},{16,8},{20,12},{24,16},{28,20},{9,1},{13,5},{17,9},{2... | collective-permute-start | bytes 2359304 | tf_op jit(solution)/shard_map/ppermute | solution.py:494
  22.9 3.2 %collective-permute-start.6 = (bf16[512,768]{1,0:T(8,128)(2,1)}, bf16[512,768]{1,0:T(8,128)(2,1)}, u32[]{:S(2)}, u32[]{:S(2)}) collective-permute-start(bf16[512,768]{1,0:T(8,128)(2,1)} %refs_2_.3), channel_id=1, source_target_pairs={{0,4},{4,8},{8,12},{12,16},{16,20},{20,24},{24,28},{1,5},{5,9},{9,... | collective-permute-start | bytes 2359304 | tf_op jit(solution)/shard_map/ppermute | solution.py:494
  26.1 2.4 %pick_halos.1 = (bf16[2,64,2560]{2,1,0:T(8,128)(2,1)}, bf16[2,64,2560]{2,1,0:T(8,128)(2,1)}) custom-call(s32[1]{0:T(128)} %bitcast.scal, bf16[128,2560]{1,0:T(8,128)(2,1)} %refs_2_.2, bf16[128,2560]{1,0:T(8,128)(2,1)} %refs_3_.1), custom_call_target="tpu_custom_call" | custom-call | bytes 2621440 | tf_op jit(solution)/shard_map/pick_halos/pallas_call | solution.py:79
  28.4 0.1 collective-permute-start
  28.5 1.5 %collective-permute-start.1 = (bf16[2,64,2560]{2,1,0:T(8,128)(2,1)}, bf16[2,64,2560]{2,1,0:T(8,128)(2,1)}, u32[]{:S(2)}, u32[]{:S(2)}) collective-permute-start(bf16[2,64,2560]{2,1,0:T(8,128)(2,1)} %get-tuple-element.23), channel_id=1, source_target_pairs={{1,2},{2,1},{5,6},{6,5},{9,10},{10,9},{13,14},{14,13},{17,18},{18,... | collective-permute-start | bytes 1966088 | tf_op jit(solution)/shard_map/ppermute | solution.py:500
  30.0 3.8 %all-to-all-start = ((bf16[4,128,1536]{2,1,0:T(8,128)(2,1)}), bf16[4,128,1536]{2,1,0:T(8,128)(2,1)S(1)}, u32[]{:S(2)}, u32[]{:S(2)}) async-start(bf16[4,128,1536]{2,1,0:T(8,128)(2,1)} %bitcast.3), calls=%async_computation | async-start | bytes 3145728 | tf_op jit(solution)/shard_map/all_to_all | solution.py:558
  33.8 0.1 window_bias.1.bias
  33.9 1.9 %collective-permute-start.5 = (bf16[512,1536]{1,0:T(8,128)(2,1)}, bf16[512,1536]{1,0:T(8,128)(2,1)S(1)}, u32[]{:S(2)}, u32[]{:S(2)}) collective-permute-start(bf16[512,1536]{1,0:T(8,128)(2,1)} %collective-permute-done.4.refs_1_), channel_id=1, source_target_pairs={{0,1},{2,3},{1,0},{3,2},{4,5},{6,7},{5,4},{7,6},{8,9},{10,11},{9,8... | collective-permute-start | bytes 4718600 | tf_op jit(solution)/shard_map/ppermute | solution.py:500
  35.7 0.6 pair_weights.1.together
  36.3 0.0 copy-start.1
  36.3 0.0 collective-permute-done.1.refs_5_
  36.3 7.3 %window_attention.1 = (bf16[128,2560]{1,0:T(8,128)(2,1)}, bf16[128,2560]{1,0:T(8,128)(2,1)}, bf16[128,2560]{1,0:T(8,128)(2,1)}, bf16[2,64,2560]{2,1,0:T(8,128)(2,1)}, bf16[2,64,2560]{2,1,0:T(8,128)(2,1)}) custom-call(f32[256,256]{1,0:T(8,128)S(1)} %window_bias.1.bias, bf16[128,2560]{1,0:T(8,128)(2,1)} %refs_0_.1, bf16[128,2560]{1,0:T(8,128)(2,1)} %refs_1_.1, ...), custom_call_target="tpu_custom_call" | custom-call | flops 1677721600 | bytes 7208960 | tf_op jit(solution)/shard_map/window_attention/pallas_call | solution.py:261
  43.7 9.2 %collective-permute-start.2 = (bf16[2,64,2560]{2,1,0:T(8,128)(2,1)}, bf16[2,64,2560]{2,1,0:T(8,128)(2,1)}, u32[]{:S(2)}, u32[]{:S(2)}) collective-permute-start(bf16[2,64,2560]{2,1,0:T(8,128)(2,1)} %get-tuple-element.27), channel_id=1, source_target_pairs={{0,1},{2,3},{1,0},{3,2},{4,5},{6,7},{5,4},{7,6},{8,9},{10,11},{9,8... | collective-permute-start | bytes 1966088 | tf_op jit(solution)/shard_map/ppermute | solution.py:500
  52.8 1.6 %collective-permute-start.3 = (bf16[2,64,2560]{2,1,0:T(8,128)(2,1)}, bf16[2,64,2560]{2,1,0:T(8,128)(2,1)}, u32[]{:S(2)}, u32[]{:S(2)}) collective-permute-start(bf16[2,64,2560]{2,1,0:T(8,128)(2,1)} %get-tuple-element.28), channel_id=1, source_target_pairs={{1,2},{2,1},{5,6},{6,5},{9,10},{10,9},{13,14},{14,13},{17,18},{18,... | collective-permute-start | bytes 1966088 | tf_op jit(solution)/shard_map/ppermute | solution.py:500
  54.5 4.1 %pair_scores.1.st = bf16[3,512,512]{2,1,0:T(8,128)(2,1)} custom-call(s32[1]{0:T(128)} %bitcast.scal, bf16[512,1536]{1,0:T(8,128)(2,1)S(1)} %copy-done.1, bf16[512,1536]{1,0:T(8,128)(2,1)S(1)} %copy-done, bf16[512,1536]{1,0:T(8,128)(2,1)S(1)} %collective-permute-done.5.refs_0_, bf16[512,1536]{1,0:T(8,128)(2,1)} %collective-permute-done.4.refs_1_), custom_call_target="tpu_custom_call" | custom-call | flops 20000000000 | bytes 1572864 | tf_op jit(solution)/shard_map/pair_scores/pallas_call | solution.py:318
  58.6 0.0 collective-permute-done.6.refs_0_
  58.6 1.4 %copy-done.2 = bf16[3,512,512]{2,1,0:T(8,128)(2,1)S(1)} copy-done((bf16[3,512,512]{2,1,0:T(8,128)(2,1)S(1)}, bf16[3,512,512]{2,1,0:T(8,128)(2,1)}, u32[]{:S(2)}) %copy-start.2) | copy-done | bytes 1572888
  60.0 3.0 %pair_rates.1 = (f32[4,1,128]{2,1,0:T(1,128)S(1)}, f32[4,1,128]{2,1,0:T(1,128)S(1)}) custom-call(s32[1]{0:T(128)} %bitcast.scal, f32[3,128]{1,0:T(4,128)S(1)} %pair_weights.1.together, bf16[3,512,512]{2,1,0:T(8,128)(2,1)S(1)} %copy-done.2, bf16[512,768]{1,0:T(8,128)(2,1)S(1)} %copy-done.3, bf16[512,768]{1,0:T(8,128)(2,1)} %collective-permute-done.6.refs_0_, ...), custom_call_target="tpu_custom_call" | custom-call | flops 1207959552 | bytes 5505024 | tf_op jit(solution)/shard_map/pair_rates/pallas_call | solution.py:372
  63.0 1.3 %collective-permute-start.8 = (f32[4,1,128]{2,1,0:T(1,128)S(1)}, f32[4,1,128]{2,1,0:T(1,128)S(1)}, u32[]{:S(2)}, u32[]{:S(2)}) collective-permute-start(f32[4,1,128]{2,1,0:T(1,128)S(1)} %get-tuple-element.34), channel_id=1, source_target_pairs={{4,0},{8,4},{12,8},{16,12},{20,16},{24,20},{28,24},{5,1},{9,5},{13... | collective-permute-start | bytes 6152 | tf_op jit(solution)/shard_map/ppermute | solution.py:494
  64.3 5.0 %collective-permute-done.8.received = f32[4,1,128]{2,1,0:T(1,128)S(1)} collective-permute-done((f32[4,1,128]{2,1,0:T(1,128)S(1)}, f32[4,1,128]{2,1,0:T(1,128)S(1)}, u32[]{:S(2)}, u32[]{:S(2)}) %collective-permute-start.8) | collective-permute-done | bytes 2080 | tf_op jit(solution)/shard_map/ppermute | solution.py:494
  69.3 0.9 %collective-permute-start.9 = (f32[2,1,128]{2,1,0:T(1,128)S(1)}, f32[2,1,128]{2,1,0:T(1,128)S(1)}, u32[]{:S(2)}, u32[]{:S(2)}) collective-permute-start(f32[2,1,128]{2,1,0:T(1,128)S(1)} %get-tuple-element.36), channel_id=1, source_target_pairs={{0,1},{1,0},{2,3},{3,2},{4,5},{5,4},{6,7},{7,6},{8,9},{9,8},{10,11... | collective-permute-start | bytes 3080 | tf_op jit(solution)/shard_map/ppermute | solution.py:505
  70.3 0.8 %collective-permute-done.9.received = f32[2,1,128]{2,1,0:T(1,128)S(1)} collective-permute-done((f32[2,1,128]{2,1,0:T(1,128)S(1)}, f32[2,1,128]{2,1,0:T(1,128)S(1)}, u32[]{:S(2)}, u32[]{:S(2)}) %collective-permute-start.9) | collective-permute-done | bytes 1056 | tf_op jit(solution)/shard_map/ppermute | solution.py:505
  71.1 1.6 %collective-permute-start.10 = (f32[1,1,128]{2,1,0:T(1,128)S(1)}, f32[1,1,128]{2,1,0:T(1,128)S(1)}, u32[]{:S(2)}, u32[]{:S(2)}) collective-permute-start(f32[1,1,128]{2,1,0:T(1,128)S(1)} %get-tuple-element.38), channel_id=1, source_target_pairs={{0,2},{1,3},{2,0},{3,1},{4,6},{5,7},{6,4},{7,5},{8,10},{9,11},{10,... | collective-permute-start | bytes 1544 | tf_op jit(solution)/shard_map/ppermute | solution.py:505
  72.6 0.9 %sum_parts.1 = bf16[128,1536]{1,0:T(8,128)(2,1)} custom-call(bf16[4,128,1536]{2,1,0:T(8,128)(2,1)S(1)} %all-to-all-done.parts), custom_call_target="tpu_custom_call" | custom-call | flops 786432 | bytes 1572864 | tf_op jit(solution)/shard_map/sum_parts/pallas_call | solution.py:480
  73.6 2.7 %add_margins.1 = (bf16[128,2560]{1,0:T(8,128)(2,1)}, bf16[128,2560]{1,0:T(8,128)(2,1)}) custom-call(s32[1]{0:T(128)} %bitcast.scal, bf16[128,2560]{1,0:T(8,128)(2,1)} %get-tuple-element.25.dk, bf16[128,2560]{1,0:T(8,128)(2,1)} %get-tuple-element.26.dv, bf16[2,64,2560]{2,1,0:T(8,128)(2,1)} %collective-permute-done.2.mc, ...), custom_call_target="tpu_custom_call" | custom-call | flops 655360 | bytes 3932160 | tf_op jit(solution)/shard_map/add_margins/pallas_call | solution.py:456
  76.3 0.5 fold_rates.5
  (23 shorter events, 0.1 us)
Async XLA Ops:
  0.6 8.8 %copy-start = (bf16[512,1536]{1,0:T(8,128)(2,1)S(1)}, bf16[512,1536]{1,0:T(8,128)(2,1)}, u32[]{:S(2)}) copy-start(bf16[512,1536]{1,0:T(8,128)(2,1)} %q0.1) | copy-start | bytes 4718596
  0.6 8.8 %copy-start.4 = (bf16[1,1536,768]{2,1,0:T(8,128)(2,1)S(1)}, bf16[1,1536,768]{2,1,0:T(8,128)(2,1)}, u32[]{:S(2)}) copy-start(bf16[1,1536,768]{2,1,0:T(8,128)(2,1)} %gw.1) | copy-start | bytes 7077892
  3.4 30.5 %collective-permute-start.4 = (bf16[512,1536]{1,0:T(8,128)(2,1)}, bf16[512,1536]{1,0:T(8,128)(2,1)}, u32[]{:S(2)}, u32[]{:S(2)}) collective-permute-start(bf16[512,1536]{1,0:T(8,128)(2,1)} %pick_outgoing.1), channel_id=1, source_target_pairs={{9,1},{11,3},{0,4},{13,5},{2,6},{15,7},{4,8},{17,9},{6,10},{19,11}... | collective-permute-start | bytes 4718600 | tf_op jit(solution)/shard_map/ppermute | solution.py:516
  9.5 1.7 %copy-start.5 = (bf16[1,1536,768]{2,1,0:T(8,128)(2,1)S(1)}, bf16[1,1536,768]{2,1,0:T(8,128)(2,1)}, u32[]{:S(2)}) copy-start(bf16[1,1536,768]{2,1,0:T(8,128)(2,1)} %uw.1) | copy-start | bytes 7077892
  11.1 1.7 %copy-start.6 = (bf16[1,768,1536]{2,1,0:T(8,128)(2,1)S(1)}, bf16[1,768,1536]{2,1,0:T(8,128)(2,1)}, u32[]{:S(2)}) copy-start(bf16[1,768,1536]{2,1,0:T(8,128)(2,1)} %dw.1) | copy-start | bytes 7077892
  12.8 1.4 %copy-start.7 = (bf16[512,1536]{1,0:T(8,128)(2,1)S(1)}, bf16[512,1536]{1,0:T(8,128)(2,1)}, u32[]{:S(2)}) copy-start(bf16[512,1536]{1,0:T(8,128)(2,1)} %og.1) | copy-start | bytes 4718596
  21.6 37.0 %collective-permute-start.7 = (bf16[512,768]{1,0:T(8,128)(2,1)}, bf16[512,768]{1,0:T(8,128)(2,1)}, u32[]{:S(2)}, u32[]{:S(2)}) collective-permute-start(bf16[512,768]{1,0:T(8,128)(2,1)} %get-tuple-element.32.g0), channel_id=1, source_target_pairs={{8,0},{12,4},{16,8},{20,12},{24,16},{28,20},{9,1},{13,5},{17,9},{2... | collective-permute-start | bytes 2359304 | tf_op jit(solution)/shard_map/ppermute | solution.py:494
  22.9 35.7 %collective-permute-start.6 = (bf16[512,768]{1,0:T(8,128)(2,1)}, bf16[512,768]{1,0:T(8,128)(2,1)}, u32[]{:S(2)}, u32[]{:S(2)}) collective-permute-start(bf16[512,768]{1,0:T(8,128)(2,1)} %refs_2_.3), channel_id=1, source_target_pairs={{0,4},{4,8},{8,12},{12,16},{16,20},{20,24},{24,28},{1,5},{5,9},{9,... | collective-permute-start | bytes 2359304 | tf_op jit(solution)/shard_map/ppermute | solution.py:494
  28.4 7.9 %collective-permute-start = (bf16[2,64,2560]{2,1,0:T(8,128)(2,1)}, bf16[2,64,2560]{2,1,0:T(8,128)(2,1)}, u32[]{:S(2)}, u32[]{:S(2)}) collective-permute-start(bf16[2,64,2560]{2,1,0:T(8,128)(2,1)} %get-tuple-element.22), channel_id=1, source_target_pairs={{0,1},{2,3},{1,0},{3,2},{4,5},{6,7},{5,4},{7,6},{8,9},{10,11},{9,8... | collective-permute-start | bytes 1966088 | tf_op jit(solution)/shard_map/ppermute | solution.py:500
  28.5 7.8 %collective-permute-start.1 = (bf16[2,64,2560]{2,1,0:T(8,128)(2,1)}, bf16[2,64,2560]{2,1,0:T(8,128)(2,1)}, u32[]{:S(2)}, u32[]{:S(2)}) collective-permute-start(bf16[2,64,2560]{2,1,0:T(8,128)(2,1)} %get-tuple-element.23), channel_id=1, source_target_pairs={{1,2},{2,1},{5,6},{6,5},{9,10},{10,9},{13,14},{14,13},{17,18},{18,... | collective-permute-start | bytes 1966088 | tf_op jit(solution)/shard_map/ppermute | solution.py:500
  30.0 42.6 %all-to-all-start = ((bf16[4,128,1536]{2,1,0:T(8,128)(2,1)}), bf16[4,128,1536]{2,1,0:T(8,128)(2,1)S(1)}, u32[]{:S(2)}, u32[]{:S(2)}) async-start(bf16[4,128,1536]{2,1,0:T(8,128)(2,1)} %bitcast.3), calls=%async_computation | async-start | bytes 3145728 | tf_op jit(solution)/shard_map/all_to_all | solution.py:558
  33.8 1.9 %copy-start.8 = (s32[4]{0:T(128)S(1)}, s32[4]{0:T(128)}, u32[]{:S(2)}) copy-start(s32[4]{0:T(128)} %clips.1) | copy-start | bytes 52
  33.9 20.6 %collective-permute-start.5 = (bf16[512,1536]{1,0:T(8,128)(2,1)}, bf16[512,1536]{1,0:T(8,128)(2,1)S(1)}, u32[]{:S(2)}, u32[]{:S(2)}) collective-permute-start(bf16[512,1536]{1,0:T(8,128)(2,1)} %collective-permute-done.4.refs_1_), channel_id=1, source_target_pairs={{0,1},{2,3},{1,0},{3,2},{4,5},{6,7},{5,4},{7,6},{8,9},{10,11},{9,8... | collective-permute-start | bytes 4718600 | tf_op jit(solution)/shard_map/ppermute | solution.py:500
  36.3 18.2 %copy-start.1 = (bf16[512,1536]{1,0:T(8,128)(2,1)S(1)}, bf16[512,1536]{1,0:T(8,128)(2,1)}, u32[]{:S(2)}) copy-start(bf16[512,1536]{1,0:T(8,128)(2,1)} %k0.1) | copy-start | bytes 4718596
  43.7 29.9 %collective-permute-start.2 = (bf16[2,64,2560]{2,1,0:T(8,128)(2,1)}, bf16[2,64,2560]{2,1,0:T(8,128)(2,1)}, u32[]{:S(2)}, u32[]{:S(2)}) collective-permute-start(bf16[2,64,2560]{2,1,0:T(8,128)(2,1)} %get-tuple-element.27), channel_id=1, source_target_pairs={{0,1},{2,3},{1,0},{3,2},{4,5},{6,7},{5,4},{7,6},{8,9},{10,11},{9,8... | collective-permute-start | bytes 1966088 | tf_op jit(solution)/shard_map/ppermute | solution.py:500
  52.8 5.8 %copy-start.3 = (bf16[512,768]{1,0:T(8,128)(2,1)S(1)}, bf16[512,768]{1,0:T(8,128)(2,1)}, u32[]{:S(2)}) copy-start(bf16[512,768]{1,0:T(8,128)(2,1)} %get-tuple-element.32.g0) | copy-start | bytes 2359300
  52.8 20.8 %collective-permute-start.3 = (bf16[2,64,2560]{2,1,0:T(8,128)(2,1)}, bf16[2,64,2560]{2,1,0:T(8,128)(2,1)}, u32[]{:S(2)}, u32[]{:S(2)}) collective-permute-start(bf16[2,64,2560]{2,1,0:T(8,128)(2,1)} %get-tuple-element.28), channel_id=1, source_target_pairs={{1,2},{2,1},{5,6},{6,5},{9,10},{10,9},{13,14},{14,13},{17,18},{18,... | collective-permute-start | bytes 1966088 | tf_op jit(solution)/shard_map/ppermute | solution.py:500
  58.6 1.4 %copy-start.2 = (bf16[3,512,512]{2,1,0:T(8,128)(2,1)S(1)}, bf16[3,512,512]{2,1,0:T(8,128)(2,1)}, u32[]{:S(2)}) copy-start(bf16[3,512,512]{2,1,0:T(8,128)(2,1)} %pair_scores.1.st) | copy-start | bytes 4718596
  63.0 6.3 %collective-permute-start.8 = (f32[4,1,128]{2,1,0:T(1,128)S(1)}, f32[4,1,128]{2,1,0:T(1,128)S(1)}, u32[]{:S(2)}, u32[]{:S(2)}) collective-permute-start(f32[4,1,128]{2,1,0:T(1,128)S(1)} %get-tuple-element.34), channel_id=1, source_target_pairs={{4,0},{8,4},{12,8},{16,12},{20,16},{24,20},{28,24},{5,1},{9,5},{13... | collective-permute-start | bytes 6152 | tf_op jit(solution)/shard_map/ppermute | solution.py:494
  69.3 1.8 %collective-permute-start.9 = (f32[2,1,128]{2,1,0:T(1,128)S(1)}, f32[2,1,128]{2,1,0:T(1,128)S(1)}, u32[]{:S(2)}, u32[]{:S(2)}) collective-permute-start(f32[2,1,128]{2,1,0:T(1,128)S(1)} %get-tuple-element.36), channel_id=1, source_target_pairs={{0,1},{1,0},{2,3},{3,2},{4,5},{5,4},{6,7},{7,6},{8,9},{9,8},{10,11... | collective-permute-start | bytes 3080 | tf_op jit(solution)/shard_map/ppermute | solution.py:505
  71.1 5.2 %collective-permute-start.10 = (f32[1,1,128]{2,1,0:T(1,128)S(1)}, f32[1,1,128]{2,1,0:T(1,128)S(1)}, u32[]{:S(2)}, u32[]{:S(2)}) collective-permute-start(f32[1,1,128]{2,1,0:T(1,128)S(1)} %get-tuple-element.38), channel_id=1, source_target_pairs={{0,2},{1,3},{2,0},{3,1},{4,6},{5,7},{6,4},{7,5},{8,10},{9,11},{10,... | collective-permute-start | bytes 1544 | tf_op jit(solution)/shard_map/ppermute | solution.py:505

commit v2 on v1

--- a/solution.py
+++ b/solution.py
@@ -119,7 +119,10 @@
     )(scal, clips)
 
 
-def fast_kernel(step, q, og, gw, uw, dw, gate_out, part_out, gate_grad, up_grad, part, sems):
+def fast_kernel(step, ends, scal, q, og, gw, uw, dw, gate_out, keep, send, *refs):
+    gate_grad, up_grad, part, gate_sem, sems = refs
+    rows = keep.shape[1]
+    odd = scal[0] % 2
     for j in range(gw.shape[2] // step):
         cols = slice(j * step, (j + 1) * step)
         gate = jnp.dot(q[...], gw[0, :, cols], preferred_element_type=F32)
@@ -128,40 +131,51 @@
         sig = jax.nn.sigmoid(gate)
         gate_grad[:, cols] = (hidden * up * sig * (1.0 + gate * (1.0 - sig))).astype(BF16)
         up_grad[:, cols] = (hidden * (gate * sig)).astype(BF16)
-    copies = [pltpu.make_async_copy(gate_grad, gate_out, sems.at[0])]
+    copies = [pltpu.make_async_copy(gate_grad, gate_out, gate_sem)]
     copies[0].start()
-    for j in range(q.shape[1] // step):
-        rows = slice(j * step, (j + 1) * step)
-        part[:, rows] = (
-            dot_last(gate_grad[...], gw[0, rows, :]) + dot_last(up_grad[...], uw[0, rows, :])
+    begin = 0
+    for at in range(0, q.shape[1], step):
+        cols = slice(at, at + step)
+        part[:, cols] = (
+            dot_last(gate_grad[...], gw[0, cols, :]) + dot_last(up_grad[...], uw[0, cols, :])
         ).astype(BF16)
-        copy = pltpu.make_async_copy(part.at[:, rows], part_out.at[:, rows], sems.at[1 + j])
-        copy.start()
-        copies.append(copy)
+        if at + step in ends:
+            cols = slice(begin, at + step)
+            for n in range(2 * keep.shape[0]):
+                source, sem = part.at[n * rows : (n + 1) * rows, cols], sems.at[ends.index(at + step), n]
+                stay = pltpu.make_async_copy(source, keep.at[n // 2, :, cols], sem)
+                leave = pltpu.make_async_copy(source, send.at[n // 2, :, cols], sem)
+                pl.when(odd == n % 2)(stay.start)
+                pl.when(odd != n % 2)(leave.start)
+                copies.append(stay)
+            begin = at + step
     for copy in copies:
         copy.wait()
 
 
-def fast(query, outgrad, gate_w, up_w, down_w):
+def fast(scal, query, outgrad, gate_w, up_w, down_w, tiles):
     rows, width = query.shape
     hidden = gate_w.shape[2]
     step = next(s for s in (256, 128) if hidden % s == 0 and width % s == 0)
+    ends = sorted({width // step * 2 // 3 * step, width})
     vmem = pl.BlockSpec(memory_space=pltpu.VMEM)
-    return pl.pallas_call(
-        functools.partial(fast_kernel, step),
-        in_specs=[vmem] * 5,
-        out_specs=[pl.BlockSpec(memory_space=pltpu.HBM)] * 2,
-        out_shape=[pltpu.HBM((rows, n), BF16) for n in (hidden, width)],
+    half = pltpu.HBM((tiles // 2, rows // tiles, width), BF16)
+    return pl.pallas_call(
+        functools.partial(fast_kernel, step, ends),
+        in_specs=[pl.BlockSpec(memory_space=pltpu.SMEM)] + [vmem] * 5,
+        out_specs=[pl.BlockSpec(memory_space=pltpu.HBM)] * 3,
+        out_shape=[pltpu.HBM((rows, hidden), BF16), half, half],
         scratch_shapes=[
             pltpu.VMEM((rows, hidden), BF16),
             pltpu.VMEM((rows, hidden), BF16),
             pltpu.VMEM((rows, width), BF16),
-            pltpu.SemaphoreType.DMA((1 + width // step,)),
+            pltpu.SemaphoreType.DMA,
+            pltpu.SemaphoreType.DMA((len(ends), tiles)),
         ],
         cost_estimate=cost(20 * 10**9, 6 * width * hidden + 8 * rows * width),
         compiler_params=room(16, (6 * rows * width + 6 * width * hidden + 4 * rows * hidden) * 5 // 4),
         name="fast_weights",
-    )(query, outgrad, gate_w, up_w, down_w)
+    )(scal, query, outgrad, gate_w, up_w, down_w)
 
 
 def bias_kernel(reach, last, scal, out):
@@ -182,6 +196,23 @@
     out[:, rows:] = bias
 
 
+def share_kernel(share, together, out):
+    out[...] = together[...] * share
+
+
+def pair_shares(together, share):
+    vmem = pl.BlockSpec(memory_space=pltpu.VMEM)
+    return pl.pallas_call(
+        functools.partial(share_kernel, share),
+        in_specs=[vmem],
+        out_specs=vmem,
+        out_shape=jax.ShapeDtypeStruct(together.shape, F32),
+        cost_estimate=cost(20 * 10**9, 4096),
+        compiler_params=pltpu.CompilerParams(vmem_limit_bytes=1 << 20),
+        name="pair_shares",
+    )(together)
+
+
 def window_bias(scal, rows, reach, last):
     return pl.pallas_call(
         functools.partial(bias_kernel, reach, last),
@@ -194,18 +225,23 @@
     )(scal)
 
 
-def attention_kernel(every, bias, *refs):
+def attention_kernel(load_ends, store_ends, bias, *refs):
     sources, outs, local, held = refs[:6], refs[6:11], refs[11:17], refs[17:22]
     load_sems, sems = refs[22:]
     q, g, k, v, hc, hx = local
     dk_own, dv_own, dq, mc, mx = held
-    loads, copies = [], []
-    for at in range(0, q.shape[1], every):
-        part = (Ellipsis, slice(at, at + every))
-        for i, (source, ref) in enumerate(zip(sources, local)):
-            sem = load_sems.at[at // every, i]
-            loads.append(pltpu.make_async_copy(source.at[part], ref.at[part], sem))
-            loads[-1].start()
+    loads, copies = {}, []
+    begin = 0
+    for n, end in enumerate(load_ends):
+        part = (Ellipsis, slice(begin, end))
+        loads[begin] = [
+            pltpu.make_async_copy(source.at[part], ref.at[part], load_sems.at[n, i])
+            for i, (source, ref) in enumerate(zip(sources, local))
+        ]
+        for copy in loads[begin]:
+            copy.start()
+        begin = end
+    begin, stores = 0, 0
     rows, reach = q.shape[0], hc.shape[1]
     wide = 2 * HEAD
     scaling = 1.0 / math.sqrt(HEAD)
@@ -218,9 +254,8 @@
         )
 
     for start in range(0, q.shape[1], wide):
-        if start % every == 0:
-            for copy in loads[start // every * 6 : start // every * 6 + 6]:
-                copy.wait()
+        for copy in loads.get(start, ()):
+            copy.wait()
         col = slice(start, start + wide)
         kk = jnp.concatenate([k[:, col], hc[0, :, col], hx[0, :, col]], axis=0)
         vv = jnp.concatenate([v[:, col], hc[1, :, col], hx[1, :, col]], axis=0)
@@ -241,12 +276,12 @@
             own[:, col] = grad[:rows].astype(BF16)
             mc[i, :, col] = grad[rows : rows + reach].astype(BF16)
             mx[i, :, col] = grad[rows + reach :].astype(BF16)
-        if (start + wide) % every == 0:
-            done = (Ellipsis, slice(start + wide - every, start + wide))
+        if start + wide in store_ends:
+            done = (Ellipsis, slice(begin, start + wide))
             for i, (ref, out) in enumerate(zip(held, outs)):
-                sem = sems.at[start // every, i]
-                copies.append(pltpu.make_async_copy(ref.at[done], out.at[done], sem))
+                copies.append(pltpu.make_async_copy(ref.at[done], out.at[done], sems.at[stores, i]))
                 copies[-1].start()
+            begin, stores = start + wide, stores + 1
     for copy in copies:
         copy.wait()
 
@@ -255,22 +290,26 @@
     rows, width = query.shape
     reach = halo_c.shape[1]
     keys = rows + 2 * reach
-    every = next(n for n in (10, 4, 2) if width % (n * HEAD) == 0) * HEAD
+    twos = width // (2 * HEAD)
+    load_ends = sorted({2 * HEAD * n for n in (-(-twos // 5), -(-twos // 2), twos)})
+    store_ends = sorted({2 * HEAD * n for n in (-(-twos // 2), -(-twos * 4 // 5), twos)})
     vmem = pl.BlockSpec(memory_space=pltpu.VMEM)
     flat, half = (rows, width), (2, reach, width)
     return pl.pallas_call(
-        functools.partial(attention_kernel, every),
-        in_specs=[vmem] + [pl.BlockSpec(memory_space=pltpu.HBM)] * 6,
+        functools.partial(attention_kernel, load_ends, store_ends),
+        in_specs=[vmem]
+        + [pl.BlockSpec(memory_space=pltpu.HBM)] * 4
+        + [pl.BlockSpec(memory_space=pl.ANY)] * 2,
         out_specs=[pl.BlockSpec(memory_space=pltpu.HBM)] * 5,
         out_shape=[pltpu.HBM(x, BF16) for x in (flat, flat, flat, half, half)],
         scratch_shapes=[pltpu.VMEM(x, BF16) for x in [flat] * 4 + [half] * 2 + [flat] * 3 + [half] * 2]
-        + [pltpu.SemaphoreType.DMA((width // every, 6)), pltpu.SemaphoreType.DMA((width // every, 5))],
+        + [pltpu.SemaphoreType.DMA((len(load_ends), 6)), pltpu.SemaphoreType.DMA((len(store_ends), 5))],
         cost_estimate=cost(
             20 * rows * keys * width, 22 * width * rows, width // HEAD * rows * keys
         ),
         compiler_params=pltpu.CompilerParams(vmem_limit_bytes=14 << 20),
         name="window_attention",
-    )(bias, *far(query, out_grad, key, value, halo_c, halo_x))
+    )(bias, *far(query, out_grad, key, value), halo_c, halo_x)
 
 
 def scores_kernel(n_two, scal, k0, q0, *refs):
@@ -315,9 +354,10 @@
     n_two = len(received)
     vmem = pl.BlockSpec(memory_space=pltpu.VMEM)
     hbm = pl.BlockSpec(memory_space=pltpu.HBM)
+    anywhere = pl.BlockSpec(memory_space=pl.ANY)
     return pl.pallas_call(
         functools.partial(scores_kernel, n_two),
-        in_specs=[pl.BlockSpec(memory_space=pltpu.SMEM)] + [vmem] * (2 + n_two) + [hbm] * n_two,
+        in_specs=[pl.BlockSpec(memory_space=pltpu.SMEM)] + [vmem] * (2 + n_two) + [anywhere] * n_two,
         out_specs=hbm,
         out_shape=pltpu.HBM((pairs, rows, rows), BF16),
         scratch_shapes=[pltpu.VMEM((rows, width), BF16)] * n_two
@@ -329,10 +369,10 @@
         cost_estimate=cost(20 * 10**9, 2 * pairs * rows * rows),
         compiler_params=room(20, 14 * pairs * rows * rows // 3 + 4 * (1 + n_two) * rows * width),
         name="pair_scores",
-    )(scal, k0, q0, *paired, *far(*received))
-
-
-def rates_kernel(share, n_far, scal, together, st, g0, *refs):
+    )(scal, k0, q0, *paired, *received)
+
+
+def rates_kernel(n_far, scal, shares, st, g0, *refs):
     sources, own_out, before_out = refs[:n_far], refs[n_far], refs[n_far + 1]
     held, sems = refs[n_far + 2 : -1], refs[-1]
     f1, moved, f0 = held[0], held[1:-1], held[-1]
@@ -347,7 +387,7 @@
     def pair(n, g, f):
         products = dot_last(g[...], f[...])
         summed = jnp.sum(st[n].astype(F32) * products, axis=0, keepdims=True)
-        return summed * (together[n : n + 1, 0:1] * share)
+        return summed * shares[n : n + 1, 0:1]
 
     loads[0].wait()
     before = pair(0, g0, f1)
@@ -364,16 +404,17 @@
         before_out[n] = before[:, part]
 
 
-def rates(scal, together, st, f0, f1, g0, moved, tiles):
+def rates(scal, shares, st, f0, f1, g0, moved, tiles):
     rows, width = f0.shape
     pairs = st.shape[0]
     vmem = pl.BlockSpec(memory_space=pltpu.VMEM)
     n_far = 2 + len(moved)
     return pl.pallas_call(
-        functools.partial(rates_kernel, 1.0 / rows, n_far),
+        functools.partial(rates_kernel, n_far),
         in_specs=[pl.BlockSpec(memory_space=pltpu.SMEM)]
         + [vmem] * 3
-        + [pl.BlockSpec(memory_space=pltpu.HBM)] * n_far,
+        + [pl.BlockSpec(memory_space=pl.ANY)] * (n_far - 1)
+        + [pl.BlockSpec(memory_space=pltpu.HBM)],
         out_specs=[vmem] * 2,
         out_shape=[jax.ShapeDtypeStruct((tiles, 1, rows // tiles), F32)] * 2,
         scratch_shapes=[pltpu.VMEM((rows, width), BF16)] * n_far
@@ -383,17 +424,17 @@
         ),
         compiler_params=room(14, (2 * pairs + 16) * rows * rows + 4 * (1 + n_far) * rows * width),
         name="pair_rates",
-    )(scal, *near(together, st, g0), *far(f1, *moved, f0))
+    )(scal, *near(shares, st, g0), f1, *moved, *far(f0))
 
 
 def fold_kernel(bit, scal, kept, received, *outs):
     if len(outs) == 1:
-        outs[0][...] = kept[...] + received[...]
+        outs[0][...] = (kept[...].astype(F32) + received[...].astype(F32)).astype(kept.dtype)
         return
     keep, send = outs
     side = lax.rem(lax.div(scal[0], 1 << bit), 2)
     for n in range(kept.shape[0]):
-        total = kept[n] + received[n]
+        total = (kept[n].astype(F32) + received[n].astype(F32)).astype(kept.dtype)
 
         def put(ref):
             ref[n // 2] = total
@@ -413,8 +454,7 @@
         out_specs=[vmem] if last else [vmem] * 2,
         out_shape=[out] if last else [out] * 2,
         cost_estimate=cost(kept.size, 12 * kept.size),
-        compiler_params=pltpu.CompilerParams(vmem_limit_bytes=1 << 20),
-        name="fold_rates",
+        compiler_params=room(1, 3 * kept.dtype.itemsize * kept.size + (1 << 20)),
     )(scal, kept, received)
 
 
@@ -468,26 +508,6 @@
     )(scal, *far(dk, dv), mc, mx)
 
 
-def sum_kernel(parts, out):
-    total = parts[0].astype(F32)
-    for n in range(1, parts.shape[0]):
-        total += parts[n].astype(F32)
-    out[...] = total.astype(BF16)
-
-
-def sum_parts(parts):
-    vmem = pl.BlockSpec(memory_space=pltpu.VMEM)
-    return pl.pallas_call(
-        sum_kernel,
-        in_specs=[vmem],
-        out_specs=vmem,
-        out_shape=jax.ShapeDtypeStruct(parts.shape[1:], BF16),
-        cost_estimate=cost(parts.size, 2 * parts.size),
-        compiler_params=pltpu.CompilerParams(vmem_limit_bytes=8 << 20),
-        name="sum_parts",
-    )(parts)
-
-
 def shifted(array, axis, by):
     devices = lax.axis_size(axis)
     pairs = [(i + by, i) for i in range(devices) if 0 <= i + by < devices]
@@ -550,12 +570,17 @@
     halo_c = swapped(halo_c, "space", 0)
     halo_x = swapped(halo_x, "space", 1)
 
-    gate_grad_b, input_part = fast(fast_query, fast_outgrad, gate_weights, up_weights, down_weights)
+    gate_grad_b, part, sent = fast(
+        scal, fast_query, fast_outgrad, gate_weights, up_weights, down_weights, tiles
+    )
+    for bit in range(tiles.bit_length() - 1):
+        arrived = across(sent, "space", bit)
+        part, *rest = fold(scal, part, arrived, bit + 1)
+        sent = rest[0] if rest else None
+    fast_grad = part[0]
     moved = []
     for v in shifts:
         moved.append(shifted(gate_grad_b, "tm", v))
-
-    parts = lax.all_to_all(input_part.reshape(tiles, tile_rows, -1), "space", 0, 0)
 
     bias = window_bias(scal, tile_rows, tile_rows // 2, rows)
     dk, dv, query_grad, margin_c, margin_x = attention(
@@ -569,8 +594,10 @@
         paired.append(swapped(array, "space", 0))
     pairs = 1 + 2 * len(shifts)
     st = scores(scal, fast_key, fast_query, received, paired, pairs)
-    fast_grad = sum_parts(parts)
-    own, before = rates(scal, together, st, gate_factor, factor_before, gate_grad_b, moved, tiles)
+    shares = pair_shares(together, 1.0 / rows)
+    own, before = rates(
+        scal, shares, st, gate_factor, factor_before, gate_grad_b, moved, tiles
+    )
     arrived = shifted(before, "tm", 1)
     key_grad, value_grad = add_margins(scal, dk, dv, margin_c, margin_x)
     kept = own

time: 77.4 us -> 67.1 us (0.87)
  starting transfers between devices: 32.4 us -> 23.2 us
  Pallas kernels: 31.6 us -> 27.8 us
  waiting for transfers between devices: 5.85 us -> 8.57 us
    ppermute x5, starting transfers between devices: 14.3 us -> 8.6 us  [swapped(): return lax.ppermute(array, axis, pairs + [(j, i) for i, j in pairs])]
    all_to_all x1 -> x0, starting transfers between devices: 3.79 us -> none  [per_device(): lax.all_to_all(input_part.reshape(tiles, tile_rows, -1), 'space', 0, 0)]
    ppermute x2 -> x4, waiting for transfers between devices: 0.82 us -> 3.51 us  [across(): return lax.ppermute(array, axis, pairs)]
    pallas_call x4, Pallas kernels: 18.6 us -> 16.3 us  [the longest x1 7.45 us: fast(): pl.pallas_call(functools.partial(fast_kernel, step, ends), in_specs=[pl.B...]
    pallas_call x3 -> x5, Pallas kernels: 0.53 us -> 1.75 us  [fold(): pl.pallas_call(functools.partial(fold_kernel, bit), in_specs=[pl.BlockSpe...]
    pallas_call x1, Pallas kernels: 2.75 us -> 1.57 us  [pick(): pl.pallas_call(pick_kernel, in_specs=[pl.BlockSpec(memory_space=pltpu.SME...]
    pallas_call x1, Pallas kernels: 2.35 us -> 1.31 us  [pick_halos(): pl.pallas_call(halos_kernel, in_specs=[pl.BlockSpec(memory_space=pltpu.SM...]
    ppermute x1, starting transfers between devices: 6.06 us -> 5.13 us  [moved_apart(): return lax.ppermute(array, ('tm', 'space'), pairs)]
  transfers between devices with their start and end apart: 12 -> 13, of which waited for: 2 -> 4; matrix products, arithmetic and copies ran while one was open for 0% -> 0% of each run, Pallas kernels for 37% -> 38%
where the time goes in v2:
time: 67.1 us; the launch traced here: 66.7 us
  Pallas kernels  27.8 us (41%)
  starting transfers between devices  23.2 us (35%)
  waiting for transfers between devices  8.57 us (13%)
  local copies, waits for them, and re-layouts  6.17 us (9%)
  between operations  0.94 us (1%)
    ppermute x5, starting transfers between devices, swapped(): return lax.ppermute(array, axis, pairs + [(j, i) for i, j in pairs])  8.6 us
    pallas_call x1, Pallas kernels, fast(): pl.pallas_call(functools.partial(fast_kernel, step, ends), in_specs=[pl.B...  7.45 us
    pallas_call x1, Pallas kernels, attention(): pl.pallas_call(functools.partial(attention_kernel, load_ends, store_ends)...  6.85 us
    unnamed x22, local copies, waits for them, and re-layouts  6.17 us
    ppermute x3, starting transfers between devices, shifted(): return lax.ppermute(array, axis, pairs)  6.09 us
    ppermute x1, starting transfers between devices, moved_apart(): return lax.ppermute(array, ('tm', 'space'), pairs)  5.13 us
    ppermute x3, waiting for transfers between devices, shifted(): return lax.ppermute(array, axis, pairs)  4.18 us
    pallas_call x1, Pallas kernels, scores(): pl.pallas_call(functools.partial(scores_kernel, n_two), in_specs=[pl.Bloc...  3.97 us
  transfers between devices with their start and end apart: 13, of which 4 were waited for; matrix products, arithmetic and copies ran while one was open for 0% of the time, Pallas kernels for 38%

profile of v2, /device:TPU:0, one launch (start us, length us, event | category | flops | bytes accessed | tf_op | source)
XLA Modules:
  0.0 66.7 jit_solution(2550270179596009453)
XLA Ops:
  0.7 1.6 %pick_outgoing.1 = bf16[512,1536]{1,0:T(8,128)(2,1)S(1)} custom-call(s32[1]{0:T(128)} %bitcast.scal, bf16[512,1536]{1,0:T(8,128)(2,1)} %k0.1, bf16[512,1536]{1,0:T(8,128)(2,1)} %q0.1), custom_call_target="tpu_custom_call" | custom-call | bytes 3145728 | tf_op jit(solution)/shard_map/pick_outgoing/pallas_call | solution.py:49
  2.2 5.1 %collective-permute-start.6 = (bf16[512,1536]{1,0:T(8,128)(2,1)S(1)}, bf16[512,1536]{1,0:T(8,128)(2,1)S(1)}, u32[]{:S(2)}, u32[]{:S(2)}) collective-permute-start(bf16[512,1536]{1,0:T(8,128)(2,1)S(1)} %pick_outgoing.1), channel_id=1, source_target_pairs={{9,1},{11,3},{0,4},{13,5},{2,6},{15,7},{4,8},{17,9},{6,10},{19,11}... | collective-permute-start | bytes 4718600 | tf_op jit(solution)/shard_map/ppermute | solution.py:536
  7.4 1.7 %copy-done.6 = bf16[1,1536,768]{2,1,0:T(8,128)(2,1)S(1)} copy-done((bf16[1,1536,768]{2,1,0:T(8,128)(2,1)S(1)}, bf16[1,1536,768]{2,1,0:T(8,128)(2,1)}, u32[]{:S(2)}) %copy-start.6) | copy-done | bytes 2359320
  9.1 1.7 %copy-done.7 = bf16[1,768,1536]{2,1,0:T(8,128)(2,1)S(1)} copy-done((bf16[1,768,1536]{2,1,0:T(8,128)(2,1)S(1)}, bf16[1,768,1536]{2,1,0:T(8,128)(2,1)}, u32[]{:S(2)}) %copy-start.7) | copy-done | bytes 2359320
  10.7 1.4 %copy-done.8 = bf16[512,1536]{1,0:T(8,128)(2,1)S(1)} copy-done((bf16[512,1536]{1,0:T(8,128)(2,1)S(1)}, bf16[512,1536]{1,0:T(8,128)(2,1)}, u32[]{:S(2)}) %copy-start.8) | copy-done | bytes 1572888
  12.1 7.5 %fast_weights.1 = (bf16[512,768]{1,0:T(8,128)(2,1)}, bf16[2,128,1536]{2,1,0:T(8,128)(2,1)}, bf16[2,128,1536]{2,1,0:T(8,128)(2,1)}) custom-call(s32[1]{0:T(128)} %bitcast.scal, bf16[512,1536]{1,0:T(8,128)(2,1)S(1)} %copy-done, bf16[512,1536]{1,0:T(8,128)(2,1)S(1)} %copy-done.8, bf16[1,1536,768]{2,1,0:T(8,128)(2,1)S(1)} %copy-done.5, ...), custom_call_target="tpu_custom_call" | custom-call | flops 20000000000 | bytes 13369344 | tf_op jit(solution)/shard_map/fast_weights/pallas_call | solution.py:163
  19.6 1.3 %collective-permute-start.9 = (bf16[512,768]{1,0:T(8,128)(2,1)}, bf16[512,768]{1,0:T(8,128)(2,1)S(1)}, u32[]{:S(2)}, u32[]{:S(2)}) collective-permute-start(bf16[512,768]{1,0:T(8,128)(2,1)} %get-tuple-element.38.g0), channel_id=1, source_target_pairs={{8,0},{12,4},{16,8},{20,12},{24,16},{28,20},{9,1},{13,5},{17,9},{2... | collective-permute-start | bytes 2359304 | tf_op jit(solution)/shard_map/ppermute | solution.py:514
  20.9 0.1 collective-permute-start.4
  21.0 1.3 %pick_halos.1 = (bf16[2,64,2560]{2,1,0:T(8,128)(2,1)S(1)}, bf16[2,64,2560]{2,1,0:T(8,128)(2,1)S(1)}) custom-call(s32[1]{0:T(128)} %bitcast.scal, bf16[128,2560]{1,0:T(8,128)(2,1)} %refs_2_.2, bf16[128,2560]{1,0:T(8,128)(2,1)} %refs_3_.1), custom_call_target="tpu_custom_call" | custom-call | bytes 2621440 | tf_op jit(solution)/shard_map/pick_halos/pallas_call | solution.py:79
  22.3 0.6 collective-permute-start
  22.9 0.8 %collective-permute-start.1 = (bf16[2,64,2560]{2,1,0:T(8,128)(2,1)S(1)}, bf16[2,64,2560]{2,1,0:T(8,128)(2,1)S(1)}, u32[]{:S(2)}, u32[]{:S(2)}) collective-permute-start(bf16[2,64,2560]{2,1,0:T(8,128)(2,1)S(1)} %get-tuple-element.26), channel_id=1, source_target_pairs={{1,2},{2,1},{5,6},{6,5},{9,10},{10,9},{13,14},{14,13},{17,18},{18,... | collective-permute-start | bytes 1966088 | tf_op jit(solution)/shard_map/ppermute | solution.py:520
  23.8 0.6 pair_weights.1.together
  24.3 0.9 %collective-permute-done.6.refs_1_ = bf16[512,1536]{1,0:T(8,128)(2,1)S(1)} collective-permute-done((bf16[512,1536]{1,0:T(8,128)(2,1)S(1)}, bf16[512,1536]{1,0:T(8,128)(2,1)S(1)}, u32[]{:S(2)}, u32[]{:S(2)}) %collective-permute-start.6) | collective-permute-done | bytes 1572896 | tf_op jit(solution)/shard_map/ppermute | solution.py:536
  25.2 2.0 %collective-permute-start.7 = (bf16[512,1536]{1,0:T(8,128)(2,1)S(1)}, bf16[512,1536]{1,0:T(8,128)(2,1)S(1)}, u32[]{:S(2)}, u32[]{:S(2)}) collective-permute-start(bf16[512,1536]{1,0:T(8,128)(2,1)S(1)} %collective-permute-done.6.refs_1_), channel_id=1, source_target_pairs={{0,1},{2,3},{1,0},{3,2},{4,5},{6,7},{5,4},{7,6},{8,9},{10,11},{9,8... | collective-permute-start | bytes 4718600 | tf_op jit(solution)/shard_map/ppermute | solution.py:520
  27.2 3.5 %collective-permute-start.8 = (bf16[512,768]{1,0:T(8,128)(2,1)S(1)}, bf16[512,768]{1,0:T(8,128)(2,1)S(1)}, u32[]{:S(2)}, u32[]{:S(2)}) collective-permute-start(bf16[512,768]{1,0:T(8,128)(2,1)S(1)} %copy-done.10), channel_id=1, source_target_pairs={{0,4},{4,8},{8,12},{12,16},{16,20},{20,24},{24,28},{1,5},{5,9},{9,... | collective-permute-start | bytes 2359304 | tf_op jit(solution)/shard_map/ppermute | solution.py:514
  30.8 6.8 %window_attention.1 = (bf16[128,2560]{1,0:T(8,128)(2,1)}, bf16[128,2560]{1,0:T(8,128)(2,1)}, bf16[128,2560]{1,0:T(8,128)(2,1)}, bf16[2,64,2560]{2,1,0:T(8,128)(2,1)}, bf16[2,64,2560]{2,1,0:T(8,128)(2,1)}) custom-call(f32[256,256]{1,0:T(8,128)S(1)} %window_bias.1.bias, bf16[128,2560]{1,0:T(8,128)(2,1)} %refs_0_.1, bf16[128,2560]{1,0:T(8,128)(2,1)} %refs_1_.1, ...), custom_call_target="tpu_custom_call" | custom-call | flops 1677721600 | bytes 7208960 | tf_op jit(solution)/shard_map/window_attention/pallas_call | solution.py:298
  37.6 4.5 %collective-permute-start.2 = (bf16[2,64,2560]{2,1,0:T(8,128)(2,1)}, bf16[2,64,2560]{2,1,0:T(8,128)(2,1)S(1)}, u32[]{:S(2)}, u32[]{:S(2)}) collective-permute-start(bf16[2,64,2560]{2,1,0:T(8,128)(2,1)} %get-tuple-element.30), channel_id=1, source_target_pairs={{0,1},{2,3},{1,0},{3,2},{4,5},{6,7},{5,4},{7,6},{8,9},{10,11},{9,8... | collective-permute-start | bytes 1966088 | tf_op jit(solution)/shard_map/ppermute | solution.py:520
  42.1 0.7 %collective-permute-start.3 = (bf16[2,64,2560]{2,1,0:T(8,128)(2,1)}, bf16[2,64,2560]{2,1,0:T(8,128)(2,1)S(1)}, u32[]{:S(2)}, u32[]{:S(2)}) collective-permute-start(bf16[2,64,2560]{2,1,0:T(8,128)(2,1)} %get-tuple-element.31), channel_id=1, source_target_pairs={{1,2},{2,1},{5,6},{6,5},{9,10},{10,9},{13,14},{14,13},{17,18},{18,... | collective-permute-start | bytes 1966088 | tf_op jit(solution)/shard_map/ppermute | solution.py:520
  42.8 0.4 shard_map.155
  43.3 3.1 %collective-permute-start.5 = (bf16[1,128,1536]{2,1,0:T(8,128)(2,1)S(1)}, bf16[1,128,1536]{2,1,0:T(8,128)(2,1)S(1)}, u32[]{:S(2)}, u32[]{:S(2)}) collective-permute-start(bf16[1,128,1536]{2,1,0:T(8,128)(2,1)S(1)} %get-tuple-element.37), channel_id=1, source_target_pairs={{0,2},{1,3},{2,0},{3,1},{4,6},{5,7},{6,4},{7,5},{8,10},{9,11},{10,... | collective-permute-start | bytes 1179656 | tf_op jit(solution)/shard_map/ppermute | solution.py:525
  46.3 4.0 %pair_scores.1.st = bf16[3,512,512]{2,1,0:T(8,128)(2,1)} custom-call(s32[1]{0:T(128)} %bitcast.scal, bf16[512,1536]{1,0:T(8,128)(2,1)S(1)} %copy-done.1, bf16[512,1536]{1,0:T(8,128)(2,1)S(1)} %copy-done, bf16[512,1536]{1,0:T(8,128)(2,1)S(1)} %collective-permute-done.7.refs_0_, bf16[512,1536]{1,0:T(8,128)(2,1)S(1)} %collective-permute-done.6.refs_1_), custom_call_target="tpu_custom_call" | custom-call | flops 20000000000 | bytes 1572864 | tf_op jit(solution)/shard_map/pair_scores/pallas_call | solution.py:358
  50.3 1.4 %copy-done.2 = bf16[3,512,512]{2,1,0:T(8,128)(2,1)S(1)} copy-done((bf16[3,512,512]{2,1,0:T(8,128)(2,1)S(1)}, bf16[3,512,512]{2,1,0:T(8,128)(2,1)}, u32[]{:S(2)}) %copy-start.2) | copy-done | bytes 1572888
  51.7 2.0 %pair_rates.1 = (f32[4,1,128]{2,1,0:T(1,128)S(1)}, f32[4,1,128]{2,1,0:T(1,128)S(1)}) custom-call(s32[1]{0:T(128)} %bitcast.scal, f32[3,128]{1,0:T(4,128)S(1)} %pair_shares.1.shares, bf16[3,512,512]{2,1,0:T(8,128)(2,1)S(1)} %copy-done.2, bf16[512,768]{1,0:T(8,128)(2,1)S(1)} %copy-done.3, bf16[512,768]{1,0:T(8,128)(2,1)S(1)} %collective-permute-done.8.refs_0_, ...), custom_call_target="tpu_custom_call" | custom-call | flops 1207959552 | bytes 5505024 | tf_op jit(solution)/shard_map/pair_rates/pallas_call | solution.py:412
  53.7 1.3 %collective-permute-start.10 = (f32[4,1,128]{2,1,0:T(1,128)S(1)}, f32[4,1,128]{2,1,0:T(1,128)S(1)}, u32[]{:S(2)}, u32[]{:S(2)}) collective-permute-start(f32[4,1,128]{2,1,0:T(1,128)S(1)} %get-tuple-element.40), channel_id=1, source_target_pairs={{4,0},{8,4},{12,8},{16,12},{20,16},{24,20},{28,24},{5,1},{9,5},{13... | collective-permute-start | bytes 6152 | tf_op jit(solution)/shard_map/ppermute | solution.py:514
  55.0 4.2 %collective-permute-done.10.received = f32[4,1,128]{2,1,0:T(1,128)S(1)} collective-permute-done((f32[4,1,128]{2,1,0:T(1,128)S(1)}, f32[4,1,128]{2,1,0:T(1,128)S(1)}, u32[]{:S(2)}, u32[]{:S(2)}) %collective-permute-start.10) | collective-permute-done | bytes 2080 | tf_op jit(solution)/shard_map/ppermute | solution.py:514
  59.2 0.1 collective-permute-start.11
  59.3 1.1 %collective-permute-done.11.received = f32[2,1,128]{2,1,0:T(1,128)S(1)} collective-permute-done((f32[2,1,128]{2,1,0:T(1,128)S(1)}, f32[2,1,128]{2,1,0:T(1,128)S(1)}, u32[]{:S(2)}, u32[]{:S(2)}) %collective-permute-start.11) | collective-permute-done | bytes 1056 | tf_op jit(solution)/shard_map/ppermute | solution.py:525
  60.5 0.2 collective-permute-start.12
  60.6 2.4 %collective-permute-done.5.received = bf16[1,128,1536]{2,1,0:T(8,128)(2,1)S(1)} collective-permute-done((bf16[1,128,1536]{2,1,0:T(8,128)(2,1)S(1)}, bf16[1,128,1536]{2,1,0:T(8,128)(2,1)S(1)}, u32[]{:S(2)}, u32[]{:S(2)}) %collective-permute-start.5) | collective-permute-done | bytes 393248 | tf_op jit(solution)/shard_map/ppermute | solution.py:525
  63.0 0.8 %shard_map.156 = bf16[1,128,1536]{2,1,0:T(8,128)(2,1)} custom-call(s32[1]{0:T(128)} %bitcast.scal, bf16[1,128,1536]{2,1,0:T(8,128)(2,1)S(1)} %get-tuple-element.36.kept, bf16[1,128,1536]{2,1,0:T(8,128)(2,1)S(1)} %collective-permute-done.5.received), custom_call_target="tpu_custom_call" | custom-call | flops 196608 | bytes 2359296 | tf_op jit(solution)/shard_map/pallas_call | solution.py:451
  63.9 2.3 %add_margins.1 = (bf16[128,2560]{1,0:T(8,128)(2,1)}, bf16[128,2560]{1,0:T(8,128)(2,1)}) custom-call(s32[1]{0:T(128)} %bitcast.scal, bf16[128,2560]{1,0:T(8,128)(2,1)} %get-tuple-element.28.dk, bf16[128,2560]{1,0:T(8,128)(2,1)} %get-tuple-element.29.dv, bf16[2,64,2560]{2,1,0:T(8,128)(2,1)S(1)} %collective-permute-done.2.mc, ...), custom_call_target="tpu_custom_call" | custom-call | flops 655360 | bytes 3932160 | tf_op jit(solution)/shard_map/add_margins/pallas_call | solution.py:496
  66.1 0.5 shard_map.159
  (31 shorter events, 0.1 us)
Async XLA Ops:
  0.6 6.7 %copy-start = (bf16[512,1536]{1,0:T(8,128)(2,1)S(1)}, bf16[512,1536]{1,0:T(8,128)(2,1)}, u32[]{:S(2)}) copy-start(bf16[512,1536]{1,0:T(8,128)(2,1)} %q0.1) | copy-start | bytes 4718596
  0.6 6.7 %copy-start.5 = (bf16[1,1536,768]{2,1,0:T(8,128)(2,1)S(1)}, bf16[1,1536,768]{2,1,0:T(8,128)(2,1)}, u32[]{:S(2)}) copy-start(bf16[1,1536,768]{2,1,0:T(8,128)(2,1)} %gw.1) | copy-start | bytes 7077892
  2.2 23.0 %collective-permute-start.6 = (bf16[512,1536]{1,0:T(8,128)(2,1)S(1)}, bf16[512,1536]{1,0:T(8,128)(2,1)S(1)}, u32[]{:S(2)}, u32[]{:S(2)}) collective-permute-start(bf16[512,1536]{1,0:T(8,128)(2,1)S(1)} %pick_outgoing.1), channel_id=1, source_target_pairs={{9,1},{11,3},{0,4},{13,5},{2,6},{15,7},{4,8},{17,9},{6,10},{19,11}... | collective-permute-start | bytes 4718600 | tf_op jit(solution)/shard_map/ppermute | solution.py:536
  7.4 1.7 %copy-start.6 = (bf16[1,1536,768]{2,1,0:T(8,128)(2,1)S(1)}, bf16[1,1536,768]{2,1,0:T(8,128)(2,1)}, u32[]{:S(2)}) copy-start(bf16[1,1536,768]{2,1,0:T(8,128)(2,1)} %uw.1) | copy-start | bytes 7077892
  9.1 1.7 %copy-start.7 = (bf16[1,768,1536]{2,1,0:T(8,128)(2,1)S(1)}, bf16[1,768,1536]{2,1,0:T(8,128)(2,1)}, u32[]{:S(2)}) copy-start(bf16[1,768,1536]{2,1,0:T(8,128)(2,1)} %dw.1) | copy-start | bytes 7077892
  10.7 1.4 %copy-start.8 = (bf16[512,1536]{1,0:T(8,128)(2,1)S(1)}, bf16[512,1536]{1,0:T(8,128)(2,1)}, u32[]{:S(2)}) copy-start(bf16[512,1536]{1,0:T(8,128)(2,1)} %og.1) | copy-start | bytes 4718596
  19.6 30.7 %collective-permute-start.9 = (bf16[512,768]{1,0:T(8,128)(2,1)}, bf16[512,768]{1,0:T(8,128)(2,1)S(1)}, u32[]{:S(2)}, u32[]{:S(2)}) collective-permute-start(bf16[512,768]{1,0:T(8,128)(2,1)} %get-tuple-element.38.g0), channel_id=1, source_target_pairs={{8,0},{12,4},{16,8},{20,12},{24,16},{28,20},{9,1},{13,5},{17,9},{2... | collective-permute-start | bytes 2359304 | tf_op jit(solution)/shard_map/ppermute | solution.py:514
  20.9 21.2 %collective-permute-start.4 = (bf16[2,128,1536]{2,1,0:T(8,128)(2,1)}, bf16[2,128,1536]{2,1,0:T(8,128)(2,1)S(1)}, u32[]{:S(2)}, u32[]{:S(2)}) collective-permute-start(bf16[2,128,1536]{2,1,0:T(8,128)(2,1)} %get-tuple-element.35), channel_id=1, source_target_pairs={{0,1},{1,0},{2,3},{3,2},{4,5},{5,4},{6,7},{7,6},{8,9},{9,8},{10,11... | collective-permute-start | bytes 2359304 | tf_op jit(solution)/shard_map/ppermute | solution.py:525
  22.3 4.9 %collective-permute-start = (bf16[2,64,2560]{2,1,0:T(8,128)(2,1)S(1)}, bf16[2,64,2560]{2,1,0:T(8,128)(2,1)S(1)}, u32[]{:S(2)}, u32[]{:S(2)}) collective-permute-start(bf16[2,64,2560]{2,1,0:T(8,128)(2,1)S(1)} %get-tuple-element.25), channel_id=1, source_target_pairs={{0,1},{2,3},{1,0},{3,2},{4,5},{6,7},{5,4},{7,6},{8,9},{10,11},{9,8... | collective-permute-start | bytes 1966088 | tf_op jit(solution)/shard_map/ppermute | solution.py:520
  22.8 0.9 %copy-start.9 = (s32[4]{0:T(128)S(1)}, s32[4]{0:T(128)}, u32[]{:S(2)}) copy-start(s32[4]{0:T(128)} %clips.1) | copy-start | bytes 52
  22.9 7.9 %collective-permute-start.1 = (bf16[2,64,2560]{2,1,0:T(8,128)(2,1)S(1)}, bf16[2,64,2560]{2,1,0:T(8,128)(2,1)S(1)}, u32[]{:S(2)}, u32[]{:S(2)}) collective-permute-start(bf16[2,64,2560]{2,1,0:T(8,128)(2,1)S(1)} %get-tuple-element.26), channel_id=1, source_target_pairs={{1,2},{2,1},{5,6},{6,5},{9,10},{10,9},{13,14},{14,13},{17,18},{18,... | collective-permute-start | bytes 1966088 | tf_op jit(solution)/shard_map/ppermute | solution.py:520
  24.3 2.9 %copy-start.10 = (bf16[512,768]{1,0:T(8,128)(2,1)S(1)}, bf16[512,768]{1,0:T(8,128)(2,1)}, u32[]{:S(2)}) copy-start(bf16[512,768]{1,0:T(8,128)(2,1)} %refs_2_.3) | copy-start | bytes 2359300
  25.2 18.0 %collective-permute-start.7 = (bf16[512,1536]{1,0:T(8,128)(2,1)S(1)}, bf16[512,1536]{1,0:T(8,128)(2,1)S(1)}, u32[]{:S(2)}, u32[]{:S(2)}) collective-permute-start(bf16[512,1536]{1,0:T(8,128)(2,1)S(1)} %collective-permute-done.6.refs_1_), channel_id=1, source_target_pairs={{0,1},{2,3},{1,0},{3,2},{4,5},{6,7},{5,4},{7,6},{8,9},{10,11},{9,8... | collective-permute-start | bytes 4718600 | tf_op jit(solution)/shard_map/ppermute | solution.py:520
  27.2 15.6 %copy-start.4 = (bf16[2,128,1536]{2,1,0:T(8,128)(2,1)S(1)}, bf16[2,128,1536]{2,1,0:T(8,128)(2,1)}, u32[]{:S(2)}) copy-start(bf16[2,128,1536]{2,1,0:T(8,128)(2,1)} %get-tuple-element.34.kept) | copy-start | bytes 2359300
  27.2 23.1 %collective-permute-start.8 = (bf16[512,768]{1,0:T(8,128)(2,1)S(1)}, bf16[512,768]{1,0:T(8,128)(2,1)S(1)}, u32[]{:S(2)}, u32[]{:S(2)}) collective-permute-start(bf16[512,768]{1,0:T(8,128)(2,1)S(1)} %copy-done.10), channel_id=1, source_target_pairs={{0,4},{4,8},{8,12},{12,16},{16,20},{20,24},{24,28},{1,5},{5,9},{9,... | collective-permute-start | bytes 2359304 | tf_op jit(solution)/shard_map/ppermute | solution.py:514
  37.6 8.7 %copy-start.1 = (bf16[512,1536]{1,0:T(8,128)(2,1)S(1)}, bf16[512,1536]{1,0:T(8,128)(2,1)}, u32[]{:S(2)}) copy-start(bf16[512,1536]{1,0:T(8,128)(2,1)} %k0.1) | copy-start | bytes 4718596
  37.6 26.2 %collective-permute-start.2 = (bf16[2,64,2560]{2,1,0:T(8,128)(2,1)}, bf16[2,64,2560]{2,1,0:T(8,128)(2,1)S(1)}, u32[]{:S(2)}, u32[]{:S(2)}) collective-permute-start(bf16[2,64,2560]{2,1,0:T(8,128)(2,1)} %get-tuple-element.30), channel_id=1, source_target_pairs={{0,1},{2,3},{1,0},{3,2},{4,5},{6,7},{5,4},{7,6},{8,9},{10,11},{9,8... | collective-permute-start | bytes 1966088 | tf_op jit(solution)/shard_map/ppermute | solution.py:520
  42.1 21.7 %collective-permute-start.3 = (bf16[2,64,2560]{2,1,0:T(8,128)(2,1)}, bf16[2,64,2560]{2,1,0:T(8,128)(2,1)S(1)}, u32[]{:S(2)}, u32[]{:S(2)}) collective-permute-start(bf16[2,64,2560]{2,1,0:T(8,128)(2,1)} %get-tuple-element.31), channel_id=1, source_target_pairs={{1,2},{2,1},{5,6},{6,5},{9,10},{10,9},{13,14},{14,13},{17,18},{18,... | collective-permute-start | bytes 1966088 | tf_op jit(solution)/shard_map/ppermute | solution.py:520
  43.2 7.1 %copy-start.3 = (bf16[512,768]{1,0:T(8,128)(2,1)S(1)}, bf16[512,768]{1,0:T(8,128)(2,1)}, u32[]{:S(2)}) copy-start(bf16[512,768]{1,0:T(8,128)(2,1)} %get-tuple-element.38.g0) | copy-start | bytes 2359300
  43.3 19.7 %collective-permute-start.5 = (bf16[1,128,1536]{2,1,0:T(8,128)(2,1)S(1)}, bf16[1,128,1536]{2,1,0:T(8,128)(2,1)S(1)}, u32[]{:S(2)}, u32[]{:S(2)}) collective-permute-start(bf16[1,128,1536]{2,1,0:T(8,128)(2,1)S(1)} %get-tuple-element.37), channel_id=1, source_target_pairs={{0,2},{1,3},{2,0},{3,1},{4,6},{5,7},{6,4},{7,5},{8,10},{9,11},{10,... | collective-permute-start | bytes 1179656 | tf_op jit(solution)/shard_map/ppermute | solution.py:525
  50.3 1.4 %copy-start.2 = (bf16[3,512,512]{2,1,0:T(8,128)(2,1)S(1)}, bf16[3,512,512]{2,1,0:T(8,128)(2,1)}, u32[]{:S(2)}) copy-start(bf16[3,512,512]{2,1,0:T(8,128)(2,1)} %pair_scores.1.st) | copy-start | bytes 4718596
  53.7 5.5 %collective-permute-start.10 = (f32[4,1,128]{2,1,0:T(1,128)S(1)}, f32[4,1,128]{2,1,0:T(1,128)S(1)}, u32[]{:S(2)}, u32[]{:S(2)}) collective-permute-start(f32[4,1,128]{2,1,0:T(1,128)S(1)} %get-tuple-element.40), channel_id=1, source_target_pairs={{4,0},{8,4},{12,8},{16,12},{20,16},{24,20},{28,24},{5,1},{9,5},{13... | collective-permute-start | bytes 6152 | tf_op jit(solution)/shard_map/ppermute | solution.py:514
  59.2 1.2 %collective-permute-start.11 = (f32[2,1,128]{2,1,0:T(1,128)S(1)}, f32[2,1,128]{2,1,0:T(1,128)S(1)}, u32[]{:S(2)}, u32[]{:S(2)}) collective-permute-start(f32[2,1,128]{2,1,0:T(1,128)S(1)} %get-tuple-element.42), channel_id=1, source_target_pairs={{0,1},{1,0},{2,3},{3,2},{4,5},{5,4},{6,7},{7,6},{8,9},{9,8},{10,11... | collective-permute-start | bytes 3080 | tf_op jit(solution)/shard_map/ppermute | solution.py:525
  60.5 5.7 %collective-permute-start.12 = (f32[1,1,128]{2,1,0:T(1,128)S(1)}, f32[1,1,128]{2,1,0:T(1,128)S(1)}, u32[]{:S(2)}, u32[]{:S(2)}) collective-permute-start(f32[1,1,128]{2,1,0:T(1,128)S(1)} %get-tuple-element.44), channel_id=1, source_target_pairs={{0,2},{1,3},{2,0},{3,1},{4,6},{5,7},{6,4},{7,5},{8,10},{9,11},{10,... | collective-permute-start | bytes 1544 | tf_op jit(solution)/shard_map/ppermute | solution.py:525

commit v3 on v2

--- a/solution.py
+++ b/solution.py
@@ -91,32 +91,36 @@
 
 def weights_kernel(shifts, tiles, scal, clips, out):
     at = lax.div(scal[0], tiles)
-    starts, total = [], 0
-    for n in range(clips.shape[0]):
+    starts, total = [], jnp.zeros((1, 1), jnp.int32)
+    for n in range(clips.shape[1]):
         starts.append(total)
-        total = total + clips[n]
-
-    def together(u, v):
-        apart = jnp.bool_(False)
+        total = total + clips[0:1, n : n + 1]
+    begins = {}
+    for x in range(0, 1 + max((1, *shifts))):
+        found = jnp.zeros((1, 1), F32)
+        for start in starts:
+            found = jnp.maximum(found, jnp.where(start == at + x, 1.0, 0.0))
+        begins[x] = found
+    for n, (u, v) in enumerate([(1, 0)] + [(u, v) for v in shifts for u in (0, 1)]):
+        apart = jnp.zeros((1, 1), F32)
         for x in range(1 - u, v + 1):
-            for start in starts:
-                apart = apart | (start == at + x)
-        return jnp.where(apart, 0.0, 1.0)
-
-    for n, (u, v) in enumerate([(1, 0)] + [(u, v) for v in shifts for u in (0, 1)]):
-        out[n : n + 1, :] = jnp.full((1, out.shape[1]), together(u, v), F32)
+            apart = jnp.maximum(apart, begins[x])
+        out[n : n + 1, :] = jnp.broadcast_to(1.0 - apart, (1, out.shape[1]))
 
 
 def pair_weights(scal, clips, shifts, tiles):
     return pl.pallas_call(
         functools.partial(weights_kernel, shifts, tiles),
-        in_specs=[pl.BlockSpec(memory_space=pltpu.SMEM)] * 2,
+        in_specs=[
+            pl.BlockSpec(memory_space=pltpu.SMEM),
+            pl.BlockSpec(memory_space=pltpu.VMEM),
+        ],
         out_specs=pl.BlockSpec(memory_space=pltpu.VMEM),
         out_shape=jax.ShapeDtypeStruct((1 + 2 * len(shifts), HEAD), F32),
         cost_estimate=cost(20 * 10**9, 4096),
         compiler_params=pltpu.CompilerParams(vmem_limit_bytes=1 << 20),
         name="pair_weights",
-    )(scal, clips)
+    )(scal, clips.reshape(1, -1))
 
 
 def fast_kernel(step, ends, scal, q, og, gw, uw, dw, gate_out, keep, send, *refs):
@@ -159,12 +163,20 @@
     step = next(s for s in (256, 128) if hidden % s == 0 and width % s == 0)
     ends = sorted({width // step * 2 // 3 * step, width})
     vmem = pl.BlockSpec(memory_space=pltpu.VMEM)
-    half = pltpu.HBM((tiles // 2, rows // tiles, width), BF16)
+    half = (tiles // 2, rows // tiles, width)
     return pl.pallas_call(
         functools.partial(fast_kernel, step, ends),
         in_specs=[pl.BlockSpec(memory_space=pltpu.SMEM)] + [vmem] * 5,
-        out_specs=[pl.BlockSpec(memory_space=pltpu.HBM)] * 3,
-        out_shape=[pltpu.HBM((rows, hidden), BF16), half, half],
+        out_specs=[
+            pl.BlockSpec(memory_space=pltpu.HBM),
+            pl.BlockSpec(memory_space=pl.ANY),
+            pl.BlockSpec(memory_space=pltpu.HBM),
+        ],
+        out_shape=[
+            pltpu.HBM((rows, hidden), BF16),
+            jax.ShapeDtypeStruct(half, BF16),
+            pltpu.HBM(half, BF16),
+        ],
         scratch_shapes=[
             pltpu.VMEM((rows, hidden), BF16),
             pltpu.VMEM((rows, hidden), BF16),
@@ -358,8 +370,8 @@
     return pl.pallas_call(
         functools.partial(scores_kernel, n_two),
         in_specs=[pl.BlockSpec(memory_space=pltpu.SMEM)] + [vmem] * (2 + n_two) + [anywhere] * n_two,
-        out_specs=hbm,
-        out_shape=pltpu.HBM((pairs, rows, rows), BF16),
+        out_specs=anywhere,
+        out_shape=jax.ShapeDtypeStruct((pairs, rows, rows), BF16),
         scratch_shapes=[pltpu.VMEM((rows, width), BF16)] * n_two
         + [
             pltpu.VMEM((pairs, rows, rows), BF16),

time: 67.1 us -> 67.2 us (level)
  waiting for transfers between devices: 8.57 us -> 10.8 us
  local copies, waits for them, and re-layouts: 6.17 us -> 4.76 us
  Pallas kernels: 27.8 us -> 27 us
    ppermute x4, waiting for transfers between devices: 3.51 us -> 5.44 us  [across(): return lax.ppermute(array, axis, pairs)]
    unnamed x22 -> x18, local copies, waits for them, and re-layouts: 6.17 us -> 4.76 us
  transfers between devices with their start and end apart: 13 -> 13, of which waited for: 4 -> 4; matrix products, arithmetic and copies ran while one was open for 0% -> 0% of each run, Pallas kernels for 38% -> 37%
where the time goes in v3:
time: 67.2 us; the launch traced here: 66.8 us
  Pallas kernels  27 us (40%)
  starting transfers between devices  23.3 us (35%)
  waiting for transfers between devices  10.8 us (16%)
  local copies, waits for them, and re-layouts  4.76 us (7%)
  between operations  0.91 us (1%)
    ppermute x5, starting transfers between devices, swapped(): return lax.ppermute(array, axis, pairs + [(j, i) for i, j in pairs])  8.82 us
    pallas_call x1, Pallas kernels, fast(): pl.pallas_call(functools.partial(fast_kernel, step, ends), in_specs=[pl.B...  7.55 us
    pallas_call x1, Pallas kernels, attention(): pl.pallas_call(functools.partial(attention_kernel, load_ends, store_ends)...  6.85 us
    ppermute x3, starting transfers between devices, shifted(): return lax.ppermute(array, axis, pairs)  5.96 us
    ppermute x4, waiting for transfers between devices, across(): return lax.ppermute(array, axis, pairs)  5.44 us
    ppermute x1, starting transfers between devices, moved_apart(): return lax.ppermute(array, ('tm', 'space'), pairs)  5.13 us
    unnamed x18, local copies, waits for them, and re-layouts  4.76 us
    ppermute x3, waiting for transfers between devices, shifted(): return lax.ppermute(array, axis, pairs)  4.18 us
  transfers between devices with their start and end apart: 13, of which 4 were waited for; matrix products, arithmetic and copies ran while one was open for 0% of the time, Pallas kernels for 37%

profile of v3, /device:TPU:0, one launch (start us, length us, event | category | flops | bytes accessed | tf_op | source)
XLA Modules:
  0.0 66.8 jit_solution(1262495565066591982)
XLA Ops:
  0.7 1.6 %pick_outgoing.1 = bf16[512,1536]{1,0:T(8,128)(2,1)S(1)} custom-call(s32[1]{0:T(128)} %bitcast.scal, bf16[512,1536]{1,0:T(8,128)(2,1)} %k0.1, bf16[512,1536]{1,0:T(8,128)(2,1)} %q0.1), custom_call_target="tpu_custom_call" | custom-call | bytes 3145728 | tf_op jit(solution)/shard_map/pick_outgoing/pallas_call | solution.py:49
  2.2 5.1 %collective-permute-start.6 = (bf16[512,1536]{1,0:T(8,128)(2,1)S(1)}, bf16[512,1536]{1,0:T(8,128)(2,1)S(1)}, u32[]{:S(2)}, u32[]{:S(2)}) collective-permute-start(bf16[512,1536]{1,0:T(8,128)(2,1)S(1)} %pick_outgoing.1), channel_id=1, source_target_pairs={{9,1},{11,3},{0,4},{13,5},{2,6},{15,7},{4,8},{17,9},{6,10},{19,11}... | collective-permute-start | bytes 4718600 | tf_op jit(solution)/shard_map/ppermute | solution.py:548
  7.4 1.7 %copy-done.4 = bf16[1,1536,768]{2,1,0:T(8,128)(2,1)S(1)} copy-done((bf16[1,1536,768]{2,1,0:T(8,128)(2,1)S(1)}, bf16[1,1536,768]{2,1,0:T(8,128)(2,1)}, u32[]{:S(2)}) %copy-start.4) | copy-done | bytes 2359320
  9.1 1.7 %copy-done.5 = bf16[1,768,1536]{2,1,0:T(8,128)(2,1)S(1)} copy-done((bf16[1,768,1536]{2,1,0:T(8,128)(2,1)S(1)}, bf16[1,768,1536]{2,1,0:T(8,128)(2,1)}, u32[]{:S(2)}) %copy-start.5) | copy-done | bytes 2359320
  10.7 1.4 %copy-done.6 = bf16[512,1536]{1,0:T(8,128)(2,1)S(1)} copy-done((bf16[512,1536]{1,0:T(8,128)(2,1)S(1)}, bf16[512,1536]{1,0:T(8,128)(2,1)}, u32[]{:S(2)}) %copy-start.6) | copy-done | bytes 1572888
  12.1 7.5 %fast_weights.1 = (bf16[512,768]{1,0:T(8,128)(2,1)}, bf16[2,128,1536]{2,1,0:T(8,128)(2,1)S(1)}, bf16[2,128,1536]{2,1,0:T(8,128)(2,1)}) custom-call(s32[1]{0:T(128)} %bitcast.scal, bf16[512,1536]{1,0:T(8,128)(2,1)S(1)} %copy-done, bf16[512,1536]{1,0:T(8,128)(2,1)S(1)} %copy-done.6, bf16[1,1536,768]{2,1,0:T(8,128)(2,1)S(1)} %copy-done.3, ...), custom_call_target="tpu_custom_call" | custom-call | flops 20000000000 | bytes 13369344 | tf_op jit(solution)/shard_map/fast_weights/pallas_call | solution.py:167
  19.7 1.3 %collective-permute-start.9 = (bf16[512,768]{1,0:T(8,128)(2,1)}, bf16[512,768]{1,0:T(8,128)(2,1)S(1)}, u32[]{:S(2)}, u32[]{:S(2)}) collective-permute-start(bf16[512,768]{1,0:T(8,128)(2,1)} %get-tuple-element.38.g0), channel_id=1, source_target_pairs={{8,0},{12,4},{16,8},{20,12},{24,16},{28,20},{9,1},{13,5},{17,9},{2... | collective-permute-start | bytes 2359304 | tf_op jit(solution)/shard_map/ppermute | solution.py:526
  21.0 0.1 collective-permute-start.4
  21.1 1.3 %pick_halos.1 = (bf16[2,64,2560]{2,1,0:T(8,128)(2,1)S(1)}, bf16[2,64,2560]{2,1,0:T(8,128)(2,1)S(1)}) custom-call(s32[1]{0:T(128)} %bitcast.scal, bf16[128,2560]{1,0:T(8,128)(2,1)} %refs_2_.2, bf16[128,2560]{1,0:T(8,128)(2,1)} %refs_3_.1), custom_call_target="tpu_custom_call" | custom-call | bytes 2621440 | tf_op jit(solution)/shard_map/pick_halos/pallas_call | solution.py:79
  22.4 0.6 collective-permute-start
  22.9 0.8 %collective-permute-start.1 = (bf16[2,64,2560]{2,1,0:T(8,128)(2,1)S(1)}, bf16[2,64,2560]{2,1,0:T(8,128)(2,1)S(1)}, u32[]{:S(2)}, u32[]{:S(2)}) collective-permute-start(bf16[2,64,2560]{2,1,0:T(8,128)(2,1)S(1)} %get-tuple-element.26), channel_id=1, source_target_pairs={{1,2},{2,1},{5,6},{6,5},{9,10},{10,9},{13,14},{14,13},{17,18},{18,... | collective-permute-start | bytes 1966088 | tf_op jit(solution)/shard_map/ppermute | solution.py:532
  23.8 0.1 window_bias.1.bias
  23.9 0.2 pair_weights.1.together
  24.0 1.2 %collective-permute-done.6.refs_1_ = bf16[512,1536]{1,0:T(8,128)(2,1)S(1)} collective-permute-done((bf16[512,1536]{1,0:T(8,128)(2,1)S(1)}, bf16[512,1536]{1,0:T(8,128)(2,1)S(1)}, u32[]{:S(2)}, u32[]{:S(2)}) %collective-permute-start.6) | collective-permute-done | bytes 1572896 | tf_op jit(solution)/shard_map/ppermute | solution.py:548
  25.2 1.7 %collective-permute-start.7 = (bf16[512,1536]{1,0:T(8,128)(2,1)S(1)}, bf16[512,1536]{1,0:T(8,128)(2,1)S(1)}, u32[]{:S(2)}, u32[]{:S(2)}) collective-permute-start(bf16[512,1536]{1,0:T(8,128)(2,1)S(1)} %collective-permute-done.6.refs_1_), channel_id=1, source_target_pairs={{0,1},{2,3},{1,0},{3,2},{4,5},{6,7},{5,4},{7,6},{8,9},{10,11},{9,8... | collective-permute-start | bytes 4718600 | tf_op jit(solution)/shard_map/ppermute | solution.py:532
  26.9 3.4 %collective-permute-start.8 = (bf16[512,768]{1,0:T(8,128)(2,1)S(1)}, bf16[512,768]{1,0:T(8,128)(2,1)S(1)}, u32[]{:S(2)}, u32[]{:S(2)}) collective-permute-start(bf16[512,768]{1,0:T(8,128)(2,1)S(1)} %copy-done.8), channel_id=1, source_target_pairs={{0,4},{4,8},{8,12},{12,16},{16,20},{20,24},{24,28},{1,5},{5,9},{9,... | collective-permute-start | bytes 2359304 | tf_op jit(solution)/shard_map/ppermute | solution.py:526
  30.3 6.9 %window_attention.1 = (bf16[128,2560]{1,0:T(8,128)(2,1)}, bf16[128,2560]{1,0:T(8,128)(2,1)}, bf16[128,2560]{1,0:T(8,128)(2,1)}, bf16[2,64,2560]{2,1,0:T(8,128)(2,1)}, bf16[2,64,2560]{2,1,0:T(8,128)(2,1)}) custom-call(f32[256,256]{1,0:T(8,128)S(1)} %window_bias.1.bias, bf16[128,2560]{1,0:T(8,128)(2,1)} %refs_0_.1, bf16[128,2560]{1,0:T(8,128)(2,1)} %refs_1_.1, ...), custom_call_target="tpu_custom_call" | custom-call | flops 1677721600 | bytes 7208960 | tf_op jit(solution)/shard_map/window_attention/pallas_call | solution.py:310
  37.1 5.1 %collective-permute-start.2 = (bf16[2,64,2560]{2,1,0:T(8,128)(2,1)}, bf16[2,64,2560]{2,1,0:T(8,128)(2,1)S(1)}, u32[]{:S(2)}, u32[]{:S(2)}) collective-permute-start(bf16[2,64,2560]{2,1,0:T(8,128)(2,1)} %get-tuple-element.30), channel_id=1, source_target_pairs={{0,1},{2,3},{1,0},{3,2},{4,5},{6,7},{5,4},{7,6},{8,9},{10,11},{9,8... | collective-permute-start | bytes 1966088 | tf_op jit(solution)/shard_map/ppermute | solution.py:532
  42.2 0.7 %collective-permute-start.3 = (bf16[2,64,2560]{2,1,0:T(8,128)(2,1)}, bf16[2,64,2560]{2,1,0:T(8,128)(2,1)S(1)}, u32[]{:S(2)}, u32[]{:S(2)}) collective-permute-start(bf16[2,64,2560]{2,1,0:T(8,128)(2,1)} %get-tuple-element.31), channel_id=1, source_target_pairs={{1,2},{2,1},{5,6},{6,5},{9,10},{10,9},{13,14},{14,13},{17,18},{18,... | collective-permute-start | bytes 1966088 | tf_op jit(solution)/shard_map/ppermute | solution.py:532
  42.9 0.4 shard_map.155
  43.3 3.1 %collective-permute-start.5 = (bf16[1,128,1536]{2,1,0:T(8,128)(2,1)S(1)}, bf16[1,128,1536]{2,1,0:T(8,128)(2,1)S(1)}, u32[]{:S(2)}, u32[]{:S(2)}) collective-permute-start(bf16[1,128,1536]{2,1,0:T(8,128)(2,1)S(1)} %get-tuple-element.37), channel_id=1, source_target_pairs={{0,2},{1,3},{2,0},{3,1},{4,6},{5,7},{6,4},{7,5},{8,10},{9,11},{10,... | collective-permute-start | bytes 1179656 | tf_op jit(solution)/shard_map/ppermute | solution.py:537
  46.4 3.5 %pair_scores.1.st = bf16[3,512,512]{2,1,0:T(8,128)(2,1)S(1)} custom-call(s32[1]{0:T(128)} %bitcast.scal, bf16[512,1536]{1,0:T(8,128)(2,1)S(1)} %copy-done.1, bf16[512,1536]{1,0:T(8,128)(2,1)S(1)} %copy-done, bf16[512,1536]{1,0:T(8,128)(2,1)S(1)} %collective-permute-done.7.refs_0_, bf16[512,1536]{1,0:T(8,128)(2,1)S(1)} %collective-permute-done.6.refs_1_), custom_call_target="tpu_custom_call" | custom-call | flops 20000000000 | bytes 1572864 | tf_op jit(solution)/shard_map/pair_scores/pallas_call | solution.py:370
  49.9 2.0 %pair_rates.1 = (f32[4,1,128]{2,1,0:T(1,128)S(1)}, f32[4,1,128]{2,1,0:T(1,128)S(1)}) custom-call(s32[1]{0:T(128)} %bitcast.scal, f32[3,128]{1,0:T(4,128)S(1)} %pair_shares.1.shares, bf16[3,512,512]{2,1,0:T(8,128)(2,1)S(1)} %pair_scores.1.st, bf16[512,768]{1,0:T(8,128)(2,1)S(1)} %copy-done.2, bf16[512,768]{1,0:T(8,128)(2,1)S(1)} %collective-permute-done.8.refs_0_, ...), custom_call_target="tpu_custom_call" | custom-call | flops 1207959552 | bytes 5505024 | tf_op jit(solution)/shard_map/pair_rates/pallas_call | solution.py:424
  51.9 1.3 %collective-permute-start.10 = (f32[4,1,128]{2,1,0:T(1,128)S(1)}, f32[4,1,128]{2,1,0:T(1,128)S(1)}, u32[]{:S(2)}, u32[]{:S(2)}) collective-permute-start(f32[4,1,128]{2,1,0:T(1,128)S(1)} %get-tuple-element.40), channel_id=1, source_target_pairs={{4,0},{8,4},{12,8},{16,12},{20,16},{24,20},{28,24},{5,1},{9,5},{13... | collective-permute-start | bytes 6152 | tf_op jit(solution)/shard_map/ppermute | solution.py:526
  53.2 4.2 %collective-permute-done.10.received = f32[4,1,128]{2,1,0:T(1,128)S(1)} collective-permute-done((f32[4,1,128]{2,1,0:T(1,128)S(1)}, f32[4,1,128]{2,1,0:T(1,128)S(1)}, u32[]{:S(2)}, u32[]{:S(2)}) %collective-permute-start.10) | collective-permute-done | bytes 2080 | tf_op jit(solution)/shard_map/ppermute | solution.py:526
  57.4 0.1 collective-permute-start.11
  57.5 1.1 %collective-permute-done.11.received = f32[2,1,128]{2,1,0:T(1,128)S(1)} collective-permute-done((f32[2,1,128]{2,1,0:T(1,128)S(1)}, f32[2,1,128]{2,1,0:T(1,128)S(1)}, u32[]{:S(2)}, u32[]{:S(2)}) %collective-permute-start.11) | collective-permute-done | bytes 1056 | tf_op jit(solution)/shard_map/ppermute | solution.py:537
  58.6 0.2 collective-permute-start.12
  58.8 4.3 %collective-permute-done.5.received = bf16[1,128,1536]{2,1,0:T(8,128)(2,1)S(1)} collective-permute-done((bf16[1,128,1536]{2,1,0:T(8,128)(2,1)S(1)}, bf16[1,128,1536]{2,1,0:T(8,128)(2,1)S(1)}, u32[]{:S(2)}, u32[]{:S(2)}) %collective-permute-start.5) | collective-permute-done | bytes 393248 | tf_op jit(solution)/shard_map/ppermute | solution.py:537
  63.1 0.8 %shard_map.156 = bf16[1,128,1536]{2,1,0:T(8,128)(2,1)} custom-call(s32[1]{0:T(128)} %bitcast.scal, bf16[1,128,1536]{2,1,0:T(8,128)(2,1)S(1)} %get-tuple-element.36.kept, bf16[1,128,1536]{2,1,0:T(8,128)(2,1)S(1)} %collective-permute-done.5.received), custom_call_target="tpu_custom_call" | custom-call | flops 196608 | bytes 2359296 | tf_op jit(solution)/shard_map/pallas_call | solution.py:463
  64.0 2.3 %add_margins.1 = (bf16[128,2560]{1,0:T(8,128)(2,1)}, bf16[128,2560]{1,0:T(8,128)(2,1)}) custom-call(s32[1]{0:T(128)} %bitcast.scal, bf16[128,2560]{1,0:T(8,128)(2,1)} %get-tuple-element.28.dk, bf16[128,2560]{1,0:T(8,128)(2,1)} %get-tuple-element.29.dv, bf16[2,64,2560]{2,1,0:T(8,128)(2,1)S(1)} %collective-permute-done.2.mc, ...), custom_call_target="tpu_custom_call" | custom-call | flops 655360 | bytes 3932160 | tf_op jit(solution)/shard_map/add_margins/pallas_call | solution.py:508
  66.2 0.5 shard_map.159
  (27 shorter events, 0.1 us)
Async XLA Ops:
  0.6 6.7 %copy-start = (bf16[512,1536]{1,0:T(8,128)(2,1)S(1)}, bf16[512,1536]{1,0:T(8,128)(2,1)}, u32[]{:S(2)}) copy-start(bf16[512,1536]{1,0:T(8,128)(2,1)} %q0.1) | copy-start | bytes 4718596
  0.6 6.7 %copy-start.3 = (bf16[1,1536,768]{2,1,0:T(8,128)(2,1)S(1)}, bf16[1,1536,768]{2,1,0:T(8,128)(2,1)}, u32[]{:S(2)}) copy-start(bf16[1,1536,768]{2,1,0:T(8,128)(2,1)} %gw.1) | copy-start | bytes 7077892
  2.2 23.0 %collective-permute-start.6 = (bf16[512,1536]{1,0:T(8,128)(2,1)S(1)}, bf16[512,1536]{1,0:T(8,128)(2,1)S(1)}, u32[]{:S(2)}, u32[]{:S(2)}) collective-permute-start(bf16[512,1536]{1,0:T(8,128)(2,1)S(1)} %pick_outgoing.1), channel_id=1, source_target_pairs={{9,1},{11,3},{0,4},{13,5},{2,6},{15,7},{4,8},{17,9},{6,10},{19,11}... | collective-permute-start | bytes 4718600 | tf_op jit(solution)/shard_map/ppermute | solution.py:548
  7.4 1.7 %copy-start.4 = (bf16[1,1536,768]{2,1,0:T(8,128)(2,1)S(1)}, bf16[1,1536,768]{2,1,0:T(8,128)(2,1)}, u32[]{:S(2)}) copy-start(bf16[1,1536,768]{2,1,0:T(8,128)(2,1)} %uw.1) | copy-start | bytes 7077892
  9.1 1.7 %copy-start.5 = (bf16[1,768,1536]{2,1,0:T(8,128)(2,1)S(1)}, bf16[1,768,1536]{2,1,0:T(8,128)(2,1)}, u32[]{:S(2)}) copy-start(bf16[1,768,1536]{2,1,0:T(8,128)(2,1)} %dw.1) | copy-start | bytes 7077892
  10.7 1.4 %copy-start.6 = (bf16[512,1536]{1,0:T(8,128)(2,1)S(1)}, bf16[512,1536]{1,0:T(8,128)(2,1)}, u32[]{:S(2)}) copy-start(bf16[512,1536]{1,0:T(8,128)(2,1)} %og.1) | copy-start | bytes 4718596
  19.7 30.2 %collective-permute-start.9 = (bf16[512,768]{1,0:T(8,128)(2,1)}, bf16[512,768]{1,0:T(8,128)(2,1)S(1)}, u32[]{:S(2)}, u32[]{:S(2)}) collective-permute-start(bf16[512,768]{1,0:T(8,128)(2,1)} %get-tuple-element.38.g0), channel_id=1, source_target_pairs={{8,0},{12,4},{16,8},{20,12},{24,16},{28,20},{9,1},{13,5},{17,9},{2... | collective-permute-start | bytes 2359304 | tf_op jit(solution)/shard_map/ppermute | solution.py:526
  21.0 21.2 %collective-permute-start.4 = (bf16[2,128,1536]{2,1,0:T(8,128)(2,1)}, bf16[2,128,1536]{2,1,0:T(8,128)(2,1)S(1)}, u32[]{:S(2)}, u32[]{:S(2)}) collective-permute-start(bf16[2,128,1536]{2,1,0:T(8,128)(2,1)} %get-tuple-element.35), channel_id=1, source_target_pairs={{0,1},{1,0},{2,3},{3,2},{4,5},{5,4},{6,7},{7,6},{8,9},{9,8},{10,11... | collective-permute-start | bytes 2359304 | tf_op jit(solution)/shard_map/ppermute | solution.py:537
  22.4 4.5 %collective-permute-start = (bf16[2,64,2560]{2,1,0:T(8,128)(2,1)S(1)}, bf16[2,64,2560]{2,1,0:T(8,128)(2,1)S(1)}, u32[]{:S(2)}, u32[]{:S(2)}) collective-permute-start(bf16[2,64,2560]{2,1,0:T(8,128)(2,1)S(1)} %get-tuple-element.25), channel_id=1, source_target_pairs={{0,1},{2,3},{1,0},{3,2},{4,5},{6,7},{5,4},{7,6},{8,9},{10,11},{9,8... | collective-permute-start | bytes 1966088 | tf_op jit(solution)/shard_map/ppermute | solution.py:532
  22.9 0.9 %copy-start.7 = (s32[4]{0:T(128)S(1)}, s32[4]{0:T(128)}, u32[]{:S(2)}) copy-start(s32[4]{0:T(128)} %param.23) | copy-start | bytes 52
  22.9 7.3 %collective-permute-start.1 = (bf16[2,64,2560]{2,1,0:T(8,128)(2,1)S(1)}, bf16[2,64,2560]{2,1,0:T(8,128)(2,1)S(1)}, u32[]{:S(2)}, u32[]{:S(2)}) collective-permute-start(bf16[2,64,2560]{2,1,0:T(8,128)(2,1)S(1)} %get-tuple-element.26), channel_id=1, source_target_pairs={{1,2},{2,1},{5,6},{6,5},{9,10},{10,9},{13,14},{14,13},{17,18},{18,... | collective-permute-start | bytes 1966088 | tf_op jit(solution)/shard_map/ppermute | solution.py:532
  24.0 2.9 %copy-start.8 = (bf16[512,768]{1,0:T(8,128)(2,1)S(1)}, bf16[512,768]{1,0:T(8,128)(2,1)}, u32[]{:S(2)}) copy-start(bf16[512,768]{1,0:T(8,128)(2,1)} %refs_2_.3) | copy-start | bytes 2359300
  25.2 18.1 %collective-permute-start.7 = (bf16[512,1536]{1,0:T(8,128)(2,1)S(1)}, bf16[512,1536]{1,0:T(8,128)(2,1)S(1)}, u32[]{:S(2)}, u32[]{:S(2)}) collective-permute-start(bf16[512,1536]{1,0:T(8,128)(2,1)S(1)} %collective-permute-done.6.refs_1_), channel_id=1, source_target_pairs={{0,1},{2,3},{1,0},{3,2},{4,5},{6,7},{5,4},{7,6},{8,9},{10,11},{9,8... | collective-permute-start | bytes 4718600 | tf_op jit(solution)/shard_map/ppermute | solution.py:532
  26.9 23.0 %collective-permute-start.8 = (bf16[512,768]{1,0:T(8,128)(2,1)S(1)}, bf16[512,768]{1,0:T(8,128)(2,1)S(1)}, u32[]{:S(2)}, u32[]{:S(2)}) collective-permute-start(bf16[512,768]{1,0:T(8,128)(2,1)S(1)} %copy-done.8), channel_id=1, source_target_pairs={{0,4},{4,8},{8,12},{12,16},{16,20},{20,24},{24,28},{1,5},{5,9},{9,... | collective-permute-start | bytes 2359304 | tf_op jit(solution)/shard_map/ppermute | solution.py:526
  37.1 9.3 %copy-start.1 = (bf16[512,1536]{1,0:T(8,128)(2,1)S(1)}, bf16[512,1536]{1,0:T(8,128)(2,1)}, u32[]{:S(2)}) copy-start(bf16[512,1536]{1,0:T(8,128)(2,1)} %k0.1) | copy-start | bytes 4718596
  37.1 26.8 %collective-permute-start.2 = (bf16[2,64,2560]{2,1,0:T(8,128)(2,1)}, bf16[2,64,2560]{2,1,0:T(8,128)(2,1)S(1)}, u32[]{:S(2)}, u32[]{:S(2)}) collective-permute-start(bf16[2,64,2560]{2,1,0:T(8,128)(2,1)} %get-tuple-element.30), channel_id=1, source_target_pairs={{0,1},{2,3},{1,0},{3,2},{4,5},{6,7},{5,4},{7,6},{8,9},{10,11},{9,8... | collective-permute-start | bytes 1966088 | tf_op jit(solution)/shard_map/ppermute | solution.py:532
  42.2 21.7 %collective-permute-start.3 = (bf16[2,64,2560]{2,1,0:T(8,128)(2,1)}, bf16[2,64,2560]{2,1,0:T(8,128)(2,1)S(1)}, u32[]{:S(2)}, u32[]{:S(2)}) collective-permute-start(bf16[2,64,2560]{2,1,0:T(8,128)(2,1)} %get-tuple-element.31), channel_id=1, source_target_pairs={{1,2},{2,1},{5,6},{6,5},{9,10},{10,9},{13,14},{14,13},{17,18},{18,... | collective-permute-start | bytes 1966088 | tf_op jit(solution)/shard_map/ppermute | solution.py:532
  43.3 6.6 %copy-start.2 = (bf16[512,768]{1,0:T(8,128)(2,1)S(1)}, bf16[512,768]{1,0:T(8,128)(2,1)}, u32[]{:S(2)}) copy-start(bf16[512,768]{1,0:T(8,128)(2,1)} %get-tuple-element.38.g0) | copy-start | bytes 2359300
  43.3 19.8 %collective-permute-start.5 = (bf16[1,128,1536]{2,1,0:T(8,128)(2,1)S(1)}, bf16[1,128,1536]{2,1,0:T(8,128)(2,1)S(1)}, u32[]{:S(2)}, u32[]{:S(2)}) collective-permute-start(bf16[1,128,1536]{2,1,0:T(8,128)(2,1)S(1)} %get-tuple-element.37), channel_id=1, source_target_pairs={{0,2},{1,3},{2,0},{3,1},{4,6},{5,7},{6,4},{7,5},{8,10},{9,11},{10,... | collective-permute-start | bytes 1179656 | tf_op jit(solution)/shard_map/ppermute | solution.py:537
  51.9 5.5 %collective-permute-start.10 = (f32[4,1,128]{2,1,0:T(1,128)S(1)}, f32[4,1,128]{2,1,0:T(1,128)S(1)}, u32[]{:S(2)}, u32[]{:S(2)}) collective-permute-start(f32[4,1,128]{2,1,0:T(1,128)S(1)} %get-tuple-element.40), channel_id=1, source_target_pairs={{4,0},{8,4},{12,8},{16,12},{20,16},{24,20},{28,24},{5,1},{9,5},{13... | collective-permute-start | bytes 6152 | tf_op jit(solution)/shard_map/ppermute | solution.py:526
  57.4 1.2 %collective-permute-start.11 = (f32[2,1,128]{2,1,0:T(1,128)S(1)}, f32[2,1,128]{2,1,0:T(1,128)S(1)}, u32[]{:S(2)}, u32[]{:S(2)}) collective-permute-start(f32[2,1,128]{2,1,0:T(1,128)S(1)} %get-tuple-element.42), channel_id=1, source_target_pairs={{0,1},{1,0},{2,3},{3,2},{4,5},{5,4},{6,7},{7,6},{8,9},{9,8},{10,11... | collective-permute-start | bytes 3080 | tf_op jit(solution)/shard_map/ppermute | solution.py:537
  58.6 7.6 %collective-permute-start.12 = (f32[1,1,128]{2,1,0:T(1,128)S(1)}, f32[1,1,128]{2,1,0:T(1,128)S(1)}, u32[]{:S(2)}, u32[]{:S(2)}) collective-permute-start(f32[1,1,128]{2,1,0:T(1,128)S(1)} %get-tuple-element.44), channel_id=1, source_target_pairs={{0,2},{1,3},{2,0},{3,1},{4,6},{5,7},{6,4},{7,5},{8,10},{9,11},{10,... | collective-permute-start | bytes 1544 | tf_op jit(solution)/shard_map/ppermute | solution.py:537

commit v4 on v3

--- a/solution.py
+++ b/solution.py
@@ -312,8 +312,10 @@
         in_specs=[vmem]
         + [pl.BlockSpec(memory_space=pltpu.HBM)] * 4
         + [pl.BlockSpec(memory_space=pl.ANY)] * 2,
-        out_specs=[pl.BlockSpec(memory_space=pltpu.HBM)] * 5,
-        out_shape=[pltpu.HBM(x, BF16) for x in (flat, flat, flat, half, half)],
+        out_specs=[pl.BlockSpec(memory_space=pl.ANY)] * 2
+        + [pl.BlockSpec(memory_space=pltpu.HBM)] * 3,
+        out_shape=[jax.ShapeDtypeStruct(flat, BF16)] * 2
+        + [pltpu.HBM(x, BF16) for x in (flat, half, half)],
         scratch_shapes=[pltpu.VMEM(x, BF16) for x in [flat] * 4 + [half] * 2 + [flat] * 3 + [half] * 2]
         + [pltpu.SemaphoreType.DMA((len(load_ends), 6)), pltpu.SemaphoreType.DMA((len(store_ends), 5))],
         cost_estimate=cost(
@@ -508,8 +510,7 @@
     return pl.pallas_call(
         functools.partial(margins_kernel, parts),
         in_specs=[pl.BlockSpec(memory_space=pltpu.SMEM)]
-        + [hbm] * 2
-        + [pl.BlockSpec(memory_space=pl.ANY)] * 2,
+        + [pl.BlockSpec(memory_space=pl.ANY)] * 4,
         out_specs=[hbm] * 2,
         out_shape=[pltpu.HBM((rows, width), BF16)] * 2,
         scratch_shapes=[pltpu.VMEM(x, BF16) for x in (whole, half, half, whole)]
@@ -517,7 +518,7 @@
         cost_estimate=cost(2 * rows * width, 12 * rows * width),
         compiler_params=pltpu.CompilerParams(vmem_limit_bytes=8 << 20),
         name="add_margins",
-    )(scal, *far(dk, dv), mc, mx)
+    )(scal, dk, dv, mc, mx)
 
 
 def shifted(array, axis, by):

time: 67.2 us -> 66.8 us (level)
    pallas_call x1, Pallas kernels: 2.27 us -> 1.59 us  [add_margins(): pl.pallas_call(functools.partial(margins_kernel, parts), in_specs=[pl.Blo...]
where the time goes in v4:
time: 66.8 us; the launch traced here: 66.4 us
  Pallas kernels  26.6 us (40%)
  starting transfers between devices  23.3 us (35%)
  waiting for transfers between devices  10.8 us (16%)
  local copies, waits for them, and re-layouts  4.76 us (7%)
  between operations  0.91 us (1%)
    ppermute x5, starting transfers between devices, swapped(): return lax.ppermute(array, axis, pairs + [(j, i) for i, j in pairs])  8.82 us
    pallas_call x1, Pallas kernels, fast(): pl.pallas_call(functools.partial(fast_kernel, step, ends), in_specs=[pl.B...  7.55 us
    pallas_call x1, Pallas kernels, attention(): pl.pallas_call(functools.partial(attention_kernel, load_ends, store_ends)...  7.17 us
    ppermute x3, starting transfers between devices, shifted(): return lax.ppermute(array, axis, pairs)  5.96 us
    ppermute x4, waiting for transfers between devices, across(): return lax.ppermute(array, axis, pairs)  5.43 us
    ppermute x1, starting transfers between devices, moved_apart(): return lax.ppermute(array, ('tm', 'space'), pairs)  5.13 us
    unnamed x18, local copies, waits for them, and re-layouts  4.76 us
    ppermute x3, waiting for transfers between devices, shifted(): return lax.ppermute(array, axis, pairs)  4.18 us
  transfers between devices with their start and end apart: 13, of which 4 were waited for; matrix products, arithmetic and copies ran while one was open for 0% of the time, Pallas kernels for 37%

profile of v4, /device:TPU:0, one launch (start us, length us, event | category | flops | bytes accessed | tf_op | source)
XLA Modules:
  0.0 66.4 jit_solution(706015369382197098)
XLA Ops:
  0.7 1.6 %pick_outgoing.1 = bf16[512,1536]{1,0:T(8,128)(2,1)S(1)} custom-call(s32[1]{0:T(128)} %bitcast.scal, bf16[512,1536]{1,0:T(8,128)(2,1)} %k0.1, bf16[512,1536]{1,0:T(8,128)(2,1)} %q0.1), custom_call_target="tpu_custom_call" | custom-call | bytes 3145728 | tf_op jit(solution)/shard_map/pick_outgoing/pallas_call | solution.py:49
  2.2 5.1 %collective-permute-start.6 = (bf16[512,1536]{1,0:T(8,128)(2,1)S(1)}, bf16[512,1536]{1,0:T(8,128)(2,1)S(1)}, u32[]{:S(2)}, u32[]{:S(2)}) collective-permute-start(bf16[512,1536]{1,0:T(8,128)(2,1)S(1)} %pick_outgoing.1), channel_id=1, source_target_pairs={{9,1},{11,3},{0,4},{13,5},{2,6},{15,7},{4,8},{17,9},{6,10},{19,11}... | collective-permute-start | bytes 4718600 | tf_op jit(solution)/shard_map/ppermute | solution.py:549
  7.4 1.7 %copy-done.4 = bf16[1,1536,768]{2,1,0:T(8,128)(2,1)S(1)} copy-done((bf16[1,1536,768]{2,1,0:T(8,128)(2,1)S(1)}, bf16[1,1536,768]{2,1,0:T(8,128)(2,1)}, u32[]{:S(2)}) %copy-start.4) | copy-done | bytes 2359320
  9.1 1.7 %copy-done.5 = bf16[1,768,1536]{2,1,0:T(8,128)(2,1)S(1)} copy-done((bf16[1,768,1536]{2,1,0:T(8,128)(2,1)S(1)}, bf16[1,768,1536]{2,1,0:T(8,128)(2,1)}, u32[]{:S(2)}) %copy-start.5) | copy-done | bytes 2359320
  10.7 1.4 %copy-done.6 = bf16[512,1536]{1,0:T(8,128)(2,1)S(1)} copy-done((bf16[512,1536]{1,0:T(8,128)(2,1)S(1)}, bf16[512,1536]{1,0:T(8,128)(2,1)}, u32[]{:S(2)}) %copy-start.6) | copy-done | bytes 1572888
  12.1 7.5 %fast_weights.1 = (bf16[512,768]{1,0:T(8,128)(2,1)}, bf16[2,128,1536]{2,1,0:T(8,128)(2,1)S(1)}, bf16[2,128,1536]{2,1,0:T(8,128)(2,1)}) custom-call(s32[1]{0:T(128)} %bitcast.scal, bf16[512,1536]{1,0:T(8,128)(2,1)S(1)} %copy-done, bf16[512,1536]{1,0:T(8,128)(2,1)S(1)} %copy-done.6, bf16[1,1536,768]{2,1,0:T(8,128)(2,1)S(1)} %copy-done.3, ...), custom_call_target="tpu_custom_call" | custom-call | flops 20000000000 | bytes 13369344 | tf_op jit(solution)/shard_map/fast_weights/pallas_call | solution.py:167
  19.7 1.3 %collective-permute-start.9 = (bf16[512,768]{1,0:T(8,128)(2,1)}, bf16[512,768]{1,0:T(8,128)(2,1)S(1)}, u32[]{:S(2)}, u32[]{:S(2)}) collective-permute-start(bf16[512,768]{1,0:T(8,128)(2,1)} %get-tuple-element.38.g0), channel_id=1, source_target_pairs={{8,0},{12,4},{16,8},{20,12},{24,16},{28,20},{9,1},{13,5},{17,9},{2... | collective-permute-start | bytes 2359304 | tf_op jit(solution)/shard_map/ppermute | solution.py:527
  21.0 0.1 collective-permute-start.4
  21.1 1.3 %pick_halos.1 = (bf16[2,64,2560]{2,1,0:T(8,128)(2,1)S(1)}, bf16[2,64,2560]{2,1,0:T(8,128)(2,1)S(1)}) custom-call(s32[1]{0:T(128)} %bitcast.scal, bf16[128,2560]{1,0:T(8,128)(2,1)} %refs_2_.2, bf16[128,2560]{1,0:T(8,128)(2,1)} %refs_3_.1), custom_call_target="tpu_custom_call" | custom-call | bytes 2621440 | tf_op jit(solution)/shard_map/pick_halos/pallas_call | solution.py:79
  22.4 0.6 collective-permute-start
  22.9 0.8 %collective-permute-start.1 = (bf16[2,64,2560]{2,1,0:T(8,128)(2,1)S(1)}, bf16[2,64,2560]{2,1,0:T(8,128)(2,1)S(1)}, u32[]{:S(2)}, u32[]{:S(2)}) collective-permute-start(bf16[2,64,2560]{2,1,0:T(8,128)(2,1)S(1)} %get-tuple-element.26), channel_id=1, source_target_pairs={{1,2},{2,1},{5,6},{6,5},{9,10},{10,9},{13,14},{14,13},{17,18},{18,... | collective-permute-start | bytes 1966088 | tf_op jit(solution)/shard_map/ppermute | solution.py:533
  23.8 0.1 window_bias.1.bias
  23.9 0.2 pair_weights.1.together
  24.0 1.2 %collective-permute-done.6.refs_1_ = bf16[512,1536]{1,0:T(8,128)(2,1)S(1)} collective-permute-done((bf16[512,1536]{1,0:T(8,128)(2,1)S(1)}, bf16[512,1536]{1,0:T(8,128)(2,1)S(1)}, u32[]{:S(2)}, u32[]{:S(2)}) %collective-permute-start.6) | collective-permute-done | bytes 1572896 | tf_op jit(solution)/shard_map/ppermute | solution.py:549
  25.2 1.7 %collective-permute-start.7 = (bf16[512,1536]{1,0:T(8,128)(2,1)S(1)}, bf16[512,1536]{1,0:T(8,128)(2,1)S(1)}, u32[]{:S(2)}, u32[]{:S(2)}) collective-permute-start(bf16[512,1536]{1,0:T(8,128)(2,1)S(1)} %collective-permute-done.6.refs_1_), channel_id=1, source_target_pairs={{0,1},{2,3},{1,0},{3,2},{4,5},{6,7},{5,4},{7,6},{8,9},{10,11},{9,8... | collective-permute-start | bytes 4718600 | tf_op jit(solution)/shard_map/ppermute | solution.py:533
  26.9 3.4 %collective-permute-start.8 = (bf16[512,768]{1,0:T(8,128)(2,1)S(1)}, bf16[512,768]{1,0:T(8,128)(2,1)S(1)}, u32[]{:S(2)}, u32[]{:S(2)}) collective-permute-start(bf16[512,768]{1,0:T(8,128)(2,1)S(1)} %copy-done.8), channel_id=1, source_target_pairs={{0,4},{4,8},{8,12},{12,16},{16,20},{20,24},{24,28},{1,5},{5,9},{9,... | collective-permute-start | bytes 2359304 | tf_op jit(solution)/shard_map/ppermute | solution.py:527
  30.3 7.2 %window_attention.1 = (bf16[128,2560]{1,0:T(8,128)(2,1)S(1)}, bf16[128,2560]{1,0:T(8,128)(2,1)S(1)}, bf16[128,2560]{1,0:T(8,128)(2,1)}, bf16[2,64,2560]{2,1,0:T(8,128)(2,1)}, bf16[2,64,2560]{2,1,0:T(8,128)(2,1)}) custom-call(f32[256,256]{1,0:T(8,128)S(1)} %window_bias.1.bias, bf16[128,2560]{1,0:T(8,128)(2,1)} %refs_0_.1, bf16[128,2560]{1,0:T(8,128)(2,1)} %refs_1_.1, ...), custom_call_target="tpu_custom_call" | custom-call | flops 1677721600 | bytes 7208960 | tf_op jit(solution)/shard_map/window_attention/pallas_call | solution.py:310
  37.5 5.1 %collective-permute-start.2 = (bf16[2,64,2560]{2,1,0:T(8,128)(2,1)}, bf16[2,64,2560]{2,1,0:T(8,128)(2,1)S(1)}, u32[]{:S(2)}, u32[]{:S(2)}) collective-permute-start(bf16[2,64,2560]{2,1,0:T(8,128)(2,1)} %get-tuple-element.30), channel_id=1, source_target_pairs={{0,1},{2,3},{1,0},{3,2},{4,5},{6,7},{5,4},{7,6},{8,9},{10,11},{9,8... | collective-permute-start | bytes 1966088 | tf_op jit(solution)/shard_map/ppermute | solution.py:533
  42.6 0.7 %collective-permute-start.3 = (bf16[2,64,2560]{2,1,0:T(8,128)(2,1)}, bf16[2,64,2560]{2,1,0:T(8,128)(2,1)S(1)}, u32[]{:S(2)}, u32[]{:S(2)}) collective-permute-start(bf16[2,64,2560]{2,1,0:T(8,128)(2,1)} %get-tuple-element.31), channel_id=1, source_target_pairs={{1,2},{2,1},{5,6},{6,5},{9,10},{10,9},{13,14},{14,13},{17,18},{18,... | collective-permute-start | bytes 1966088 | tf_op jit(solution)/shard_map/ppermute | solution.py:533
  43.3 0.4 shard_map.155
  43.7 3.1 %collective-permute-start.5 = (bf16[1,128,1536]{2,1,0:T(8,128)(2,1)S(1)}, bf16[1,128,1536]{2,1,0:T(8,128)(2,1)S(1)}, u32[]{:S(2)}, u32[]{:S(2)}) collective-permute-start(bf16[1,128,1536]{2,1,0:T(8,128)(2,1)S(1)} %get-tuple-element.37), channel_id=1, source_target_pairs={{0,2},{1,3},{2,0},{3,1},{4,6},{5,7},{6,4},{7,5},{8,10},{9,11},{10,... | collective-permute-start | bytes 1179656 | tf_op jit(solution)/shard_map/ppermute | solution.py:538
  46.7 3.5 %pair_scores.1.st = bf16[3,512,512]{2,1,0:T(8,128)(2,1)S(1)} custom-call(s32[1]{0:T(128)} %bitcast.scal, bf16[512,1536]{1,0:T(8,128)(2,1)S(1)} %copy-done.1, bf16[512,1536]{1,0:T(8,128)(2,1)S(1)} %copy-done, bf16[512,1536]{1,0:T(8,128)(2,1)S(1)} %collective-permute-done.7.refs_0_, bf16[512,1536]{1,0:T(8,128)(2,1)S(1)} %collective-permute-done.6.refs_1_), custom_call_target="tpu_custom_call" | custom-call | flops 20000000000 | bytes 1572864 | tf_op jit(solution)/shard_map/pair_scores/pallas_call | solution.py:372
  50.2 2.0 %pair_rates.1 = (f32[4,1,128]{2,1,0:T(1,128)S(1)}, f32[4,1,128]{2,1,0:T(1,128)S(1)}) custom-call(s32[1]{0:T(128)} %bitcast.scal, f32[3,128]{1,0:T(4,128)S(1)} %pair_shares.1.shares, bf16[3,512,512]{2,1,0:T(8,128)(2,1)S(1)} %pair_scores.1.st, bf16[512,768]{1,0:T(8,128)(2,1)S(1)} %copy-done.2, bf16[512,768]{1,0:T(8,128)(2,1)S(1)} %collective-permute-done.8.refs_0_, ...), custom_call_target="tpu_custom_call" | custom-call | flops 1207959552 | bytes 5505024 | tf_op jit(solution)/shard_map/pair_rates/pallas_call | solution.py:426
  52.2 1.3 %collective-permute-start.10 = (f32[4,1,128]{2,1,0:T(1,128)S(1)}, f32[4,1,128]{2,1,0:T(1,128)S(1)}, u32[]{:S(2)}, u32[]{:S(2)}) collective-permute-start(f32[4,1,128]{2,1,0:T(1,128)S(1)} %get-tuple-element.40), channel_id=1, source_target_pairs={{4,0},{8,4},{12,8},{16,12},{20,16},{24,20},{28,24},{5,1},{9,5},{13... | collective-permute-start | bytes 6152 | tf_op jit(solution)/shard_map/ppermute | solution.py:527
  53.5 4.2 %collective-permute-done.10.received = f32[4,1,128]{2,1,0:T(1,128)S(1)} collective-permute-done((f32[4,1,128]{2,1,0:T(1,128)S(1)}, f32[4,1,128]{2,1,0:T(1,128)S(1)}, u32[]{:S(2)}, u32[]{:S(2)}) %collective-permute-start.10) | collective-permute-done | bytes 2080 | tf_op jit(solution)/shard_map/ppermute | solution.py:527
  57.7 0.1 collective-permute-start.11
  57.8 1.1 %collective-permute-done.11.received = f32[2,1,128]{2,1,0:T(1,128)S(1)} collective-permute-done((f32[2,1,128]{2,1,0:T(1,128)S(1)}, f32[2,1,128]{2,1,0:T(1,128)S(1)}, u32[]{:S(2)}, u32[]{:S(2)}) %collective-permute-start.11) | collective-permute-done | bytes 1056 | tf_op jit(solution)/shard_map/ppermute | solution.py:538
  59.0 0.2 collective-permute-start.12
  59.2 4.3 %collective-permute-done.5.received = bf16[1,128,1536]{2,1,0:T(8,128)(2,1)S(1)} collective-permute-done((bf16[1,128,1536]{2,1,0:T(8,128)(2,1)S(1)}, bf16[1,128,1536]{2,1,0:T(8,128)(2,1)S(1)}, u32[]{:S(2)}, u32[]{:S(2)}) %collective-permute-start.5) | collective-permute-done | bytes 393248 | tf_op jit(solution)/shard_map/ppermute | solution.py:538
  63.4 0.8 %shard_map.156 = bf16[1,128,1536]{2,1,0:T(8,128)(2,1)} custom-call(s32[1]{0:T(128)} %bitcast.scal, bf16[1,128,1536]{2,1,0:T(8,128)(2,1)S(1)} %get-tuple-element.36.kept, bf16[1,128,1536]{2,1,0:T(8,128)(2,1)S(1)} %collective-permute-done.5.received), custom_call_target="tpu_custom_call" | custom-call | flops 196608 | bytes 2359296 | tf_op jit(solution)/shard_map/pallas_call | solution.py:465
  64.3 1.6 %add_margins.1 = (bf16[128,2560]{1,0:T(8,128)(2,1)}, bf16[128,2560]{1,0:T(8,128)(2,1)}) custom-call(s32[1]{0:T(128)} %bitcast.scal, bf16[128,2560]{1,0:T(8,128)(2,1)S(1)} %get-tuple-element.28.dk, bf16[128,2560]{1,0:T(8,128)(2,1)S(1)} %get-tuple-element.29.dv, bf16[2,64,2560]{2,1,0:T(8,128)(2,1)S(1)} %collective-permute-done.2.mc, ...), custom_call_target="tpu_custom_call" | custom-call | flops 655360 | bytes 3932160 | tf_op jit(solution)/shard_map/add_margins/pallas_call | solution.py:510
  65.9 0.5 shard_map.159
  (27 shorter events, 0.1 us)
Async XLA Ops:
  0.6 6.7 %copy-start = (bf16[512,1536]{1,0:T(8,128)(2,1)S(1)}, bf16[512,1536]{1,0:T(8,128)(2,1)}, u32[]{:S(2)}) copy-start(bf16[512,1536]{1,0:T(8,128)(2,1)} %q0.1) | copy-start | bytes 4718596
  0.6 6.7 %copy-start.3 = (bf16[1,1536,768]{2,1,0:T(8,128)(2,1)S(1)}, bf16[1,1536,768]{2,1,0:T(8,128)(2,1)}, u32[]{:S(2)}) copy-start(bf16[1,1536,768]{2,1,0:T(8,128)(2,1)} %gw.1) | copy-start | bytes 7077892
  2.2 23.0 %collective-permute-start.6 = (bf16[512,1536]{1,0:T(8,128)(2,1)S(1)}, bf16[512,1536]{1,0:T(8,128)(2,1)S(1)}, u32[]{:S(2)}, u32[]{:S(2)}) collective-permute-start(bf16[512,1536]{1,0:T(8,128)(2,1)S(1)} %pick_outgoing.1), channel_id=1, source_target_pairs={{9,1},{11,3},{0,4},{13,5},{2,6},{15,7},{4,8},{17,9},{6,10},{19,11}... | collective-permute-start | bytes 4718600 | tf_op jit(solution)/shard_map/ppermute | solution.py:549
  7.4 1.7 %copy-start.4 = (bf16[1,1536,768]{2,1,0:T(8,128)(2,1)S(1)}, bf16[1,1536,768]{2,1,0:T(8,128)(2,1)}, u32[]{:S(2)}) copy-start(bf16[1,1536,768]{2,1,0:T(8,128)(2,1)} %uw.1) | copy-start | bytes 7077892
  9.1 1.7 %copy-start.5 = (bf16[1,768,1536]{2,1,0:T(8,128)(2,1)S(1)}, bf16[1,768,1536]{2,1,0:T(8,128)(2,1)}, u32[]{:S(2)}) copy-start(bf16[1,768,1536]{2,1,0:T(8,128)(2,1)} %dw.1) | copy-start | bytes 7077892
  10.7 1.4 %copy-start.6 = (bf16[512,1536]{1,0:T(8,128)(2,1)S(1)}, bf16[512,1536]{1,0:T(8,128)(2,1)}, u32[]{:S(2)}) copy-start(bf16[512,1536]{1,0:T(8,128)(2,1)} %og.1) | copy-start | bytes 4718596
  19.7 30.5 %collective-permute-start.9 = (bf16[512,768]{1,0:T(8,128)(2,1)}, bf16[512,768]{1,0:T(8,128)(2,1)S(1)}, u32[]{:S(2)}, u32[]{:S(2)}) collective-permute-start(bf16[512,768]{1,0:T(8,128)(2,1)} %get-tuple-element.38.g0), channel_id=1, source_target_pairs={{8,0},{12,4},{16,8},{20,12},{24,16},{28,20},{9,1},{13,5},{17,9},{2... | collective-permute-start | bytes 2359304 | tf_op jit(solution)/shard_map/ppermute | solution.py:527
  21.0 21.6 %collective-permute-start.4 = (bf16[2,128,1536]{2,1,0:T(8,128)(2,1)}, bf16[2,128,1536]{2,1,0:T(8,128)(2,1)S(1)}, u32[]{:S(2)}, u32[]{:S(2)}) collective-permute-start(bf16[2,128,1536]{2,1,0:T(8,128)(2,1)} %get-tuple-element.35), channel_id=1, source_target_pairs={{0,1},{1,0},{2,3},{3,2},{4,5},{5,4},{6,7},{7,6},{8,9},{9,8},{10,11... | collective-permute-start | bytes 2359304 | tf_op jit(solution)/shard_map/ppermute | solution.py:538
  22.4 4.5 %collective-permute-start = (bf16[2,64,2560]{2,1,0:T(8,128)(2,1)S(1)}, bf16[2,64,2560]{2,1,0:T(8,128)(2,1)S(1)}, u32[]{:S(2)}, u32[]{:S(2)}) collective-permute-start(bf16[2,64,2560]{2,1,0:T(8,128)(2,1)S(1)} %get-tuple-element.25), channel_id=1, source_target_pairs={{0,1},{2,3},{1,0},{3,2},{4,5},{6,7},{5,4},{7,6},{8,9},{10,11},{9,8... | collective-permute-start | bytes 1966088 | tf_op jit(solution)/shard_map/ppermute | solution.py:533
  22.9 0.9 %copy-start.7 = (s32[4]{0:T(128)S(1)}, s32[4]{0:T(128)}, u32[]{:S(2)}) copy-start(s32[4]{0:T(128)} %param.23) | copy-start | bytes 52
  22.9 7.3 %collective-permute-start.1 = (bf16[2,64,2560]{2,1,0:T(8,128)(2,1)S(1)}, bf16[2,64,2560]{2,1,0:T(8,128)(2,1)S(1)}, u32[]{:S(2)}, u32[]{:S(2)}) collective-permute-start(bf16[2,64,2560]{2,1,0:T(8,128)(2,1)S(1)} %get-tuple-element.26), channel_id=1, source_target_pairs={{1,2},{2,1},{5,6},{6,5},{9,10},{10,9},{13,14},{14,13},{17,18},{18,... | collective-permute-start | bytes 1966088 | tf_op jit(solution)/shard_map/ppermute | solution.py:533
  24.0 2.9 %copy-start.8 = (bf16[512,768]{1,0:T(8,128)(2,1)S(1)}, bf16[512,768]{1,0:T(8,128)(2,1)}, u32[]{:S(2)}) copy-start(bf16[512,768]{1,0:T(8,128)(2,1)} %refs_2_.3) | copy-start | bytes 2359300
  25.2 18.5 %collective-permute-start.7 = (bf16[512,1536]{1,0:T(8,128)(2,1)S(1)}, bf16[512,1536]{1,0:T(8,128)(2,1)S(1)}, u32[]{:S(2)}, u32[]{:S(2)}) collective-permute-start(bf16[512,1536]{1,0:T(8,128)(2,1)S(1)} %collective-permute-done.6.refs_1_), channel_id=1, source_target_pairs={{0,1},{2,3},{1,0},{3,2},{4,5},{6,7},{5,4},{7,6},{8,9},{10,11},{9,8... | collective-permute-start | bytes 4718600 | tf_op jit(solution)/shard_map/ppermute | solution.py:533
  26.9 23.4 %collective-permute-start.8 = (bf16[512,768]{1,0:T(8,128)(2,1)S(1)}, bf16[512,768]{1,0:T(8,128)(2,1)S(1)}, u32[]{:S(2)}, u32[]{:S(2)}) collective-permute-start(bf16[512,768]{1,0:T(8,128)(2,1)S(1)} %copy-done.8), channel_id=1, source_target_pairs={{0,4},{4,8},{8,12},{12,16},{16,20},{20,24},{24,28},{1,5},{5,9},{9,... | collective-permute-start | bytes 2359304 | tf_op jit(solution)/shard_map/ppermute | solution.py:527
  37.4 9.3 %copy-start.1 = (bf16[512,1536]{1,0:T(8,128)(2,1)S(1)}, bf16[512,1536]{1,0:T(8,128)(2,1)}, u32[]{:S(2)}) copy-start(bf16[512,1536]{1,0:T(8,128)(2,1)} %k0.1) | copy-start | bytes 4718596
  37.5 26.8 %collective-permute-start.2 = (bf16[2,64,2560]{2,1,0:T(8,128)(2,1)}, bf16[2,64,2560]{2,1,0:T(8,128)(2,1)S(1)}, u32[]{:S(2)}, u32[]{:S(2)}) collective-permute-start(bf16[2,64,2560]{2,1,0:T(8,128)(2,1)} %get-tuple-element.30), channel_id=1, source_target_pairs={{0,1},{2,3},{1,0},{3,2},{4,5},{6,7},{5,4},{7,6},{8,9},{10,11},{9,8... | collective-permute-start | bytes 1966088 | tf_op jit(solution)/shard_map/ppermute | solution.py:533
  42.6 21.7 %collective-permute-start.3 = (bf16[2,64,2560]{2,1,0:T(8,128)(2,1)}, bf16[2,64,2560]{2,1,0:T(8,128)(2,1)S(1)}, u32[]{:S(2)}, u32[]{:S(2)}) collective-permute-start(bf16[2,64,2560]{2,1,0:T(8,128)(2,1)} %get-tuple-element.31), channel_id=1, source_target_pairs={{1,2},{2,1},{5,6},{6,5},{9,10},{10,9},{13,14},{14,13},{17,18},{18,... | collective-permute-start | bytes 1966088 | tf_op jit(solution)/shard_map/ppermute | solution.py:533
  43.7 6.6 %copy-start.2 = (bf16[512,768]{1,0:T(8,128)(2,1)S(1)}, bf16[512,768]{1,0:T(8,128)(2,1)}, u32[]{:S(2)}) copy-start(bf16[512,768]{1,0:T(8,128)(2,1)} %get-tuple-element.38.g0) | copy-start | bytes 2359300
  43.7 19.8 %collective-permute-start.5 = (bf16[1,128,1536]{2,1,0:T(8,128)(2,1)S(1)}, bf16[1,128,1536]{2,1,0:T(8,128)(2,1)S(1)}, u32[]{:S(2)}, u32[]{:S(2)}) collective-permute-start(bf16[1,128,1536]{2,1,0:T(8,128)(2,1)S(1)} %get-tuple-element.37), channel_id=1, source_target_pairs={{0,2},{1,3},{2,0},{3,1},{4,6},{5,7},{6,4},{7,5},{8,10},{9,11},{10,... | collective-permute-start | bytes 1179656 | tf_op jit(solution)/shard_map/ppermute | solution.py:538
  52.2 5.5 %collective-permute-start.10 = (f32[4,1,128]{2,1,0:T(1,128)S(1)}, f32[4,1,128]{2,1,0:T(1,128)S(1)}, u32[]{:S(2)}, u32[]{:S(2)}) collective-permute-start(f32[4,1,128]{2,1,0:T(1,128)S(1)} %get-tuple-element.40), channel_id=1, source_target_pairs={{4,0},{8,4},{12,8},{16,12},{20,16},{24,20},{28,24},{5,1},{9,5},{13... | collective-permute-start | bytes 6152 | tf_op jit(solution)/shard_map/ppermute | solution.py:527
  57.7 1.2 %collective-permute-start.11 = (f32[2,1,128]{2,1,0:T(1,128)S(1)}, f32[2,1,128]{2,1,0:T(1,128)S(1)}, u32[]{:S(2)}, u32[]{:S(2)}) collective-permute-start(f32[2,1,128]{2,1,0:T(1,128)S(1)} %get-tuple-element.42), channel_id=1, source_target_pairs={{0,1},{1,0},{2,3},{3,2},{4,5},{5,4},{6,7},{7,6},{8,9},{9,8},{10,11... | collective-permute-start | bytes 3080 | tf_op jit(solution)/shard_map/ppermute | solution.py:538
  59.0 6.9 %collective-permute-start.12 = (f32[1,1,128]{2,1,0:T(1,128)S(1)}, f32[1,1,128]{2,1,0:T(1,128)S(1)}, u32[]{:S(2)}, u32[]{:S(2)}) collective-permute-start(f32[1,1,128]{2,1,0:T(1,128)S(1)} %get-tuple-element.44), channel_id=1, source_target_pairs={{0,2},{1,3},{2,0},{3,1},{4,6},{5,7},{6,4},{7,5},{8,10},{9,11},{10,... | collective-permute-start | bytes 1544 | tf_op jit(solution)/shard_map/ppermute | solution.py:538
